TPU v7x, 32 devices: a whole 2x2x4 slice. The times are simulated.
32 devices in a mesh: row: 8 (over y, x, core), col: 4 (over z).
Axes of the slice: x: 2, y: 2, z: 4, core: 2. Of those that a mesh axis runs over, the one named last changes fastest.
Arguments:
- hidden: bfloat16 [4128, 1792], P('row', 'col'), may hold values from -6 to 6
- norm_gain: bfloat16 [1792], P('col'), may hold values from 0.099609375 to 1.8984375
- qkv_weight: bfloat16 [1792, 2304], P('row', 'col'), may hold values from -0.125 to 0.125
- out_weight: bfloat16 [1792, 1792], P('col', 'row'), may hold values from -1.5 to 1.5
- cache: bfloat16 [40, 1024, 2048], P('row', None, 'col'), may hold values from -6 to 6
- cached: int32 [40], P('row'), may hold values from 128 to 1024, as said below
- token_mask: int32 [4128], P('row'), may hold values 0 or 1
Outputs:
- mixed: bfloat16 [4128, 1792], P('row', 'col')
Inputs may be any that keep to these rules, and one draw needn't show every extreme that they name: Some request has exactly 1024 cached positions.
All inputs are finite; a program needn't handle non-finite values. No bound on the sum of `token_mask` on one device may be relied on, other than what follows from the above.
Results may differ from a plain program's by a relative error of at most 0.0072.
Values may be sent and summed in bfloat16 or wider, within the bound.
No kernel may reach another device: no remote copies, remote signals or barrier semaphores. Data moves between devices by JAX's collectives and lax.ppermute only.
A program may use at most 64 MiB of HBM per device.

v0:
```python
import jax
import jax.numpy as jnp
from jax import lax
from jax.sharding import PartitionSpec as P

FEATURE_WIDTH = 16
HDIM = 112
SPAN_TOKENS = 512
DEC = 4


def taylor(taylor_score):
    return 1.0 + taylor_score + 0.5 * taylor_score * taylor_score


def attend(projected, cache, cached, token_mask):
    rows = projected.shape[0]
    width = 2 * FEATURE_WIDTH + HDIM
    lanes = FEATURE_WIDTH + HDIM
    heads_here = projected.shape[1] // width
    parts = projected.reshape(rows, heads_here, width)
    query_rows = parts[:, :, :FEATURE_WIDTH]
    key_rows = parts[:, :, FEATURE_WIDTH : 2 * FEATURE_WIDTH]
    values = parts[:, :, 2 * FEATURE_WIDTH :]
    store = cache.reshape(cache.shape[0], cache.shape[1], heads_here, lanes)
    capacity = cache.shape[1]
    block = min(512, capacity)
    score_scale = FEATURE_WIDTH ** (-0.5)
    live = token_mask.astype(jnp.float32)
    prefill_query_rows = query_rows[:SPAN_TOKENS]
    prior_tokens = store[0]
    offset = cached[0]

    def span_step(index, carry):
        numer, denom = carry
        span_slice = lax.dynamic_slice_in_dim(prior_tokens, index * block, block, 0)
        position = index * block + lax.iota(jnp.int32, block)
        taylor_score = (
            jnp.einsum(
                "sue,pue->usp",
                prefill_query_rows,
                span_slice[:, :, :FEATURE_WIDTH],
                preferred_element_type=jnp.float32,
            )
            * score_scale
        )
        weight = taylor(taylor_score) * (position < offset).astype(jnp.float32)[None, None, :]
        numer = numer + jnp.einsum(
            "hqk,khd->hqd",
            weight.astype(jnp.bfloat16),
            span_slice[:, :, FEATURE_WIDTH:],
            preferred_element_type=jnp.float32,
        )
        return (numer, denom + jnp.sum(weight, axis=-1))

    start_numer = jnp.zeros((heads_here, SPAN_TOKENS, HDIM), jnp.float32)
    start_denom = jnp.zeros((heads_here, SPAN_TOKENS), jnp.float32)
    span_blocks = (offset + block - 1) // block
    numer, denom = lax.fori_loop(0, span_blocks, span_step, (start_numer, start_denom))
    taylor_score = (
        jnp.einsum(
            "sue,pue->usp",
            prefill_query_rows,
            key_rows[:SPAN_TOKENS],
            preferred_element_type=jnp.float32,
        )
        * score_scale
    )
    order = lax.iota(jnp.int32, SPAN_TOKENS)
    allowed = (order[None, :] <= order[:, None]).astype(jnp.float32) * live[:SPAN_TOKENS][None, :]
    weight = taylor(taylor_score) * allowed[None]
    numer = numer + jnp.einsum(
        "hqk,khd->hqd",
        weight.astype(jnp.bfloat16),
        values[:SPAN_TOKENS],
        preferred_element_type=jnp.float32,
    )
    denom = denom + jnp.sum(weight, axis=-1)
    decode_queries = query_rows[SPAN_TOKENS:]
    past = store[1:]
    counts = cached[1:]

    def decode_step(index, carry):
        dec_numer, dec_denom = carry
        span_slice = lax.dynamic_slice_in_dim(past, index * block, block, 1)
        position = index * block + lax.iota(jnp.int32, block)
        taylor_score = (
            jnp.einsum(
                "rhf,rkhf->rhk",
                decode_queries,
                span_slice[..., :FEATURE_WIDTH],
                preferred_element_type=jnp.float32,
            )
            * score_scale
        )
        seen = (position[None, :] < counts[:, None]).astype(jnp.float32)
        weight = taylor(taylor_score) * seen[:, None, :]
        dec_numer = dec_numer + jnp.einsum(
            "rhk,rkhd->rhd",
            weight.astype(jnp.bfloat16),
            span_slice[..., FEATURE_WIDTH:],
            preferred_element_type=jnp.float32,
        )
        return (dec_numer, dec_denom + jnp.sum(weight, axis=-1))

    first_numer = jnp.zeros((DEC, heads_here, HDIM), jnp.float32)
    first_denom = jnp.zeros((DEC, heads_here), jnp.float32)
    decode_blocks = (jnp.max(counts) + block - 1) // block
    dec_numer, dec_denom = lax.fori_loop(0, decode_blocks, decode_step, (first_numer, first_denom))
    taylor_score = (
        jnp.sum(
            decode_queries.astype(jnp.float32) * key_rows[SPAN_TOKENS:].astype(jnp.float32), axis=-1
        )
        * score_scale
    )
    weight = taylor(taylor_score) * live[SPAN_TOKENS:, None]
    dec_numer = dec_numer + weight.astype(jnp.bfloat16).astype(jnp.float32)[..., None] * values[
        SPAN_TOKENS:
    ].astype(jnp.float32)
    dec_denom = dec_denom + weight
    numer_all = jnp.concatenate([jnp.transpose(numer, (1, 0, 2)), dec_numer], axis=0)
    denom_all = jnp.concatenate([jnp.transpose(denom, (1, 0)), dec_denom], axis=0)
    result = live[:, None, None] * numer_all / (denom_all + 1.0 - live[:, None])[..., None]
    return result.astype(jnp.bfloat16).reshape(rows, heads_here * HDIM)


def shards(hidden, norm_gain, qkv_weight, out_weight, cache, cached, token_mask):
    full, gain = (
        lax.all_gather(hidden, "col", axis=1, tiled=True),
        lax.all_gather(norm_gain, "col", axis=0, tiled=True),
    )
    wide = full.astype(jnp.float32)
    normed = (
        wide
        * lax.rsqrt(jnp.mean(wide * wide, axis=-1, keepdims=True) + 1e-06)
        * gain.astype(jnp.float32)
    )
    normed = normed.astype(jnp.bfloat16)
    projected = jnp.dot(
        normed,
        lax.all_gather(qkv_weight, "row", axis=0, tiled=True),
        preferred_element_type=jnp.float32,
    ).astype(jnp.bfloat16)
    attended = attend(projected, cache, cached, token_mask)
    terms = jnp.dot(
        attended,
        lax.all_gather(out_weight, "row", axis=1, tiled=True),
        preferred_element_type=jnp.float32,
    )
    mixed = lax.psum_scatter(terms, "col", scatter_dimension=1, tiled=True).astype(jnp.bfloat16)
    return mixed


def solution(mesh):
    in_specs = (
        P("row", "col"),
        P("col"),
        P("row", "col"),
        P("col", "row"),
        P("row", None, "col"),
        P("row"),
        P("row"),
    )
    out_specs = P("row", "col")
    return jax.shard_map(shards, mesh=mesh, in_specs=in_specs, out_specs=out_specs, check_vma=False)
```

profile of v0, /device:TPU:0, one launch (start us, length us, event | category | flops | bytes accessed | tf_op | source)
XLA Modules:
  0.0 219.6 jit_solution(1467507115509590201)
XLA Ops:
  8.1 1.8 copy.42
  9.9 1.4 fusion.44
  12.6 4.4 %slice.80 = bf16[4,1024,512]{2,1,0:T(8,128)(2,1)} slice(bf16[5,1024,512]{2,1,0:T(8,128)(2,1)} %param.15), slice={[1:5], [0:1024], [0:512]} | slice | bytes 8388608 | tf_op jit(solution)/shard_map/slice | solution.py:80
  17.1 7.1 %slice.81 = bf16[4,1024,4,128]{3,2,1,0:T(4,128)(2,1)} reshape(bf16[4,1024,512]{2,1,0:T(8,128)(2,1)} %slice.80) | data formatting | bytes 8388608 | tf_op jit(solution)/shard_map/slice | solution.py:80
  25.7 13.9 %all-reduce = bf16[1792]{0:T(1024)(128)(2,1)S(1)} all-reduce(bf16[1792]{0:T(1024)(128)(2,1)S(1)} %dynamic-update-slice), channel_id=1, replica_groups=mesh['row'=8,'col'=4] {'col'}, use_global_device_ids=true, to_apply=%add | all-reduce | flops 1792 | bytes 7168
  40.4 18.1 %all-gather.9.cloned.1.call-done = bf16[4,448,516]{1,2,0:T(8,128)(2,1)} async-done(((bf16[1,448,516]{1,2,0:T(8,128)(2,1)}), bf16[4,448,516]{1,2,0:T(8,128)(2,1)}) %all-gather.9.cloned.1.call-update) | async-done | bytes 1849360 | tf_op jit(solution)/shard_map/all_gather | solution.py:129
  58.4 4.6 %copy.36 = f32[4,448,516]{1,0,2:T(4,128)} copy(bf16[4,448,516]{1,2,0:T(8,128)(2,1)} %all-gather.9.cloned.1.call-done) | data formatting | bytes 5548032 | tf_op jit(solution)/shard_map/convert_element_type | solution.py:132
  63.1 6.0 %reshape.148 = f32[1792,516]{0,1:T(8,128)} reshape(f32[4,448,516]{1,0,2:T(4,128)} %copy.36) | data formatting | bytes 7397376 | tf_op jit(solution)/shard_map/convert_element_type | solution.py:132
  69.1 2.4 %multiply_reduce_fusion = f32[516]{0:T(1024)S(1)} fusion(f32[1792,516]{0,1:T(8,128)} %reshape.148), kind=kLoop, calls=%fused_computation.34 | loop fusion | flops 1848828 | bytes 3700752 | tf_op jit(solution)/shard_map/reduce_sum | solution.py:135
  71.5 16.4 %all-gather.5.cloned.1.call-done = bf16[1792,576]{1,0:T(8,128)(2,1)} async-done(((bf16[224,576]{1,0:T(8,128)(2,1)}), bf16[1792,576]{1,0:T(8,128)(2,1)}) %all-gather.5.cloned.1.call-update) | async-done | bytes 2064400 | tf_op jit(solution)/shard_map/all_gather | solution.py:141
  87.8 4.5 %fusion.28 = bf16[516,576]{1,0:T(8,128)(2,1)S(1)} fusion(bf16[1792,576]{1,0:T(8,128)(2,1)} %all-gather.5.cloned.1.call-done, f32[1792,516]{0,1:T(8,128)} %reshape.148, f32[1792]{0:T(1024)S(1)} %convert_element_type.83, f32[516]{0:T(1024)S(1)} %add_rsqrt_fusion), kind=kOutput, calls=%fused_computation.42 | convolution fusion | flops 1068293376 | bytes 6366736 | tf_op jit(solution)/shard_map/dot_general | solution.py:139
  92.8 9.9 %while.29 = (s32[]{:T(128)}, f32[4,4,112]{2,1,0:T(4,128)S(1)}, f32[4,4]{1,0:T(4,128)S(1)}, s32[]{:T(128)}, bf16[4,1024,4,128]{3,2,1,0:T(4,128)(2,1)}, /*index=5*...) while((s32[]{:T(128)}, f32[4,4,112]{2,1,0:T(4,128)S(1)}, ...), condition=%wide.region_7.8_spmd, body=%wide.region_5.7_spmd.sunk | while | flops 2169095 | bytes 23217140 | solution.py:109
  92.9 2.9 %constant_dynamic-slice_fusion.4 = bf16[4,512,4,112]{3,2,1,0:T(4,128)(2,1)S(1)} fusion(bf16[4,1024,4,128]{3,2,1,0:T(4,128)(2,1)} %get-tuple-element.378, s32[]{:T(128)S(6)} %select_n.25, s32[]{:T(128)S(6)} %add.289), kind=kLoop, calls=%fused_computation.31.clone.1 | loop fusion | bytes 3670024 | tf_op jit(solution)/shard_map/while/body/slice | solution.py:101
  97.8 2.9 %constant_dynamic-slice_fusion.4 = bf16[4,512,4,112]{3,2,1,0:T(4,128)(2,1)S(1)} fusion(bf16[4,1024,4,128]{3,2,1,0:T(4,128)(2,1)} %get-tuple-element.378, s32[]{:T(128)S(6)} %select_n.25, s32[]{:T(128)S(6)} %add.289), kind=kLoop, calls=%fused_computation.31.clone.1 | loop fusion | bytes 3670024 | tf_op jit(solution)/shard_map/while/body/slice | solution.py:101
  102.7 1.0 broadcast_in_dim.7
  103.8 7.9 %while.28 = (s32[]{:T(128)}, f32[4,512,112]{1,2,0:T(8,128)}, f32[4,512]{1,0:T(4,128)S(1)}, s32[]{:T(128)}, bf16[1024,4,128]{0,2,1:T(8,128)(2,1)S(1)}, /*index=5*...) while((s32[]{:T(128)}, f32[4,512,112]{1,2,0:T(8,128)}, ...), condition=%wide.region_3.4_spmd, body=%wide.region_1.3_spmd.sunk | while | flops 283346432 | bytes 10852555 | solution.py:59
  103.8 3.1 %bitcast_reduce_fusion.2 = (f32[4,512]{1,0:T(4,128)S(1)}, f32[4,512,512]{2,1,0:T(8,128)}) fusion(f32[512]{0:T(512)S(1)} %fusion.62, bf16[512,4,16]{0,2,1:T(8,128)(2,1)S(1)} %get-tuple-element.415, bf16[1024,4,128]{0,2,1:T(8,128)(2,1)S(1)} %get-tuple-element.414, s32[]{:T(128)S(6)} %select_n.24), kind=kOutput, calls=%fused_computation.clone.1 | convolution fusion | flops 40892416 | bytes 4335620 | tf_op jit(solution)/shard_map/while/body/sue,pue->usp/dot_general | solution.py:39
  106.9 4.7 %fusion.63 = f32[4,512,112]{1,2,0:T(8,128)} fusion(f32[4,512,112]{1,2,0:T(8,128)} %get-tuple-element.399, f32[4,512,512]{2,1,0:T(8,128)} %get-tuple-element.339, f32[512]{0:T(512)S(1)} %fusion.62, bf16[1024,4,128]{0,2,1:T(8,128)(2,1)S(1)} %get-tuple-element.414, s32[]{:T(128)S(6)} %select_n.24, s32[]{:T(128)S(6)} %add.281), kind=kOutput, calls=%fused_computation.4.clone.1 | convolution fusion | flops 242450432 | bytes 6490120 | tf_op jit(solution)/shard_map/while/body/hqk,khd->hqd/dot_general | solution.py:48
  111.9 1.3 fusion.21
  113.3 1.3 fusion.29
  114.7 1.8 all-gather.7.cloned.1.call-done
  116.6 5.2 %convolution_bitcast_fusion = f32[1792,516]{1,0:T(8,128)} fusion(bf16[516,448]{0,1:T(8,128)(2,1)S(1)} %fusion.33, bf16[448,1792]{0,1:T(8,128)(2,1)} %all-gather.7.cloned.1.call-done), kind=kOutput, calls=%fused_computation.35 | convolution fusion | flops 828506112 | bytes 5766656
  121.7 89.1 %reduce-scatter.4.cloned.1.call-done = f32[448,516]{1,0:T(8,128)} async-done(((f32[1792,516]{1,0:T(8,128)}), f32[448,516]{1,0:T(8,128)}) %reduce-scatter.4.cloned.1.call-update) | async-done | bytes 924688
  210.8 2.3 %copy.52 = bf16[516,448]{1,0:T(8,128)(2,1)} copy(f32[516,448]{0,1:T(8,128)} %bitcast.69) | data formatting | bytes 1387008
  (67 shorter events, 8.1 us)
Async XLA Ops:
  6.5 51.9 %all-gather.9.cloned.1.call-start = ((), (), s32[]{:S(2)}) async-start(), calls=%async_computation.3 | async-start | bytes 2662400 | tf_op jit(solution)/shard_map/all_gather | solution.py:129
  7.3 80.6 %all-gather.5.cloned.1.call-start = ((), (), s32[]{:S(2)}) async-start(), calls=%async_computation.1 | async-start | bytes 2580480 | tf_op jit(solution)/shard_map/all_gather | solution.py:141
  8.0 108.6 %all-gather.7.cloned.1.call-start = ((), (), s32[]{:S(2)}) async-start(), calls=%async_computation.2 | async-start | bytes 2064384 | tf_op jit(solution)/shard_map/all_gather | solution.py:147
  9.8 201.0 %reduce-scatter.4.cloned.1.call-start = ((), (), s32[]{:S(2)}) async-start(), calls=%async_computation.4 | async-start | bytes 5734400
  12.6 4.4 %copy-start.3 = (s32[516]{0:T(1024)S(1)}, s32[516]{0:T(1024)}, u32[]{:S(2)}) copy-start(s32[516]{0:T(1024)} %param.17) | copy-start | bytes 6196
  17.0 7.2 %copy-start.5 = (u32[32]{0:T(128)S(1)}, u32[32]{0:T(128)}, u32[]{:S(2)}) copy-start(u32[32]{0:T(128)} %constant.145) | copy-start | bytes 388
  17.0 8.4 %copy-start.4 = (bf16[448]{0:T(512)(128)(2,1)S(1)}, bf16[448]{0:T(512)(128)(2,1)}, u32[]{:S(2)}) copy-start(bf16[448]{0:T(512)(128)(2,1)} %param.12) | copy-start | bytes 2692
  17.1 22.6 %slice-start = ((bf16[5,1024,512]{2,1,0:T(8,128)(2,1)}), bf16[1,1024,512]{2,1,0:T(8,128)(2,1)S(1)}, s32[]{:S(2)}) async-start(bf16[5,1024,512]{2,1,0:T(8,128)(2,1)} %param.15), calls=%async_computation.5 | async-start | bytes 2097152 | tf_op jit(solution)/shard_map/slice | solution.py:31
  92.8 11.0 %copy-start.2 = (s32[5]{0:T(128)S(1)}, s32[5]{0:T(128)}, u32[]{:S(2)}) copy-start(s32[5]{0:T(128)} %param.16) | copy-start | bytes 64
  92.9 3.0 %copy-start = (bf16[4,1024,4,128]{3,2,1,0:T(4,128)(2,1)S(1)}, bf16[4,1024,4,128]{3,2,1,0:T(4,128)(2,1)}, u32[]{:S(2)}) copy-start(bf16[4,1024,4,128]{3,2,1,0:T(4,128)(2,1)} %get-tuple-element.378) | copy-start | bytes 12582916 | tf_op jit(solution)/shard_map/while
  97.8 3.0 %copy-start = (bf16[4,1024,4,128]{3,2,1,0:T(4,128)(2,1)S(1)}, bf16[4,1024,4,128]{3,2,1,0:T(4,128)(2,1)}, u32[]{:S(2)}) copy-start(bf16[4,1024,4,128]{3,2,1,0:T(4,128)(2,1)} %get-tuple-element.378) | copy-start | bytes 12582916 | tf_op jit(solution)/shard_map/while
  111.9 1.3 copy-start.1
Sparse Core Ops, SparseCore 0:
  8.9 49.4 all-gather.8
  60.3 27.4 all-gather.4
  89.7 26.7 all-gather.6
  121.9 88.9 reduce-scatter.3
where the time goes:
time: 220 us
  waiting for transfers between devices  127 us (58%)
  local copies, waits for them, and re-layouts  36.7 us (17%)
  matrix products  22 us (10%)
  between operations  15.3 us (7%)
  blocking collectives  13.9 us (6%)
  other arithmetic  4.64 us (2%)
    unnamed x5, waiting for transfers between devices  90.5 us
    all_gather x1, waiting for transfers between devices, shards(): lax.all_gather(hidden, 'col', axis=1, tiled=True)  18.1 us
    all_gather x1, waiting for transfers between devices, shards(): lax.all_gather(qkv_weight, 'row', axis=0, tiled=True)  16.4 us
    unnamed x1, blocking collectives  13.9 us
    slice x2, local copies, waits for them, and re-layouts, attend(): past = store[1:]  11.5 us
    convert_element_type x2, local copies, waits for them, and re-layouts, shards(): wide = full.astype(jnp.float32)  10.6 us
    slice x2, local copies, waits for them, and re-layouts, decode_step(): span_slice[..., FEATURE_WIDTH:]  5.85 us
    unnamed x1, matrix products  5.15 us
  transfers between devices with their start and end apart: 4, of which 4 were waited for; matrix products, arithmetic and copies ran while one was open for 25% of the time, Pallas kernels for 0%

commit v1 on v0

--- a/solution.py
+++ b/solution.py
@@ -1,12 +1,398 @@
 import jax
 import jax.numpy as jnp
 from jax import lax
+from jax.experimental import pallas as pl
+from jax.experimental.pallas import tpu as pltpu
 from jax.sharding import PartitionSpec as P
 
 FEATURE_WIDTH = 16
 HDIM = 112
 SPAN_TOKENS = 512
 DEC = 4
+LANES = FEATURE_WIDTH + HDIM
+F32 = jnp.float32
+BF16 = jnp.bfloat16
+HALF = SPAN_TOKENS // 2
+VMEM = pl.BlockSpec(memory_space=pltpu.VMEM)
+SMEM = pl.BlockSpec(memory_space=pltpu.SMEM)
+ANY = pl.BlockSpec(memory_space=pl.ANY)
+TAIL = 3 * HALF
+BODY = TAIL + HALF // 2
+EXTRA = 32
+QROWS = 224
+OROWS = 448
+
+
+def gray(place):
+    return place ^ (place >> 1)
+
+
+def call(body, outs, in_specs, scratch=(), flops=0, nbytes=0, name=None):
+    return pl.pallas_call(
+        body,
+        out_shape=outs,
+        in_specs=in_specs,
+        out_specs=jax.tree.map(lambda _: VMEM, outs),
+        scratch_shapes=scratch,
+        cost_estimate=pl.CostEstimate(flops=flops, bytes_accessed=nbytes, transcendentals=0),
+        compiler_params=pltpu.CompilerParams(vmem_limit_bytes=48 * 1024 * 1024),
+        name=name,
+    )
+
+
+def shaped(shape, dtype=BF16):
+    return jax.ShapeDtypeStruct(shape, dtype)
+
+
+def dot(a, b):
+    return jnp.dot(a, b, preferred_element_type=F32)
+
+
+def dot_nt(a, b):
+    return lax.dot_general(a, b, (((1,), (1,)), ((), ())), preferred_element_type=F32)
+
+
+def lane(shape):
+    return lax.broadcasted_iota(jnp.int32, shape, len(shape) - 1)
+
+
+def row(shape):
+    return lax.broadcasted_iota(jnp.int32, shape, 0)
+
+
+def pack_tokens(h_ref, g_ref, a_ref, b_ref):
+    for ref, base in ((a_ref, 0), (b_ref, HALF)):
+        for t in range(3):
+            ref[t * HALF : (t + 1) * HALF, :] = h_ref[base : base + HALF, t * 128 : (t + 1) * 128]
+        low = h_ref[base : base + HALF // 2, 384:448]
+        high = h_ref[base + HALF // 2 : base + HALF, 384:448]
+        ref[TAIL:BODY, :] = jnp.concatenate([low, high], axis=1)
+        ref[BODY:, :] = jnp.zeros((EXTRA, 128), BF16)
+    for t in range(3):
+        a_ref[BODY + 8 * t : BODY + 8 * t + 1, :] = g_ref[:, t * 128 : (t + 1) * 128]
+        b_ref[BODY + 8 * t : BODY + 8 * t + DEC, :] = h_ref[SPAN_TOKENS:, t * 128 : (t + 1) * 128]
+    last = g_ref[:, 384:448]
+    a_ref[BODY + 24 : BODY + 25, :] = jnp.concatenate([last, last], axis=1)
+    b_ref[BODY + 24 : BODY + 24 + DEC, 0:64] = h_ref[SPAN_TOKENS:, 384:448]
+
+
+def pack_weights(q_ref, o_ref, w_ref):
+    width = FEATURE_WIDTH + LANES
+    for h in range(4):
+        w_ref[h * QROWS : (h + 1) * QROWS, :] = q_ref[:, h * width + FEATURE_WIDTH : (h + 1) * width]
+    queries = [q_ref[:, h * width : h * width + FEATURE_WIDTH] for h in range(4)]
+    w_ref[4 * QROWS : 5 * QROWS, :] = jnp.concatenate(
+        queries + [jnp.zeros((QROWS, 64), BF16)], axis=1
+    )
+    w_ref[5 * QROWS : 5 * QROWS + OROWS, :] = o_ref[:, 0:128]
+    w_ref[5 * QROWS + OROWS :, :] = jnp.concatenate(
+        [o_ref[:, 128:224], jnp.zeros((OROWS, 32), BF16)], axis=1
+    )
+
+
+def place_weights(*refs):
+    blocks, (q_ref, o_ref) = refs[:8], refs[8:]
+    me = lax.axis_index("row")
+    for k in range(8):
+        owner = me ^ k
+        part, side = owner >> 1, owner & 1
+        start = pl.multiple_of(side * QROWS, 32)
+        for t in range(5):
+            q_ref[part, pl.ds(start, QROWS), t * 128 : (t + 1) * 128] = blocks[k][
+                t * QROWS : (t + 1) * QROWS, :
+            ]
+
+        @pl.when(side == 1)
+        def _():
+            for t in range(5):
+                q_ref[part, 448:512, t * 128 : (t + 1) * 128] = blocks[k][
+                    t * QROWS + 160 : (t + 1) * QROWS, :
+                ]
+
+    def outs(k, low, high):
+        part = (me ^ k) >> 1
+        at = 5 * QROWS
+        full = jnp.concatenate(
+            [
+                low[at : at + OROWS, :],
+                low[at + OROWS :, 0:96],
+                high[at : at + OROWS, :],
+                high[at + OROWS :, 0:96],
+            ],
+            axis=1,
+        )
+        full = jnp.concatenate([full, full[:, 384:448]], axis=1)
+        for h in range(4):
+            o_ref[part, h * LANES : h * LANES + FEATURE_WIDTH, :] = jnp.zeros(
+                (FEATURE_WIDTH, 512), BF16
+            )
+            o_ref[part, h * LANES + FEATURE_WIDTH : (h + 1) * LANES, :] = full[
+                h * HDIM : (h + 1) * HDIM, :
+            ]
+
+    for k in (0, 2, 4, 6):
+
+        @pl.when((me & 1) == 0)
+        def _():
+            outs(k, blocks[k], blocks[k + 1])
+
+        @pl.when((me & 1) == 1)
+        def _():
+            outs(k, blocks[k + 1], blocks[k])
+
+
+def as_keys(kv):
+    return jnp.where(lane(kv.shape) % LANES == FEATURE_WIDTH, 1.0, kv).astype(BF16)
+
+
+def as_values(kv, keep):
+    ones = jnp.where(lane(kv.shape) % LANES < FEATURE_WIDTH, 1.0, kv)
+    return jnp.where(keep, ones, 0.0).astype(BF16)
+
+
+def prepare_cache(cache, len_ref, k_ref, v_ref, slab, sem):
+    copy = pltpu.make_async_copy(cache.at[0], slab, sem)
+    copy.start()
+    copy.wait()
+    kv = slab[...].astype(F32)
+    k_ref[...] = as_keys(kv)
+    v_ref[...] = as_values(kv, row(kv.shape) < len_ref[0])
+
+
+def project(blocks, gain_ref, w_ref, rows):
+    place = gray(lax.axis_index("col"))
+    middle = lane((HALF // 2, 128)) < 64
+    pieces, square = [], None
+    for ref in blocks:
+        tail = ref[TAIL:BODY, :].astype(F32)
+        tail = jnp.concatenate([jnp.where(middle, tail, 0.0), jnp.where(middle, 0.0, tail)], axis=0)
+        tiles = [ref[t * HALF : (t + 1) * HALF, :].astype(F32) for t in range(3)] + [tail]
+        if rows > HALF:
+            tiles = [
+                jnp.concatenate(
+                    [
+                        tile,
+                        ref[BODY + 8 * t : BODY + 8 * t + 8, :].astype(F32),
+                        jnp.zeros((8, 128), F32),
+                    ],
+                    axis=0,
+                )
+                for t, tile in enumerate(tiles)
+            ]
+        pieces.append(tiles)
+        for tile in tiles:
+            square = tile * tile if square is None else square + tile * tile
+    mean = jnp.sum(square, axis=1, keepdims=True) * (1.0 / 1792.0)
+    scale = jnp.broadcast_to(lax.rsqrt(mean + 1e-06), (rows, 128))
+    total = None
+    for k, tiles in enumerate(pieces):
+        source = gray((place + 4 - k) & 3)
+        normed = [
+            (tile * scale * gain_ref[k][BODY + 8 * t : BODY + 8 * t + 1, :].astype(F32)).astype(BF16)
+            for t, tile in enumerate(tiles)
+        ]
+        term = dot(jnp.concatenate(normed, axis=1), w_ref[source])
+        total = term if total is None else total + term
+    total = total.astype(BF16).astype(F32)
+    return total[:, 0:512], total[:, 512:640]
+
+
+def query_of(queries, h):
+    q = pltpu.roll(queries, (128 - FEATURE_WIDTH * h) % 128, 1) if h else queries
+    at = lane(q.shape)
+    return jnp.where(at < FEATURE_WIDTH, q * FEATURE_WIDTH**-0.5, 0.0), at == FEATURE_WIDTH
+
+
+def weigh(scores, keep=None):
+    weight = scores * scores + 1.0
+    if keep is not None:
+        weight = jnp.where(keep, weight, 0.0)
+    return weight.astype(BF16)
+
+
+def divide(total, mask):
+    below = jnp.broadcast_to(total[:, 0:1], total.shape) + 2.0 * (1.0 - mask)
+    return mask * total / below
+
+
+def emit(att, o_ref, first_ref, rest, tail_rows):
+    place = gray(lax.axis_index("col"))
+    for s in range(4):
+        part = dot(att, o_ref[gray((place + 3 - s) & 3)])
+        out = first_ref if s == 0 else rest[s - 1]
+        for t in range(3):
+            out[t * HALF : (t + 1) * HALF, :] = part[:HALF, t * 128 : (t + 1) * 128].astype(out.dtype)
+        last = part[:, 384:512]
+        middle = lane((HALF // 2, 128)) < 64
+        out[TAIL:BODY, :] = jnp.where(middle, last[: HALF // 2], last[HALF // 2 : HALF]).astype(out.dtype)
+        if tail_rows:
+            for t in range(4):
+                out[BODY + 8 * t : BODY + 8 * t + 8, :] = part[
+                    HALF : HALF + 8, t * 128 : (t + 1) * 128
+                ].astype(out.dtype)
+
+
+def chunk_a(a0, a1, a2, a3, w_ref, o_ref, ck_ref, cv_ref, m_ref, first, r1, r2, r3, ka_ref, va_ref):
+    blocks = (a0, a1, a2, a3)
+    kv, queries = project(blocks, blocks, w_ref, HALF)
+    mask = m_ref[0:HALF, :]
+    ka_ref[...] = as_keys(kv)
+    va_ref[...] = as_values(kv, jnp.concatenate([mask] * 4, axis=1) > 0.0)
+    causal = lane((HALF, HALF)) <= row((HALF, HALF))
+    outs = []
+    for h in range(4):
+        at = slice(h * LANES, (h + 1) * LANES)
+        q, one = query_of(queries, h)
+        q = jnp.where(one, 1.0, q).astype(BF16)
+        total = dot(weigh(dot_nt(q, ka_ref[:, at]), causal), va_ref[:, at])
+        for b in range(2):
+            keys = slice(b * 512, (b + 1) * 512)
+            total += dot(weigh(dot_nt(q, ck_ref[keys, at])), cv_ref[keys, at])
+        outs.append(divide(total, mask).astype(BF16))
+    emit(jnp.concatenate(outs, axis=1), o_ref, first, (r1, r2, r3), False)
+
+
+def chunk_b(
+    b0, b1, b2, b3, a0, a1, a2, a3, w_ref, o_ref, ck_ref, cv_ref, m_ref, ka_ref, va_ref, len_ref, cache,
+    first, r1, r2, r3, kb, vb, slab, sems,
+):
+    copies = [pltpu.make_async_copy(cache.at[d + 1], slab.at[d], sems.at[d]) for d in range(DEC)]
+    for copy in copies:
+        copy.start()
+    rows = HALF + 16
+    kv, queries = project((b0, b1, b2, b3), (a0, a1, a2, a3), w_ref, rows)
+    mask = m_ref[HALF : 2 * HALF, :]
+    kb[...] = as_keys(kv[:HALF])
+    vb[...] = as_values(kv[:HALF], jnp.concatenate([mask] * 4, axis=1) > 0.0)
+    causal = lane((HALF, HALF)) <= row((HALF, HALF))
+    outs, late = [], []
+    for h in range(4):
+        at = slice(h * LANES, (h + 1) * LANES)
+        q, one = query_of(queries, h)
+        late.append(q[HALF:])
+        q = jnp.where(one, 1.0, q)[:HALF].astype(BF16)
+        total = dot(weigh(dot_nt(q, kb[:, at]), causal), vb[:, at])
+        total += dot(weigh(dot_nt(q, ka_ref[:, at])), va_ref[:, at])
+        for b in range(2):
+            keys = slice(b * 512, (b + 1) * 512)
+            total += dot(weigh(dot_nt(q, ck_ref[keys, at])), cv_ref[keys, at])
+        outs.append(divide(total, mask))
+    late = jnp.concatenate(late, axis=1)
+    fresh = kv[HALF:]
+    own = row((16, 512)) == lane((16, 512)) // LANES
+    position = lane((16, 1024))
+    decoded = jnp.zeros((16, 512), F32)
+    for d in range(DEC):
+        copies[d].wait()
+        q = jnp.where(own, jnp.broadcast_to(late[d : d + 1], (16, 512)), 0.0)
+        new = jnp.broadcast_to(fresh[d : d + 1], (16, 512))
+        live = m_ref[2 * HALF + d : 2 * HALF + d + 1, 0:1]
+        score = dot_nt(q.astype(BF16), slab[d]) + 1.0
+        weight = jnp.where(position < len_ref[d + 1], score * score + 1.0, 0.0)
+        self_score = jnp.sum(q * new, axis=1, keepdims=True) + 1.0
+        self_weight = (self_score * self_score + 1.0) * live
+        total = dot(weight.astype(BF16), slab[d]) + self_weight.astype(BF16).astype(F32) * new
+        below = jnp.sum(weight, axis=1, keepdims=True) + self_weight + 2.0 * (1.0 - live)
+        value = jnp.sum(jnp.where(own, live * total / below, 0.0), axis=0, keepdims=True)
+        decoded = jnp.where(row((16, 512)) == d, jnp.broadcast_to(value, (16, 512)), decoded)
+    att = jnp.concatenate([jnp.concatenate(outs, axis=1), decoded], axis=0).astype(BF16)
+    emit(att, o_ref, first, (r1, r2, r3), True)
+
+
+def finish(ra, pa, rb, pb, out):
+    for recv, part, base in ((ra, pa, 0), (rb, pb, HALF)):
+        for t in range(3):
+            at = slice(t * HALF, (t + 1) * HALF)
+            out[base : base + HALF, t * 128 : (t + 1) * 128] = (
+                recv[at, :].astype(F32) + part[at, :]
+            ).astype(BF16)
+        tail = recv[TAIL:BODY, :].astype(F32) + part[TAIL:BODY, :]
+        out[base : base + HALF // 2, 384:448] = tail[:, 0:64].astype(BF16)
+        out[base + HALF // 2 : base + HALF, 384:448] = tail[:, 64:128].astype(BF16)
+    for t in range(4):
+        at = slice(BODY + 8 * t, BODY + 8 * t + DEC)
+        width = 128 if t < 3 else 64
+        late = (rb[at, :].astype(F32) + pb[at, :])[:, 0:width]
+        out[SPAN_TOKENS:, t * 128 : t * 128 + width] = late.astype(BF16)
+
+
+def shards(hidden, norm_gain, qkv_weight, out_weight, cache, cached, token_mask):
+    ring = [(gray(p), gray((p + 1) % 4)) for p in range(4)]
+
+    def onward(x):
+        return lax.ppermute(x, "col", ring)
+
+    def across(x, k):
+        return lax.ppermute(x, "row", [(i, i ^ k) for i in range(8)])
+
+    a, b = call(
+        pack_tokens,
+        (shaped((BODY + EXTRA, 128)), shaped((BODY + EXTRA, 128))),
+        [VMEM, VMEM],
+        nbytes=2_000_000,
+        name="pack_tokens",
+    )(hidden, norm_gain.reshape(1, -1))
+    a, b = [a], [b]
+    a.append(onward(a[-1]))
+    b.append(onward(b[-1]))
+    own = call(pack_weights, shaped((5 * QROWS + 2 * OROWS, 128)), [VMEM, VMEM], nbytes=2_000_000, name="pack_weights")(
+        qkv_weight, out_weight
+    )
+    plane = [own, across(own, 2), across(own, 4), across(own, 6)]
+    for _ in range(2):
+        a.append(onward(a[-1]))
+        b.append(onward(b[-1]))
+    blocks = []
+    for block in plane:
+        blocks += [block, across(block, 1)]
+    w, o = call(
+        place_weights,
+        (shaped((4, 512, 640)), shaped((4, 512, 512))),
+        [VMEM] * 8,
+        nbytes=8_000_000,
+        name="place_weights",
+    )(*blocks)
+    ck, cv = call(
+        prepare_cache,
+        (shaped((1024, 512)), shaped((1024, 512))),
+        [ANY, SMEM],
+        scratch=[pltpu.VMEM((1024, 512), BF16), pltpu.SemaphoreType.DMA],
+        nbytes=3_000_000,
+        name="prepare_cache",
+    )(cache, cached)
+    mask = jnp.broadcast_to(token_mask.astype(F32)[:, None], (token_mask.shape[0], 128))
+    body = shaped((BODY, 128), F32)
+    first, *rest_a, ka, va = call(
+        chunk_a,
+        (shaped((BODY, 128)), body, body, body, shaped((HALF, 512)), shaped((HALF, 512))),
+        [VMEM] * 9,
+        flops=4_000_000_000,
+        nbytes=12_000_000,
+        name="chunk_a",
+    )(*a, w, o, ck, cv, mask)
+    send_a = onward(first)
+    body = shaped((BODY + EXTRA, 128), F32)
+    first, *rest_b = call(
+        chunk_b,
+        (shaped((BODY + EXTRA, 128)), body, body, body),
+        [VMEM] * 15 + [SMEM, ANY],
+        scratch=[
+            pltpu.VMEM((HALF, 512), BF16),
+            pltpu.VMEM((HALF, 512), BF16),
+            pltpu.VMEM((DEC, 1024, 512), BF16),
+            pltpu.SemaphoreType.DMA((DEC,)),
+        ],
+        flops=5_000_000_000,
+        nbytes=16_000_000,
+        name="chunk_b",
+    )(*b, *a, w, o, ck, cv, mask, ka, va, cached, cache)
+    send_b = onward(first)
+    for s in range(2):
+        send_a = onward((send_a.astype(F32) + rest_a[s]).astype(BF16))
+        send_b = onward((send_b.astype(F32) + rest_b[s]).astype(BF16))
+    return call(finish, shaped(hidden.shape), [VMEM] * 4, nbytes=3_000_000, name="finish")(
+        send_a, rest_a[2], send_b, rest_b[2]
+    )
 
 
 def taylor(taylor_score):
@@ -124,7 +510,7 @@
     return result.astype(jnp.bfloat16).reshape(rows, heads_here * HDIM)
 
 
-def shards(hidden, norm_gain, qkv_weight, out_weight, cache, cached, token_mask):
+def plain_shards(hidden, norm_gain, qkv_weight, out_weight, cache, cached, token_mask):
     full, gain = (
         lax.all_gather(hidden, "col", axis=1, tiled=True),
         lax.all_gather(norm_gain, "col", axis=0, tiled=True),
@@ -162,4 +548,5 @@
         P("row"),
     )
     out_specs = P("row", "col")
-    return jax.shard_map(shards, mesh=mesh, in_specs=in_specs, out_specs=out_specs, check_vma=False)
+    body = shards if (mesh.shape["row"], mesh.shape["col"]) == (8, 4) else plain_shards
+    return jax.shard_map(body, mesh=mesh, in_specs=in_specs, out_specs=out_specs, check_vma=False)

time: 220 us -> 100 us (0.45)
  waiting for transfers between devices: 127 us -> 52.1 us
  local copies, waits for them, and re-layouts: 36.7 us -> 5.78 us
  Pallas kernels: 0 us -> 22.5 us
  matrix products: 22 us -> 0 us
  starting transfers between devices: 0.12 us -> 18.7 us
  between operations: 15.3 us -> 0.16 us
  blocking collectives: 13.9 us -> 0 us
  other arithmetic: 4.64 us -> 0.89 us
    unnamed x5 -> x0, waiting for transfers between devices: 90.5 us -> none
    ppermute x0 -> x19, waiting for transfers between devices: none -> 52.1 us  [the longest x12 46.6 us: onward(): return lax.ppermute(x, 'col', ring)]
    all_gather x3 -> x0, waiting for transfers between devices: 36.3 us -> none  [the longest x1 18.1 us: shards(): lax.all_gather(hidden, 'col', axis=1, tiled=True)]
    pallas_call x0 -> x7, Pallas kernels: none -> 22.5 us  [the longest x1 9.98 us: shards(): call(chunk_b, (shaped((BODY + EXTRA, 128)), body, body, body), [VMEM] * 1...]
    slice x13 -> x0, local copies, waits for them, and re-layouts: 19.4 us -> none  [the longest x2 11.5 us: attend(): past = store[1:]]
    ppermute x0 -> x19, starting transfers between devices: none -> 18.7 us  [the longest x12 13.1 us: onward(): return lax.ppermute(x, 'col', ring)]
    dot_general x9 -> x0, matrix products: 16.9 us -> none  [the longest x1 4.73 us: span_step(): jnp.einsum('hqk,khd->hqd', weight.astype(jnp.bfloat16), span_slice[:, :,...]
    unnamed x1 -> x0, blocking collectives: 13.9 us -> none
  transfers between devices with their start and end apart: 4 -> 19, of which waited for: 4 -> 9; matrix products, arithmetic and copies ran while one was open for 25% -> 2% of each run, Pallas kernels for 0% -> 11%
where the time goes in v1:
time: 100 us
  waiting for transfers between devices  52.1 us (52%)
  Pallas kernels  22.5 us (22%)
  starting transfers between devices  18.7 us (19%)
  local copies, waits for them, and re-layouts  5.78 us (6%)
    ppermute x12, waiting for transfers between devices, onward(): return lax.ppermute(x, 'col', ring)  46.6 us
    ppermute x12, starting transfers between devices, onward(): return lax.ppermute(x, 'col', ring)  13.1 us
    pallas_call x1, Pallas kernels, shards(): call(chunk_b, (shaped((BODY + EXTRA, 128)), body, body, body), [VMEM] * 1...  9.98 us
    pallas_call x1, Pallas kernels, shards(): call(chunk_a, (shaped((BODY, 128)), body, body, body, shaped((HALF, 512))...  6.24 us
    ppermute x7, starting transfers between devices, across(): return lax.ppermute(x, 'row', [(i, i ^ k) for i in range(8)])  5.57 us
    ppermute x7, waiting for transfers between devices, across(): return lax.ppermute(x, 'row', [(i, i ^ k) for i in range(8)])  5.52 us
    unnamed x14, local copies, waits for them, and re-layouts  4.98 us
    pallas_call x1, Pallas kernels, shards(): call(place_weights, (shaped((4, 512, 640)), shaped((4, 512, 512))), [VMEM...  2.92 us
  transfers between devices with their start and end apart: 19, of which 9 were waited for; matrix products, arithmetic and copies ran while one was open for 2% of the time, Pallas kernels for 11%

profile of v1, /device:TPU:0, one launch (start us, length us, event | category | flops | bytes accessed | tf_op | source)
XLA Modules:
  0.0 100.2 jit_solution(1715741152359685313)
XLA Ops:
  0.0 1.0 copy-done.1
  2.1 3.0 %collective-permute-start.4 = (bf16[2016,128]{1,0:T(8,128)(2,1)S(1)}, bf16[2016,128]{1,0:T(8,128)(2,1)S(1)}, u32[]{:S(2)}, u32[]{:S(2)}) collective-permute-start(bf16[2016,128]{1,0:T(8,128)(2,1)S(1)} %pack_weights.1.refs_0_), channel_id=1, source_target_pairs={{0,8},{4,12},{8,0},{12,4},{16,24},{20,28},{24,16},{28,20},{1,9},{5... | collective-permute-start | bytes 1548296 | tf_op jit(solution)/shard_map/ppermute | solution.py:326
  5.1 1.5 %collective-permute-start.6 = (bf16[2016,128]{1,0:T(8,128)(2,1)S(1)}, bf16[2016,128]{1,0:T(8,128)(2,1)S(1)}, u32[]{:S(2)}, u32[]{:S(2)}) collective-permute-start(bf16[2016,128]{1,0:T(8,128)(2,1)S(1)} %pack_weights.1.refs_0_), channel_id=1, source_target_pairs={{0,16},{4,20},{8,24},{12,28},{16,0},{20,4},{24,8},{28,12},{1,17},{... | collective-permute-start | bytes 1548296 | tf_op jit(solution)/shard_map/ppermute | solution.py:326
  7.3 1.0 %copy-done = bf16[516,448]{1,0:T(8,128)(2,1)S(1)} copy-done((bf16[516,448]{1,0:T(8,128)(2,1)S(1)}, bf16[516,448]{1,0:T(8,128)(2,1)}, u32[]{:S(2)}) %copy-start) | copy-done | bytes 462360
  8.4 2.1 %collective-permute-start = (bf16[928,128]{1,0:T(8,128)(2,1)S(1)}, bf16[928,128]{1,0:T(8,128)(2,1)S(1)}, u32[]{:S(2)}, u32[]{:S(2)}) collective-permute-start(bf16[928,128]{1,0:T(8,128)(2,1)S(1)} %get-tuple-element.21.a0), channel_id=1, source_target_pairs={{0,1},{1,3},{3,2},{2,0},{4,5},{5,7},{7,6},{6,4},{8,9},{9,11},{11,1... | collective-permute-start | bytes 712712 | tf_op jit(solution)/shard_map/ppermute | solution.py:323
  10.5 2.6 %collective-permute-start.13 = (bf16[928,128]{1,0:T(8,128)(2,1)S(1)}, bf16[928,128]{1,0:T(8,128)(2,1)S(1)}, u32[]{:S(2)}, u32[]{:S(2)}) collective-permute-start(bf16[928,128]{1,0:T(8,128)(2,1)S(1)} %get-tuple-element.30.b0), channel_id=1, source_target_pairs={{0,1},{1,3},{3,2},{2,0},{4,5},{5,7},{7,6},{6,4},{8,9},{9,11},{11,1... | collective-permute-start | bytes 712712 | tf_op jit(solution)/shard_map/ppermute | solution.py:323
  13.1 5.1 %collective-permute-done.a1 = bf16[928,128]{1,0:T(8,128)(2,1)S(1)} collective-permute-done((bf16[928,128]{1,0:T(8,128)(2,1)S(1)}, bf16[928,128]{1,0:T(8,128)(2,1)S(1)}, u32[]{:S(2)}, u32[]{:S(2)}) %collective-permute-start) | collective-permute-done | bytes 237600 | tf_op jit(solution)/shard_map/ppermute | solution.py:323
  18.2 1.1 %collective-permute-start.1 = (bf16[928,128]{1,0:T(8,128)(2,1)S(1)}, bf16[928,128]{1,0:T(8,128)(2,1)S(1)}, u32[]{:S(2)}, u32[]{:S(2)}) collective-permute-start(bf16[928,128]{1,0:T(8,128)(2,1)S(1)} %collective-permute-done.a1), channel_id=1, source_target_pairs={{0,1},{1,3},{3,2},{2,0},{4,5},{5,7},{7,6},{6,4},{8,9},{9,11},{11,1... | collective-permute-start | bytes 712712 | tf_op jit(solution)/shard_map/ppermute | solution.py:323
  19.4 4.0 %collective-permute-done.13.b1 = bf16[928,128]{1,0:T(8,128)(2,1)S(1)} collective-permute-done((bf16[928,128]{1,0:T(8,128)(2,1)S(1)}, bf16[928,128]{1,0:T(8,128)(2,1)S(1)}, u32[]{:S(2)}, u32[]{:S(2)}) %collective-permute-start.13) | collective-permute-done | bytes 237600 | tf_op jit(solution)/shard_map/ppermute | solution.py:323
  23.9 5.5 %collective-permute-done.6.refs_4_ = bf16[2016,128]{1,0:T(8,128)(2,1)S(1)} collective-permute-done((bf16[2016,128]{1,0:T(8,128)(2,1)S(1)}, bf16[2016,128]{1,0:T(8,128)(2,1)S(1)}, u32[]{:S(2)}, u32[]{:S(2)}) %collective-permute-start.6) | collective-permute-done | bytes 516128 | tf_op jit(solution)/shard_map/ppermute | solution.py:326
  29.9 1.6 %collective-permute-start.14 = (bf16[928,128]{1,0:T(8,128)(2,1)S(1)}, bf16[928,128]{1,0:T(8,128)(2,1)S(1)}, u32[]{:S(2)}, u32[]{:S(2)}) collective-permute-start(bf16[928,128]{1,0:T(8,128)(2,1)S(1)} %collective-permute-done.13.b1), channel_id=1, source_target_pairs={{0,1},{1,3},{3,2},{2,0},{4,5},{5,7},{7,6},{6,4},{8,9},{9,11},{11,1... | collective-permute-start | bytes 712712 | tf_op jit(solution)/shard_map/ppermute | solution.py:323
  31.5 7.1 %collective-permute-done.14.b2 = bf16[928,128]{1,0:T(8,128)(2,1)S(1)} collective-permute-done((bf16[928,128]{1,0:T(8,128)(2,1)S(1)}, bf16[928,128]{1,0:T(8,128)(2,1)S(1)}, u32[]{:S(2)}, u32[]{:S(2)}) %collective-permute-start.14) | collective-permute-done | bytes 237600 | tf_op jit(solution)/shard_map/ppermute | solution.py:323
  40.6 2.2 %prepare_cache.1 = (bf16[1024,512]{1,0:T(8,128)(2,1)S(1)}, bf16[1024,512]{1,0:T(8,128)(2,1)S(1)}) custom-call(bf16[5,1024,512]{2,1,0:T(8,128)(2,1)} %cache.3, s32[5]{0:T(128)S(1)} %copy-done.3), custom_call_target="tpu_custom_call" | custom-call | bytes 3000000 | tf_op jit(solution)/shard_map/prepare_cache/pallas_call | solution.py:355
  42.9 3.4 %collective-permute-start.15 = (bf16[928,128]{1,0:T(8,128)(2,1)S(1)}, bf16[928,128]{1,0:T(8,128)(2,1)S(1)}, u32[]{:S(2)}, u32[]{:S(2)}) collective-permute-start(bf16[928,128]{1,0:T(8,128)(2,1)S(1)} %collective-permute-done.14.b2), channel_id=1, source_target_pairs={{0,1},{1,3},{3,2},{2,0},{4,5},{5,7},{7,6},{6,4},{8,9},{9,11},{11,1... | collective-permute-start | bytes 712712 | tf_op jit(solution)/shard_map/ppermute | solution.py:323
  46.3 2.9 %place_weights.1 = (bf16[4,512,640]{2,1,0:T(8,128)(2,1)}, bf16[4,512,512]{2,1,0:T(8,128)(2,1)S(1)}) custom-call(bf16[2016,128]{1,0:T(8,128)(2,1)S(1)} %pack_weights.1.refs_0_, bf16[2016,128]{1,0:T(8,128)(2,1)S(1)} %collective-permute-done.3.refs_1_, bf16[2016,128]{1,0:T(8,128)(2,1)S(1)} %collective-permute-done.4.refs_2_, ...), custom_call_target="tpu_custom_call" | custom-call | bytes 8000000 | tf_op jit(solution)/shard_map/place_weights/pallas_call | solution.py:348
  49.3 1.4 %copy-done.5 = bf16[4,512,512]{2,1,0:T(8,128)(2,1)} copy-done((bf16[4,512,512]{2,1,0:T(8,128)(2,1)}, bf16[4,512,512]{2,1,0:T(8,128)(2,1)S(1)}, u32[]{:S(2)}) %copy-start.5) | copy-done | bytes 2097176
  50.8 6.2 %chunk_a.1 = (bf16[896,128]{1,0:T(8,128)(2,1)S(1)}, f32[896,128]{1,0:T(8,128)S(1)}, f32[896,128]{1,0:T(8,128)S(1)}, f32[896,128]{1,0:T(8,128)S(1)}, bf16[256,512...) custom-call(bf16[928,128]{1,0:T(8,128)(2,1)S(1)} %get-tuple-element.21.a0, bf16[928,128]{1,0:T(8,128)(2,1)S(1)} %collective-permute-done.a1, ...), custom_call_target="tpu_custom_call" | custom-call | flops 4000000000 | bytes 12000000 | tf_op jit(solution)/shard_map/chunk_a/pallas_call | solution.py:365
  57.1 10.0 %chunk_b.1 = (bf16[928,128]{1,0:T(8,128)(2,1)S(1)}, f32[928,128]{1,0:T(8,128)S(1)}, f32[928,128]{1,0:T(8,128)S(1)}, f32[928,128]{1,0:T(8,128)S(1)}) custom-call(bf16[928,128]{1,0:T(8,128)(2,1)S(1)} %get-tuple-element.30.b0, bf16[928,128]{1,0:T(8,128)(2,1)S(1)} %collective-permute-done.13.b1, bf16[928,128]{1,0:T(8,128)(2,1)S(1)} %collective-permute-done.14.b2, ...), custom_call_target="tpu_custom_call" | custom-call | flops 5000000000 | bytes 16000000 | tf_op jit(solution)/shard_map/chunk_b/pallas_call | solution.py:375
  67.1 1.2 %collective-permute-start.10 = (bf16[896,128]{1,0:T(8,128)(2,1)S(1)}, bf16[896,128]{1,0:T(8,128)(2,1)S(1)}, u32[]{:S(2)}, u32[]{:S(2)}) collective-permute-start(bf16[896,128]{1,0:T(8,128)(2,1)S(1)} %get-tuple-element.26), channel_id=1, source_target_pairs={{0,1},{1,3},{3,2},{2,0},{4,5},{5,7},{7,6},{6,4},{8,9},{9,11},{11,1... | collective-permute-start | bytes 688136 | tf_op jit(solution)/shard_map/ppermute | solution.py:323
  68.3 8.4 %collective-permute-done.16 = bf16[928,128]{1,0:T(8,128)(2,1)S(1)} collective-permute-done((bf16[928,128]{1,0:T(8,128)(2,1)S(1)}, bf16[928,128]{1,0:T(8,128)(2,1)S(1)}, u32[]{:S(2)}, u32[]{:S(2)}) %collective-permute-start.16) | collective-permute-done | bytes 237600 | tf_op jit(solution)/shard_map/ppermute | solution.py:323
  76.8 4.8 %collective-permute-done.10 = bf16[896,128]{1,0:T(8,128)(2,1)S(1)} collective-permute-done((bf16[896,128]{1,0:T(8,128)(2,1)S(1)}, bf16[896,128]{1,0:T(8,128)(2,1)S(1)}, u32[]{:S(2)}, u32[]{:S(2)}) %collective-permute-start.10) | collective-permute-done | bytes 229408 | tf_op jit(solution)/shard_map/ppermute | solution.py:323
  81.7 5.0 %collective-permute-done.17 = bf16[928,128]{1,0:T(8,128)(2,1)S(1)} collective-permute-done((bf16[928,128]{1,0:T(8,128)(2,1)S(1)}, bf16[928,128]{1,0:T(8,128)(2,1)S(1)}, u32[]{:S(2)}, u32[]{:S(2)}) %collective-permute-start.17) | collective-permute-done | bytes 237600 | tf_op jit(solution)/shard_map/ppermute | solution.py:323
  86.8 4.8 %collective-permute-done.11 = bf16[896,128]{1,0:T(8,128)(2,1)S(1)} collective-permute-done((bf16[896,128]{1,0:T(8,128)(2,1)S(1)}, bf16[896,128]{1,0:T(8,128)(2,1)S(1)}, u32[]{:S(2)}, u32[]{:S(2)}) %collective-permute-start.11) | collective-permute-done | bytes 229408 | tf_op jit(solution)/shard_map/ppermute | solution.py:323
  91.8 7.5 %collective-permute-done.12.ra = bf16[896,128]{1,0:T(8,128)(2,1)S(1)} collective-permute-done((bf16[896,128]{1,0:T(8,128)(2,1)S(1)}, bf16[896,128]{1,0:T(8,128)(2,1)S(1)}, u32[]{:S(2)}, u32[]{:S(2)}) %collective-permute-start.12) | collective-permute-done | bytes 229408 | tf_op jit(solution)/shard_map/ppermute | solution.py:323
  (42 shorter events, 6.7 us)
Async XLA Ops:
  0.0 1.0 copy-start.1
  2.1 21.3 %collective-permute-start.4 = (bf16[2016,128]{1,0:T(8,128)(2,1)S(1)}, bf16[2016,128]{1,0:T(8,128)(2,1)S(1)}, u32[]{:S(2)}, u32[]{:S(2)}) collective-permute-start(bf16[2016,128]{1,0:T(8,128)(2,1)S(1)} %pack_weights.1.refs_0_), channel_id=1, source_target_pairs={{0,8},{4,12},{8,0},{12,4},{16,24},{20,28},{24,16},{28,20},{1,9},{5... | collective-permute-start | bytes 1548296 | tf_op jit(solution)/shard_map/ppermute | solution.py:326
  5.1 24.3 %collective-permute-start.6 = (bf16[2016,128]{1,0:T(8,128)(2,1)S(1)}, bf16[2016,128]{1,0:T(8,128)(2,1)S(1)}, u32[]{:S(2)}, u32[]{:S(2)}) collective-permute-start(bf16[2016,128]{1,0:T(8,128)(2,1)S(1)} %pack_weights.1.refs_0_), channel_id=1, source_target_pairs={{0,16},{4,20},{8,24},{12,28},{16,0},{20,4},{24,8},{28,12},{1,17},{... | collective-permute-start | bytes 1548296 | tf_op jit(solution)/shard_map/ppermute | solution.py:326
  6.6 22.8 %collective-permute-start.8 = (bf16[2016,128]{1,0:T(8,128)(2,1)S(1)}, bf16[2016,128]{1,0:T(8,128)(2,1)S(1)}, u32[]{:S(2)}, u32[]{:S(2)}) collective-permute-start(bf16[2016,128]{1,0:T(8,128)(2,1)S(1)} %pack_weights.1.refs_0_), channel_id=1, source_target_pairs={{0,24},{4,28},{8,16},{12,20},{16,8},{20,12},{24,0},{28,4},{1,25},{... | collective-permute-start | bytes 1548296 | tf_op jit(solution)/shard_map/ppermute | solution.py:326
  7.3 1.0 %copy-start = (bf16[516,448]{1,0:T(8,128)(2,1)S(1)}, bf16[516,448]{1,0:T(8,128)(2,1)}, u32[]{:S(2)}) copy-start(bf16[516,448]{1,0:T(8,128)(2,1)} %h_ref.1) | copy-start | bytes 1387012
  8.4 9.8 %collective-permute-start = (bf16[928,128]{1,0:T(8,128)(2,1)S(1)}, bf16[928,128]{1,0:T(8,128)(2,1)S(1)}, u32[]{:S(2)}, u32[]{:S(2)}) collective-permute-start(bf16[928,128]{1,0:T(8,128)(2,1)S(1)} %get-tuple-element.21.a0), channel_id=1, source_target_pairs={{0,1},{1,3},{3,2},{2,0},{4,5},{5,7},{7,6},{6,4},{8,9},{9,11},{11,1... | collective-permute-start | bytes 712712 | tf_op jit(solution)/shard_map/ppermute | solution.py:323
  10.5 12.8 %collective-permute-start.13 = (bf16[928,128]{1,0:T(8,128)(2,1)S(1)}, bf16[928,128]{1,0:T(8,128)(2,1)S(1)}, u32[]{:S(2)}, u32[]{:S(2)}) collective-permute-start(bf16[928,128]{1,0:T(8,128)(2,1)S(1)} %get-tuple-element.30.b0), channel_id=1, source_target_pairs={{0,1},{1,3},{3,2},{2,0},{4,5},{5,7},{7,6},{6,4},{8,9},{9,11},{11,1... | collective-permute-start | bytes 712712 | tf_op jit(solution)/shard_map/ppermute | solution.py:323
  18.2 11.6 %collective-permute-start.1 = (bf16[928,128]{1,0:T(8,128)(2,1)S(1)}, bf16[928,128]{1,0:T(8,128)(2,1)S(1)}, u32[]{:S(2)}, u32[]{:S(2)}) collective-permute-start(bf16[928,128]{1,0:T(8,128)(2,1)S(1)} %collective-permute-done.a1), channel_id=1, source_target_pairs={{0,1},{1,3},{3,2},{2,0},{4,5},{5,7},{7,6},{6,4},{8,9},{9,11},{11,1... | collective-permute-start | bytes 712712 | tf_op jit(solution)/shard_map/ppermute | solution.py:323
  23.3 19.5 %collective-permute-start.3 = (bf16[2016,128]{1,0:T(8,128)(2,1)S(1)}, bf16[2016,128]{1,0:T(8,128)(2,1)S(1)}, u32[]{:S(2)}, u32[]{:S(2)}) collective-permute-start(bf16[2016,128]{1,0:T(8,128)(2,1)S(1)} %pack_weights.1.refs_0_), channel_id=1, source_target_pairs={{0,4},{4,0},{8,12},{12,8},{16,20},{20,16},{24,28},{28,24},{1,5},{5... | collective-permute-start | bytes 1548296 | tf_op jit(solution)/shard_map/ppermute | solution.py:326
  23.3 23.0 %collective-permute-start.5 = (bf16[2016,128]{1,0:T(8,128)(2,1)S(1)}, bf16[2016,128]{1,0:T(8,128)(2,1)S(1)}, u32[]{:S(2)}, u32[]{:S(2)}) collective-permute-start(bf16[2016,128]{1,0:T(8,128)(2,1)S(1)} %collective-permute-done.4.refs_2_), channel_id=1, source_target_pairs={{0,4},{4,0},{8,12},{12,8},{16,20},{20,16},{24,28},{28,24},{1,5},{5... | collective-permute-start | bytes 1548296 | tf_op jit(solution)/shard_map/ppermute | solution.py:326
  29.4 17.0 %collective-permute-start.7 = (bf16[2016,128]{1,0:T(8,128)(2,1)S(1)}, bf16[2016,128]{1,0:T(8,128)(2,1)S(1)}, u32[]{:S(2)}, u32[]{:S(2)}) collective-permute-start(bf16[2016,128]{1,0:T(8,128)(2,1)S(1)} %collective-permute-done.6.refs_4_), channel_id=1, source_target_pairs={{0,4},{4,0},{8,12},{12,8},{16,20},{20,16},{24,28},{28,24},{1,5},{5... | collective-permute-start | bytes 1548296 | tf_op jit(solution)/shard_map/ppermute | solution.py:326
  29.4 17.0 %collective-permute-start.9 = (bf16[2016,128]{1,0:T(8,128)(2,1)S(1)}, bf16[2016,128]{1,0:T(8,128)(2,1)S(1)}, u32[]{:S(2)}, u32[]{:S(2)}) collective-permute-start(bf16[2016,128]{1,0:T(8,128)(2,1)S(1)} %collective-permute-done.8.refs_6_), channel_id=1, source_target_pairs={{0,4},{4,0},{8,12},{12,8},{16,20},{20,16},{24,28},{28,24},{1,5},{5... | collective-permute-start | bytes 1548296 | tf_op jit(solution)/shard_map/ppermute | solution.py:326
  29.9 8.6 %collective-permute-start.14 = (bf16[928,128]{1,0:T(8,128)(2,1)S(1)}, bf16[928,128]{1,0:T(8,128)(2,1)S(1)}, u32[]{:S(2)}, u32[]{:S(2)}) collective-permute-start(bf16[928,128]{1,0:T(8,128)(2,1)S(1)} %collective-permute-done.13.b1), channel_id=1, source_target_pairs={{0,1},{1,3},{3,2},{2,0},{4,5},{5,7},{7,6},{6,4},{8,9},{9,11},{11,1... | collective-permute-start | bytes 712712 | tf_op jit(solution)/shard_map/ppermute | solution.py:323
  38.5 12.1 %collective-permute-start.2 = (bf16[928,128]{1,0:T(8,128)(2,1)S(1)}, bf16[928,128]{1,0:T(8,128)(2,1)S(1)}, u32[]{:S(2)}, u32[]{:S(2)}) collective-permute-start(bf16[928,128]{1,0:T(8,128)(2,1)S(1)} %collective-permute-done.1.a2), channel_id=1, source_target_pairs={{0,1},{1,3},{3,2},{2,0},{4,5},{5,7},{7,6},{6,4},{8,9},{9,11},{11,1... | collective-permute-start | bytes 712712 | tf_op jit(solution)/shard_map/ppermute | solution.py:323
  42.9 14.2 %copy-start.6 = (bf16[1024,512]{1,0:T(8,128)(2,1)}, bf16[1024,512]{1,0:T(8,128)(2,1)S(1)}, u32[]{:S(2)}) copy-start(bf16[1024,512]{1,0:T(8,128)(2,1)S(1)} %get-tuple-element.25.cv_ref) | copy-start | bytes 3145732
  42.9 14.1 %collective-permute-start.15 = (bf16[928,128]{1,0:T(8,128)(2,1)S(1)}, bf16[928,128]{1,0:T(8,128)(2,1)S(1)}, u32[]{:S(2)}, u32[]{:S(2)}) collective-permute-start(bf16[928,128]{1,0:T(8,128)(2,1)S(1)} %collective-permute-done.14.b2), channel_id=1, source_target_pairs={{0,1},{1,3},{3,2},{2,0},{4,5},{5,7},{7,6},{6,4},{8,9},{9,11},{11,1... | collective-permute-start | bytes 712712 | tf_op jit(solution)/shard_map/ppermute | solution.py:323
  49.3 1.4 %copy-start.5 = (bf16[4,512,512]{2,1,0:T(8,128)(2,1)}, bf16[4,512,512]{2,1,0:T(8,128)(2,1)S(1)}, u32[]{:S(2)}) copy-start(bf16[4,512,512]{2,1,0:T(8,128)(2,1)S(1)} %get-tuple-element.23.o_ref) | copy-start | bytes 6291460
  50.8 6.3 %copy-start.4 = (s32[5]{0:T(128)S(1)}, s32[5]{0:T(128)}, u32[]{:S(2)}) copy-start(s32[5]{0:T(128)} %len_ref.3) | copy-start | bytes 64
  67.0 9.7 %collective-permute-start.16 = (bf16[928,128]{1,0:T(8,128)(2,1)S(1)}, bf16[928,128]{1,0:T(8,128)(2,1)S(1)}, u32[]{:S(2)}, u32[]{:S(2)}) collective-permute-start(bf16[928,128]{1,0:T(8,128)(2,1)S(1)} %get-tuple-element.33), channel_id=1, source_target_pairs={{0,1},{1,3},{3,2},{2,0},{4,5},{5,7},{7,6},{6,4},{8,9},{9,11},{11,1... | collective-permute-start | bytes 712712 | tf_op jit(solution)/shard_map/ppermute | solution.py:323
  67.1 14.5 %collective-permute-start.10 = (bf16[896,128]{1,0:T(8,128)(2,1)S(1)}, bf16[896,128]{1,0:T(8,128)(2,1)S(1)}, u32[]{:S(2)}, u32[]{:S(2)}) collective-permute-start(bf16[896,128]{1,0:T(8,128)(2,1)S(1)} %get-tuple-element.26), channel_id=1, source_target_pairs={{0,1},{1,3},{3,2},{2,0},{4,5},{5,7},{7,6},{6,4},{8,9},{9,11},{11,1... | collective-permute-start | bytes 688136 | tf_op jit(solution)/shard_map/ppermute | solution.py:323
  76.8 10.0 %collective-permute-start.17 = (bf16[928,128]{1,0:T(8,128)(2,1)S(1)}, bf16[928,128]{1,0:T(8,128)(2,1)S(1)}, u32[]{:S(2)}, u32[]{:S(2)}) collective-permute-start(bf16[928,128]{1,0:T(8,128)(2,1)S(1)} %add_convert_fusion.1), channel_id=1, source_target_pairs={{0,1},{1,3},{3,2},{2,0},{4,5},{5,7},{7,6},{6,4},{8,9},{9,11},{11,1... | collective-permute-start | bytes 712712 | tf_op jit(solution)/shard_map/ppermute | solution.py:323
  81.7 10.0 %collective-permute-start.11 = (bf16[896,128]{1,0:T(8,128)(2,1)S(1)}, bf16[896,128]{1,0:T(8,128)(2,1)S(1)}, u32[]{:S(2)}, u32[]{:S(2)}) collective-permute-start(bf16[896,128]{1,0:T(8,128)(2,1)S(1)} %add_convert_fusion.3), channel_id=1, source_target_pairs={{0,1},{1,3},{3,2},{2,0},{4,5},{5,7},{7,6},{6,4},{8,9},{9,11},{11,1... | collective-permute-start | bytes 688136 | tf_op jit(solution)/shard_map/ppermute | solution.py:323
  86.8 12.5 %collective-permute-start.18 = (bf16[928,128]{1,0:T(8,128)(2,1)S(1)}, bf16[928,128]{1,0:T(8,128)(2,1)S(1)}, u32[]{:S(2)}, u32[]{:S(2)}) collective-permute-start(bf16[928,128]{1,0:T(8,128)(2,1)S(1)} %add_convert_fusion), channel_id=1, source_target_pairs={{0,1},{1,3},{3,2},{2,0},{4,5},{5,7},{7,6},{6,4},{8,9},{9,11},{11,1... | collective-permute-start | bytes 712712 | tf_op jit(solution)/shard_map/ppermute | solution.py:323
  91.7 7.6 %collective-permute-start.12 = (bf16[896,128]{1,0:T(8,128)(2,1)S(1)}, bf16[896,128]{1,0:T(8,128)(2,1)S(1)}, u32[]{:S(2)}, u32[]{:S(2)}) collective-permute-start(bf16[896,128]{1,0:T(8,128)(2,1)S(1)} %add_convert_fusion.2), channel_id=1, source_target_pairs={{0,1},{1,3},{3,2},{2,0},{4,5},{5,7},{7,6},{6,4},{8,9},{9,11},{11,1... | collective-permute-start | bytes 688136 | tf_op jit(solution)/shard_map/ppermute | solution.py:323
  (2 other events, 1.6 us)

commit v2 on v1

--- a/solution.py
+++ b/solution.py
@@ -15,19 +15,20 @@
 HALF = SPAN_TOKENS // 2
 VMEM = pl.BlockSpec(memory_space=pltpu.VMEM)
 SMEM = pl.BlockSpec(memory_space=pltpu.SMEM)
-ANY = pl.BlockSpec(memory_space=pl.ANY)
+HBM = pl.BlockSpec(memory_space=pltpu.MemorySpace.HBM)
 TAIL = 3 * HALF
 BODY = TAIL + HALF // 2
 EXTRA = 32
 QROWS = 224
 OROWS = 448
+WROWS = 4 * QROWS + 2 * OROWS
 
 
 def gray(place):
     return place ^ (place >> 1)
 
 
-def call(body, outs, in_specs, scratch=(), flops=0, nbytes=0, name=None):
+def call(body, outs, in_specs, scratch=(), flops=0, nbytes=0, name=None, mib=8):
     return pl.pallas_call(
         body,
         out_shape=outs,
@@ -35,7 +36,7 @@
         out_specs=jax.tree.map(lambda _: VMEM, outs),
         scratch_shapes=scratch,
         cost_estimate=pl.CostEstimate(flops=flops, bytes_accessed=nbytes, transcendentals=0),
-        compiler_params=pltpu.CompilerParams(vmem_limit_bytes=48 * 1024 * 1024),
+        compiler_params=pltpu.CompilerParams(vmem_limit_bytes=mib * 1024 * 1024),
         name=name,
     )
 
@@ -60,7 +61,13 @@
     return lax.broadcasted_iota(jnp.int32, shape, 0)
 
 
-def pack_tokens(h_ref, g_ref, a_ref, b_ref):
+def pack(hidden, gains, qkv, outs, a_ref, b_ref, w_ref, h_ref, g_ref, q_ref, o_ref, sems):
+    pairs = ((hidden, h_ref), (gains, g_ref), (qkv, q_ref), (outs, o_ref))
+    copies = [pltpu.make_async_copy(*pair, sems.at[n]) for n, pair in enumerate(pairs)]
+    for copy in copies:
+        copy.start()
+    copies[0].wait()
+    copies[1].wait()
     for ref, base in ((a_ref, 0), (b_ref, HALF)):
         for t in range(3):
             ref[t * HALF : (t + 1) * HALF, :] = h_ref[base : base + HALF, t * 128 : (t + 1) * 128]
@@ -68,77 +75,58 @@
         high = h_ref[base + HALF // 2 : base + HALF, 384:448]
         ref[TAIL:BODY, :] = jnp.concatenate([low, high], axis=1)
         ref[BODY:, :] = jnp.zeros((EXTRA, 128), BF16)
+    gain = g_ref[...].reshape(1, 448)
     for t in range(3):
-        a_ref[BODY + 8 * t : BODY + 8 * t + 1, :] = g_ref[:, t * 128 : (t + 1) * 128]
+        a_ref[BODY + 8 * t : BODY + 8 * t + 1, :] = gain[:, t * 128 : (t + 1) * 128]
         b_ref[BODY + 8 * t : BODY + 8 * t + DEC, :] = h_ref[SPAN_TOKENS:, t * 128 : (t + 1) * 128]
-    last = g_ref[:, 384:448]
+    last = gain[:, 384:448]
     a_ref[BODY + 24 : BODY + 25, :] = jnp.concatenate([last, last], axis=1)
     b_ref[BODY + 24 : BODY + 24 + DEC, 0:64] = h_ref[SPAN_TOKENS:, 384:448]
-
-
-def pack_weights(q_ref, o_ref, w_ref):
+    copies[2].wait()
+    copies[3].wait()
     width = FEATURE_WIDTH + LANES
     for h in range(4):
         w_ref[h * QROWS : (h + 1) * QROWS, :] = q_ref[:, h * width + FEATURE_WIDTH : (h + 1) * width]
-    queries = [q_ref[:, h * width : h * width + FEATURE_WIDTH] for h in range(4)]
-    w_ref[4 * QROWS : 5 * QROWS, :] = jnp.concatenate(
-        queries + [jnp.zeros((QROWS, 64), BF16)], axis=1
-    )
-    w_ref[5 * QROWS : 5 * QROWS + OROWS, :] = o_ref[:, 0:128]
-    w_ref[5 * QROWS + OROWS :, :] = jnp.concatenate(
-        [o_ref[:, 128:224], jnp.zeros((OROWS, 32), BF16)], axis=1
-    )
+    at = 4 * QROWS
+    w_ref[at : at + OROWS, :] = o_ref[:, 0:128]
+    for side in range(2):
+        pieces = [o_ref[side * QROWS : (side + 1) * QROWS, 128:224]]
+        for h in (2 * side, 2 * side + 1):
+            pieces.append(q_ref[:, h * width : h * width + FEATURE_WIDTH])
+        rows = at + OROWS + side * QROWS
+        w_ref[rows : rows + QROWS, :] = jnp.concatenate(pieces, axis=1)
 
 
 def place_weights(*refs):
-    blocks, (q_ref, o_ref) = refs[:8], refs[8:]
+    blocks, (w_ref, o_ref) = refs[:8], refs[8:]
     me = lax.axis_index("row")
-    for k in range(8):
-        owner = me ^ k
-        part, side = owner >> 1, owner & 1
-        start = pl.multiple_of(side * QROWS, 32)
-        for t in range(5):
-            q_ref[part, pl.ds(start, QROWS), t * 128 : (t + 1) * 128] = blocks[k][
-                t * QROWS : (t + 1) * QROWS, :
-            ]
-
-        @pl.when(side == 1)
+    at, late = 4 * QROWS, 4 * QROWS + OROWS
+
+    def project_rows(block):
+        queries = [block[late + s * QROWS : late + (s + 1) * QROWS, 96:128] for s in range(2)]
+        queries.append(jnp.zeros((QROWS, 64), BF16))
+        heads = [block[h * QROWS : (h + 1) * QROWS, :] for h in range(4)]
+        return heads + [jnp.concatenate(queries, axis=1)]
+
+    for core in range(2):
+
+        @pl.when(me & 1 == core)
         def _():
-            for t in range(5):
-                q_ref[part, 448:512, t * 128 : (t + 1) * 128] = blocks[k][
-                    t * QROWS + 160 : (t + 1) * QROWS, :
-                ]
-
-    def outs(k, low, high):
-        part = (me ^ k) >> 1
-        at = 5 * QROWS
-        full = jnp.concatenate(
-            [
-                low[at : at + OROWS, :],
-                low[at + OROWS :, 0:96],
-                high[at : at + OROWS, :],
-                high[at + OROWS :, 0:96],
-            ],
-            axis=1,
-        )
-        full = jnp.concatenate([full, full[:, 384:448]], axis=1)
-        for h in range(4):
-            o_ref[part, h * LANES : h * LANES + FEATURE_WIDTH, :] = jnp.zeros(
-                (FEATURE_WIDTH, 512), BF16
-            )
-            o_ref[part, h * LANES + FEATURE_WIDTH : (h + 1) * LANES, :] = full[
-                h * HDIM : (h + 1) * HDIM, :
-            ]
-
-    for k in (0, 2, 4, 6):
-
-        @pl.when((me & 1) == 0)
-        def _():
-            outs(k, blocks[k], blocks[k + 1])
-
-        @pl.when((me & 1) == 1)
-        def _():
-            outs(k, blocks[k + 1], blocks[k])
+            for k in range(4):
+                j = (me >> 1) ^ k
+                low, high = blocks[2 * k + core], blocks[2 * k + 1 - core]
+                for t, tile in enumerate(project_rows(low)):
+                    w_ref[j, 0:QROWS, t * 128 : (t + 1) * 128] = tile
+                for t, tile in enumerate(project_rows(high)):
+                    w_ref[j, QROWS : 2 * QROWS, t * 128 : (t + 1) * 128] = tile
+                    w_ref[j, 448:512, t * 128 : (t + 1) * 128] = tile[160:QROWS, :]
+                full = jnp.concatenate(
+                    [low[at:late, :], low[late:, 0:96], high[at:late, :], high[late:, 0:96]], axis=1
+                )
+                full = jnp.concatenate([full, full[:, 384:448]], axis=1)
+                for h in range(4):
+                    o_ref[j, h * LANES : h * LANES + FEATURE_WIDTH, :] = jnp.zeros((FEATURE_WIDTH, 512), BF16)
+                    o_ref[j, h * LANES + FEATURE_WIDTH : (h + 1) * LANES, :] = full[h * HDIM : (h + 1) * HDIM, :]
 
 
 def as_keys(kv):
@@ -159,8 +147,7 @@
     v_ref[...] = as_values(kv, row(kv.shape) < len_ref[0])
 
 
-def project(blocks, gain_ref, w_ref, rows):
-    place = gray(lax.axis_index("col"))
+def norm(blocks, gain_ref, out_ref, rows):
     middle = lane((HALF // 2, 128)) < 64
     pieces, square = [], None
     for ref in blocks:
@@ -184,14 +171,25 @@
             square = tile * tile if square is None else square + tile * tile
     mean = jnp.sum(square, axis=1, keepdims=True) * (1.0 / 1792.0)
     scale = jnp.broadcast_to(lax.rsqrt(mean + 1e-06), (rows, 128))
+    for k, tiles in enumerate(pieces):
+        for t, tile in enumerate(tiles):
+            gain = gain_ref[k][BODY + 8 * t : BODY + 8 * t + 1, :].astype(F32)
+            out_ref[:, k * 512 + t * 128 : k * 512 + (t + 1) * 128] = (tile * scale * gain).astype(BF16)
+
+
+def norm_a(a0, a1, a2, a3, out):
+    norm((a0, a1, a2, a3), (a0, a1, a2, a3), out, HALF)
+
+
+def norm_b(b0, b1, b2, b3, a0, a1, a2, a3, out):
+    norm((b0, b1, b2, b3), (a0, a1, a2, a3), out, HALF + 16)
+
+
+def project(normed, w_ref):
+    place = gray(lax.axis_index("col"))
     total = None
-    for k, tiles in enumerate(pieces):
-        source = gray((place + 4 - k) & 3)
-        normed = [
-            (tile * scale * gain_ref[k][BODY + 8 * t : BODY + 8 * t + 1, :].astype(F32)).astype(BF16)
-            for t, tile in enumerate(tiles)
-        ]
-        term = dot(jnp.concatenate(normed, axis=1), w_ref[source])
+    for k in range(4):
+        term = dot(normed[:, k * 512 : (k + 1) * 512], w_ref[gray((place + 4 - k) & 3)])
         total = term if total is None else total + term
     total = total.astype(BF16).astype(F32)
     return total[:, 0:512], total[:, 512:640]
@@ -232,9 +230,8 @@
                 ].astype(out.dtype)
 
 
-def chunk_a(a0, a1, a2, a3, w_ref, o_ref, ck_ref, cv_ref, m_ref, first, r1, r2, r3, ka_ref, va_ref):
-    blocks = (a0, a1, a2, a3)
-    kv, queries = project(blocks, blocks, w_ref, HALF)
+def chunk_a(normed, w_ref, o_ref, ck_ref, cv_ref, m_ref, first, r1, r2, r3, ka_ref, va_ref):
+    kv, queries = project(normed, w_ref)
     mask = m_ref[0:HALF, :]
     ka_ref[...] = as_keys(kv)
     va_ref[...] = as_values(kv, jnp.concatenate([mask] * 4, axis=1) > 0.0)
@@ -253,14 +250,13 @@
 
 
 def chunk_b(
-    b0, b1, b2, b3, a0, a1, a2, a3, w_ref, o_ref, ck_ref, cv_ref, m_ref, ka_ref, va_ref, len_ref, cache,
-    first, r1, r2, r3, kb, vb, slab, sems,
+    normed, w_ref, ck_ref, cv_ref, m_ref, ka_ref, va_ref, len_ref, cache,
+    att_ref, kb, vb, slab, sems,
 ):
     copies = [pltpu.make_async_copy(cache.at[d + 1], slab.at[d], sems.at[d]) for d in range(DEC)]
     for copy in copies:
         copy.start()
-    rows = HALF + 16
-    kv, queries = project((b0, b1, b2, b3), (a0, a1, a2, a3), w_ref, rows)
+    kv, queries = project(normed, w_ref)
     mask = m_ref[HALF : 2 * HALF, :]
     kb[...] = as_keys(kv[:HALF])
     vb[...] = as_values(kv[:HALF], jnp.concatenate([mask] * 4, axis=1) > 0.0)
@@ -295,8 +291,12 @@
         below = jnp.sum(weight, axis=1, keepdims=True) + self_weight + 2.0 * (1.0 - live)
         value = jnp.sum(jnp.where(own, live * total / below, 0.0), axis=0, keepdims=True)
         decoded = jnp.where(row((16, 512)) == d, jnp.broadcast_to(value, (16, 512)), decoded)
-    att = jnp.concatenate([jnp.concatenate(outs, axis=1), decoded], axis=0).astype(BF16)
-    emit(att, o_ref, first, (r1, r2, r3), True)
+    att_ref[:HALF, :] = jnp.concatenate(outs, axis=1).astype(BF16)
+    att_ref[HALF:, :] = decoded.astype(BF16)
+
+
+def emit_b(att_ref, o_ref, first, r1, r2, r3):
+    emit(att_ref[...], o_ref, first, (r1, r2, r3), True)
 
 
 def finish(ra, pa, rb, pb, out):
@@ -316,6 +316,14 @@
         out[SPAN_TOKENS:, t * 128 : t * 128 + width] = late.astype(BF16)
 
 
+def in_hbm(x):
+    return pltpu.with_memory_space_constraint(x, pltpu.MemorySpace.HBM)
+
+
+def after(value, *others):
+    return lax.optimization_barrier((value, *others))[0]
+
+
 def shards(hidden, norm_gain, qkv_weight, out_weight, cache, cached, token_mask):
     ring = [(gray(p), gray((p + 1) % 4)) for p in range(4)]
 
@@ -325,72 +333,85 @@
     def across(x, k):
         return lax.ppermute(x, "row", [(i, i ^ k) for i in range(8)])
 
-    a, b = call(
-        pack_tokens,
-        (shaped((BODY + EXTRA, 128)), shaped((BODY + EXTRA, 128))),
-        [VMEM, VMEM],
-        nbytes=2_000_000,
-        name="pack_tokens",
-    )(hidden, norm_gain.reshape(1, -1))
+    a, b, own = call(
+        pack,
+        (shaped((BODY + EXTRA, 128)), shaped((BODY + EXTRA, 128)), shaped((WROWS, 128))),
+        [HBM] * 4,
+        scratch=[pltpu.VMEM(x.shape, BF16) for x in (hidden, norm_gain, qkv_weight, out_weight)]
+        + [pltpu.SemaphoreType.DMA((4,))],
+        nbytes=300_000,
+        name="pack",
+    )(*(in_hbm(x) for x in (hidden, norm_gain, qkv_weight, out_weight)))
     a, b = [a], [b]
-    a.append(onward(a[-1]))
-    b.append(onward(b[-1]))
-    own = call(pack_weights, shaped((5 * QROWS + 2 * OROWS, 128)), [VMEM, VMEM], nbytes=2_000_000, name="pack_weights")(
-        qkv_weight, out_weight
-    )
-    plane = [own, across(own, 2), across(own, 4), across(own, 6)]
-    for _ in range(2):
+    for _ in range(3):
+        b.append(onward(b[-1]))
         a.append(onward(a[-1]))
-        b.append(onward(b[-1]))
-    blocks = []
-    for block in plane:
+    plane = [own] + [across(own, k) for k in (2, 4, 6)]
+    blocks = [own, across(after(own, a[2], b[2]), 1)]
+    for block in plane[1:]:
         blocks += [block, across(block, 1)]
     w, o = call(
         place_weights,
         (shaped((4, 512, 640)), shaped((4, 512, 512))),
         [VMEM] * 8,
-        nbytes=8_000_000,
+        nbytes=300_000,
         name="place_weights",
     )(*blocks)
+    a[3] = after(a[3], w)
+    na = call(norm_a, shaped((HALF, 2048)), [VMEM] * 4, nbytes=30_000_000, name="norm_a")(*a)
+    nb = call(norm_b, shaped((HALF + 16, 2048)), [VMEM] * 8, nbytes=300_000, name="norm_b")(*b, *a)
     ck, cv = call(
         prepare_cache,
         (shaped((1024, 512)), shaped((1024, 512))),
-        [ANY, SMEM],
+        [HBM, SMEM],
         scratch=[pltpu.VMEM((1024, 512), BF16), pltpu.SemaphoreType.DMA],
-        nbytes=3_000_000,
+        nbytes=300_000,
         name="prepare_cache",
-    )(cache, cached)
+        mib=12,
+    )(in_hbm(cache), cached)
     mask = jnp.broadcast_to(token_mask.astype(F32)[:, None], (token_mask.shape[0], 128))
     body = shaped((BODY, 128), F32)
     first, *rest_a, ka, va = call(
         chunk_a,
         (shaped((BODY, 128)), body, body, body, shaped((HALF, 512)), shaped((HALF, 512))),
-        [VMEM] * 9,
-        flops=4_000_000_000,
-        nbytes=12_000_000,
+        [VMEM] * 6,
+        flops=100_000_000,
+        nbytes=300_000,
         name="chunk_a",
-    )(*a, w, o, ck, cv, mask)
+        mib=20,
+    )(na, w, o, ck, cv, mask)
     send_a = onward(first)
-    body = shaped((BODY + EXTRA, 128), F32)
-    first, *rest_b = call(
+    att = call(
         chunk_b,
-        (shaped((BODY + EXTRA, 128)), body, body, body),
-        [VMEM] * 15 + [SMEM, ANY],
+        shaped((HALF + 16, 512)),
+        [VMEM] * 7 + [SMEM, HBM],
         scratch=[
             pltpu.VMEM((HALF, 512), BF16),
             pltpu.VMEM((HALF, 512), BF16),
             pltpu.VMEM((DEC, 1024, 512), BF16),
             pltpu.SemaphoreType.DMA((DEC,)),
         ],
-        flops=5_000_000_000,
-        nbytes=16_000_000,
+        flops=100_000_000,
+        nbytes=300_000,
         name="chunk_b",
-    )(*b, *a, w, o, ck, cv, mask, ka, va, cached, cache)
+        mib=20,
+    )(nb, w, ck, cv, mask, ka, va, cached, in_hbm(cache))
+    arrived = send_a
+    body = shaped((BODY + EXTRA, 128), F32)
+    first, *rest_b = call(
+        emit_b,
+        (shaped((BODY + EXTRA, 128)), body, body, body),
+        [VMEM] * 2,
+        flops=600_000_000,
+        nbytes=4_000_000,
+        name="emit_b",
+    )(after(att, arrived), o)
     send_b = onward(first)
-    for s in range(2):
-        send_a = onward((send_a.astype(F32) + rest_a[s]).astype(BF16))
-        send_b = onward((send_b.astype(F32) + rest_b[s]).astype(BF16))
-    return call(finish, shaped(hidden.shape), [VMEM] * 4, nbytes=3_000_000, name="finish")(
+    send_a = onward((arrived.astype(F32) + rest_a[0]).astype(BF16))
+    send_b = onward((after(send_b, send_a).astype(F32) + rest_b[0]).astype(BF16))
+    send_a = onward((send_a.astype(F32) + rest_a[1]).astype(BF16))
+    send_b = onward((after(send_b, send_a).astype(F32) + rest_b[1]).astype(BF16))
+    return call(finish, shaped(hidden.shape), [VMEM] * 4, nbytes=300_000, name="finish")(
         send_a, rest_a[2], send_b, rest_b[2]
     )
 

time: 100 us -> 86.4 us (0.86)
  local copies, waits for them, and re-layouts: 5.78 us -> 0.78 us
  Pallas kernels: 22.5 us -> 18.1 us
  starting transfers between devices: 18.7 us -> 15.5 us
  waiting for transfers between devices: 52.1 us -> 50.7 us
    ppermute x12, waiting for transfers between devices: 46.6 us -> 39.5 us  [onward(): return lax.ppermute(x, 'col', ring)]
    ppermute x7, waiting for transfers between devices: 5.52 us -> 11.2 us  [across(): return lax.ppermute(x, 'row', [(i, i ^ k) for i in range(8)])]
    unnamed x14 -> x2, local copies, waits for them, and re-layouts: 4.98 us -> 0.65 us
    pallas_call x1, Pallas kernels: 6.24 us -> 3.65 us  [shards(): call(chunk_a, (shaped((BODY, 128)), body, body, body, shaped((HALF, 512))...]
    pallas_call x1, Pallas kernels: 2.92 us -> 1.13 us  [shards(): call(place_weights, (shaped((4, 512, 640)), shaped((4, 512, 512))), [VMEM...]
    ppermute x12, starting transfers between devices: 13.1 us -> 11.5 us  [onward(): return lax.ppermute(x, 'col', ring)]
    ppermute x7, starting transfers between devices: 5.57 us -> 4.02 us  [across(): return lax.ppermute(x, 'row', [(i, i ^ k) for i in range(8)])]
    pallas_call x5 -> x7, Pallas kernels: 13.4 us -> 13.3 us  [the longest x1 6.96 us: shards(): call(chunk_b, shaped((HALF + 16, 512)), [VMEM] * 7 + [SMEM, HBM], scratch...]
  transfers between devices with their start and end apart: 19 -> 19, of which waited for: 9 -> 10; matrix products, arithmetic and copies ran while one was open for 2% -> 1% of each run, Pallas kernels for 11% -> 17%
where the time goes in v2:
time: 86.4 us; the launch traced here: 86.2 us
  waiting for transfers between devices  50.7 us (59%)
  Pallas kernels  18.1 us (21%)
  starting transfers between devices  15.5 us (18%)
  other arithmetic  0.89 us (1%)
    ppermute x12, waiting for transfers between devices, onward(): return lax.ppermute(x, 'col', ring)  39.5 us
    ppermute x12, starting transfers between devices, onward(): return lax.ppermute(x, 'col', ring)  11.5 us
    ppermute x7, waiting for transfers between devices, across(): return lax.ppermute(x, 'row', [(i, i ^ k) for i in range(8)])  11.2 us
    pallas_call x1, Pallas kernels, shards(): call(chunk_b, shaped((HALF + 16, 512)), [VMEM] * 7 + [SMEM, HBM], scratch...  6.96 us
    ppermute x7, starting transfers between devices, across(): return lax.ppermute(x, 'row', [(i, i ^ k) for i in range(8)])  4.02 us
    pallas_call x1, Pallas kernels, shards(): call(chunk_a, (shaped((BODY, 128)), body, body, body, shaped((HALF, 512))...  3.65 us
    pallas_call x1, Pallas kernels, shards(): call(prepare_cache, (shaped((1024, 512)), shaped((1024, 512))), [HBM, SME...  2.21 us
  transfers between devices with their start and end apart: 19, of which 10 were waited for; matrix products, arithmetic and copies ran while one was open for 1% of the time, Pallas kernels for 17%

profile of v2, /device:TPU:0, one launch (start us, length us, event | category | flops | bytes accessed | tf_op | source)
XLA Modules:
  0.0 86.2 jit_solution(16133768092188224027)
XLA Ops:
  0.0 1.5 %pack.1 = (bf16[928,128]{1,0:T(8,128)(2,1)S(1)}, bf16[928,128]{1,0:T(8,128)(2,1)S(1)}, bf16[1792,128]{1,0:T(8,128)(2,1)S(1)}) custom-call(bf16[516,448]{1,0:T(8,128)(2,1)} %hidden.1, bf16[448]{0:T(512)(128)(2,1)} %gains.1, bf16[224,576]{1,0:T(8,128)(2,1)} %qkv.1, bf16[448,224]{1,0:T(8,128)(2,1)} %outs.1), custom_call_target="tpu_custom_call" | custom-call | bytes 300000 | tf_op jit(solution)/shard_map/pack/pallas_call | solution.py:336
  1.5 3.1 %collective-permute-start.3 = (bf16[928,128]{1,0:T(8,128)(2,1)S(1)}, bf16[928,128]{1,0:T(8,128)(2,1)S(1)}, u32[]{:S(2)}, u32[]{:S(2)}) collective-permute-start(bf16[928,128]{1,0:T(8,128)(2,1)S(1)} %get-tuple-element.29.b0), channel_id=1, source_target_pairs={{0,1},{1,3},{3,2},{2,0},{4,5},{5,7},{7,6},{6,4},{8,9},{9,11},{11,1... | collective-permute-start | bytes 712712 | tf_op jit(solution)/shard_map/ppermute | solution.py:331
  4.6 2.6 %collective-permute-start = (bf16[928,128]{1,0:T(8,128)(2,1)S(1)}, bf16[928,128]{1,0:T(8,128)(2,1)S(1)}, u32[]{:S(2)}, u32[]{:S(2)}) collective-permute-start(bf16[928,128]{1,0:T(8,128)(2,1)S(1)} %get-tuple-element.27.a0), channel_id=1, source_target_pairs={{0,1},{1,3},{3,2},{2,0},{4,5},{5,7},{7,6},{6,4},{8,9},{9,11},{11,1... | collective-permute-start | bytes 712712 | tf_op jit(solution)/shard_map/ppermute | solution.py:331
  7.2 2.4 %collective-permute-start.10 = (bf16[1792,128]{1,0:T(8,128)(2,1)S(1)}, bf16[1792,128]{1,0:T(8,128)(2,1)S(1)}, u32[]{:S(2)}, u32[]{:S(2)}) collective-permute-start(bf16[1792,128]{1,0:T(8,128)(2,1)S(1)} %get-tuple-element.30.refs_0_), channel_id=1, source_target_pairs={{0,24},{4,28},{8,16},{12,20},{16,8},{20,12},{24,0},{28,4},{1,25},{... | collective-permute-start | bytes 1376264 | tf_op jit(solution)/shard_map/ppermute | solution.py:334
  10.7 1.5 %collective-permute-done.3.b1 = bf16[928,128]{1,0:T(8,128)(2,1)S(1)} collective-permute-done((bf16[928,128]{1,0:T(8,128)(2,1)S(1)}, bf16[928,128]{1,0:T(8,128)(2,1)S(1)}, u32[]{:S(2)}, u32[]{:S(2)}) %collective-permute-start.3) | collective-permute-done | bytes 237600 | tf_op jit(solution)/shard_map/ppermute | solution.py:331
  12.2 1.2 %collective-permute-start.4 = (bf16[928,128]{1,0:T(8,128)(2,1)S(1)}, bf16[928,128]{1,0:T(8,128)(2,1)S(1)}, u32[]{:S(2)}, u32[]{:S(2)}) collective-permute-start(bf16[928,128]{1,0:T(8,128)(2,1)S(1)} %collective-permute-done.3.b1), channel_id=1, source_target_pairs={{0,1},{1,3},{3,2},{2,0},{4,5},{5,7},{7,6},{6,4},{8,9},{9,11},{11,1... | collective-permute-start | bytes 712712 | tf_op jit(solution)/shard_map/ppermute | solution.py:331
  13.4 3.9 %collective-permute-done.a1 = bf16[928,128]{1,0:T(8,128)(2,1)S(1)} collective-permute-done((bf16[928,128]{1,0:T(8,128)(2,1)S(1)}, bf16[928,128]{1,0:T(8,128)(2,1)S(1)}, u32[]{:S(2)}, u32[]{:S(2)}) %collective-permute-start) | collective-permute-done | bytes 237600 | tf_op jit(solution)/shard_map/ppermute | solution.py:331
  17.3 1.2 %collective-permute-start.1 = (bf16[928,128]{1,0:T(8,128)(2,1)S(1)}, bf16[928,128]{1,0:T(8,128)(2,1)S(1)}, u32[]{:S(2)}, u32[]{:S(2)}) collective-permute-start(bf16[928,128]{1,0:T(8,128)(2,1)S(1)} %collective-permute-done.a1), channel_id=1, source_target_pairs={{0,1},{1,3},{3,2},{2,0},{4,5},{5,7},{7,6},{6,4},{8,9},{9,11},{11,1... | collective-permute-start | bytes 712712 | tf_op jit(solution)/shard_map/ppermute | solution.py:331
  18.5 3.1 %collective-permute-done.10.refs_6_ = bf16[1792,128]{1,0:T(8,128)(2,1)S(1)} collective-permute-done((bf16[1792,128]{1,0:T(8,128)(2,1)S(1)}, bf16[1792,128]{1,0:T(8,128)(2,1)S(1)}, u32[]{:S(2)}, u32[]{:S(2)}) %collective-permute-start.10) | collective-permute-done | bytes 458784 | tf_op jit(solution)/shard_map/ppermute | solution.py:334
  21.6 8.0 %collective-permute-done.8.refs_4_ = bf16[1792,128]{1,0:T(8,128)(2,1)S(1)} collective-permute-done((bf16[1792,128]{1,0:T(8,128)(2,1)S(1)}, bf16[1792,128]{1,0:T(8,128)(2,1)S(1)}, u32[]{:S(2)}, u32[]{:S(2)}) %collective-permute-start.8) | collective-permute-done | bytes 458784 | tf_op jit(solution)/shard_map/ppermute | solution.py:334
  31.0 0.7 convert_element_type.27
  32.4 2.2 %prepare_cache.1 = (bf16[1024,512]{1,0:T(8,128)(2,1)S(1)}, bf16[1024,512]{1,0:T(8,128)(2,1)S(1)}) custom-call(bf16[5,1024,512]{2,1,0:T(8,128)(2,1)} %cache.3, s32[5]{0:T(128)S(1)} %copy-done), custom_call_target="tpu_custom_call" | custom-call | bytes 300000 | tf_op jit(solution)/shard_map/prepare_cache/pallas_call | solution.py:363
  34.6 1.1 %place_weights.1 = (bf16[4,512,640]{2,1,0:T(8,128)(2,1)S(1)}, bf16[4,512,512]{2,1,0:T(8,128)(2,1)S(1)}) custom-call(bf16[1792,128]{1,0:T(8,128)(2,1)S(1)} %get-tuple-element.30.refs_0_, bf16[1792,128]{1,0:T(8,128)(2,1)S(1)} %collective-permute-done.5.refs_1_, bf16[1792,128]{1,0:T(8,128)(2,1)S(1)} %collective-permute-done.6.refs_2_, ...), custom_call_target="tpu_custom_call" | custom-call | bytes 300000 | tf_op jit(solution)/shard_map/place_weights/pallas_call | solution.py:353
  35.8 3.9 %collective-permute-done.2.a3 = bf16[928,128]{1,0:T(8,128)(2,1)S(1)} collective-permute-done((bf16[928,128]{1,0:T(8,128)(2,1)S(1)}, bf16[928,128]{1,0:T(8,128)(2,1)S(1)}, u32[]{:S(2)}, u32[]{:S(2)}) %collective-permute-start.2) | collective-permute-done | bytes 237600 | tf_op jit(solution)/shard_map/ppermute | solution.py:331
  40.3 3.6 %chunk_a.1 = (bf16[896,128]{1,0:T(8,128)(2,1)S(1)}, f32[896,128]{1,0:T(8,128)S(1)}, f32[896,128]{1,0:T(8,128)S(1)}, f32[896,128]{1,0:T(8,128)S(1)}, bf16[256,512...) custom-call(bf16[256,2048]{1,0:T(8,128)(2,1)S(1)} %norm_a.1.normed, bf16[4,512,640]{2,1,0:T(8,128)(2,1)S(1)} %get-tuple-element.31.w_ref, ...), custom_call_target="tpu_custom_call" | custom-call | flops 100000000 | bytes 300000 | tf_op jit(solution)/shard_map/chunk_a/pallas_call | solution.py:374
  44.8 7.0 %chunk_b.1.att_ref = bf16[272,512]{1,0:T(8,128)(2,1)S(1)} custom-call(bf16[272,2048]{1,0:T(8,128)(2,1)S(1)} %norm_b.1.normed, bf16[4,512,640]{2,1,0:T(8,128)(2,1)S(1)} %get-tuple-element.31.w_ref, bf16[1024,512]{1,0:T(8,128)(2,1)S(1)} %get-tuple-element.34.ck_ref, bf16[1024,512]{1,0:T(8,128)(2,1)S(1)} %get-tuple-element.35.cv_ref, ...), custom_call_target="tpu_custom_call" | custom-call | flops 100000000 | bytes 300000 | tf_op jit(solution)/shard_map/chunk_b/pallas_call | solution.py:384
  51.8 0.8 emit_b.1
  52.6 0.7 collective-permute-start.16
  53.4 0.8 collective-permute-start.13
  54.2 11.6 %collective-permute-done.13 = bf16[896,128]{1,0:T(8,128)(2,1)S(1)} collective-permute-done((bf16[896,128]{1,0:T(8,128)(2,1)S(1)}, bf16[896,128]{1,0:T(8,128)(2,1)S(1)}, u32[]{:S(2)}, u32[]{:S(2)}) %collective-permute-start.13) | collective-permute-done | bytes 229408 | tf_op jit(solution)/shard_map/ppermute | solution.py:331
  65.9 0.8 collective-permute-start.14
  66.8 11.3 %collective-permute-done.14.ra = bf16[896,128]{1,0:T(8,128)(2,1)S(1)} collective-permute-done((bf16[896,128]{1,0:T(8,128)(2,1)S(1)}, bf16[896,128]{1,0:T(8,128)(2,1)S(1)}, u32[]{:S(2)}, u32[]{:S(2)}) %collective-permute-start.14) | collective-permute-done | bytes 229408 | tf_op jit(solution)/shard_map/ppermute | solution.py:331
  78.2 7.0 %collective-permute-done.18.rb = bf16[928,128]{1,0:T(8,128)(2,1)S(1)} collective-permute-done((bf16[928,128]{1,0:T(8,128)(2,1)S(1)}, bf16[928,128]{1,0:T(8,128)(2,1)S(1)}, u32[]{:S(2)}, u32[]{:S(2)}) %collective-permute-start.18) | collective-permute-done | bytes 237600 | tf_op jit(solution)/shard_map/ppermute | solution.py:331
  85.2 0.9 %finish.1 = bf16[516,448]{1,0:T(8,128)(2,1)} custom-call(bf16[896,128]{1,0:T(8,128)(2,1)S(1)} %collective-permute-done.14.ra, f32[896,128]{1,0:T(8,128)S(1)} %get-tuple-element.39.pa, bf16[928,128]{1,0:T(8,128)(2,1)S(1)} %collective-permute-done.18.rb, f32[928,128]{1,0:T(8,128)S(1)} %get-tuple-element.48.pb), custom_call_target="tpu_custom_call" | custom-call | bytes 300000 | tf_op jit(solution)/shard_map/finish/pallas_call | solution.py:414
  (31 shorter events, 4.9 us)
Async XLA Ops:
  1.5 10.7 %collective-permute-start.3 = (bf16[928,128]{1,0:T(8,128)(2,1)S(1)}, bf16[928,128]{1,0:T(8,128)(2,1)S(1)}, u32[]{:S(2)}, u32[]{:S(2)}) collective-permute-start(bf16[928,128]{1,0:T(8,128)(2,1)S(1)} %get-tuple-element.29.b0), channel_id=1, source_target_pairs={{0,1},{1,3},{3,2},{2,0},{4,5},{5,7},{7,6},{6,4},{8,9},{9,11},{11,1... | collective-permute-start | bytes 712712 | tf_op jit(solution)/shard_map/ppermute | solution.py:331
  4.6 12.7 %collective-permute-start = (bf16[928,128]{1,0:T(8,128)(2,1)S(1)}, bf16[928,128]{1,0:T(8,128)(2,1)S(1)}, u32[]{:S(2)}, u32[]{:S(2)}) collective-permute-start(bf16[928,128]{1,0:T(8,128)(2,1)S(1)} %get-tuple-element.27.a0), channel_id=1, source_target_pairs={{0,1},{1,3},{3,2},{2,0},{4,5},{5,7},{7,6},{6,4},{8,9},{9,11},{11,1... | collective-permute-start | bytes 712712 | tf_op jit(solution)/shard_map/ppermute | solution.py:331
  7.2 14.4 %collective-permute-start.10 = (bf16[1792,128]{1,0:T(8,128)(2,1)S(1)}, bf16[1792,128]{1,0:T(8,128)(2,1)S(1)}, u32[]{:S(2)}, u32[]{:S(2)}) collective-permute-start(bf16[1792,128]{1,0:T(8,128)(2,1)S(1)} %get-tuple-element.30.refs_0_), channel_id=1, source_target_pairs={{0,24},{4,28},{8,16},{12,20},{16,8},{20,12},{24,0},{28,4},{1,25},{... | collective-permute-start | bytes 1376264 | tf_op jit(solution)/shard_map/ppermute | solution.py:334
  9.6 20.0 %collective-permute-start.8 = (bf16[1792,128]{1,0:T(8,128)(2,1)S(1)}, bf16[1792,128]{1,0:T(8,128)(2,1)S(1)}, u32[]{:S(2)}, u32[]{:S(2)}) collective-permute-start(bf16[1792,128]{1,0:T(8,128)(2,1)S(1)} %get-tuple-element.30.refs_0_), channel_id=1, source_target_pairs={{0,16},{4,20},{8,24},{12,28},{16,0},{20,4},{24,8},{28,12},{1,17},{... | collective-permute-start | bytes 1376264 | tf_op jit(solution)/shard_map/ppermute | solution.py:334
  10.1 19.6 %collective-permute-start.6 = (bf16[1792,128]{1,0:T(8,128)(2,1)S(1)}, bf16[1792,128]{1,0:T(8,128)(2,1)S(1)}, u32[]{:S(2)}, u32[]{:S(2)}) collective-permute-start(bf16[1792,128]{1,0:T(8,128)(2,1)S(1)} %get-tuple-element.30.refs_0_), channel_id=1, source_target_pairs={{0,8},{4,12},{8,0},{12,4},{16,24},{20,28},{24,16},{28,20},{1,9},{5... | collective-permute-start | bytes 1376264 | tf_op jit(solution)/shard_map/ppermute | solution.py:334
  12.2 17.9 %collective-permute-start.4 = (bf16[928,128]{1,0:T(8,128)(2,1)S(1)}, bf16[928,128]{1,0:T(8,128)(2,1)S(1)}, u32[]{:S(2)}, u32[]{:S(2)}) collective-permute-start(bf16[928,128]{1,0:T(8,128)(2,1)S(1)} %collective-permute-done.3.b1), channel_id=1, source_target_pairs={{0,1},{1,3},{3,2},{2,0},{4,5},{5,7},{7,6},{6,4},{8,9},{9,11},{11,1... | collective-permute-start | bytes 712712 | tf_op jit(solution)/shard_map/ppermute | solution.py:331
  17.3 12.8 %collective-permute-start.1 = (bf16[928,128]{1,0:T(8,128)(2,1)S(1)}, bf16[928,128]{1,0:T(8,128)(2,1)S(1)}, u32[]{:S(2)}, u32[]{:S(2)}) collective-permute-start(bf16[928,128]{1,0:T(8,128)(2,1)S(1)} %collective-permute-done.a1), channel_id=1, source_target_pairs={{0,1},{1,3},{3,2},{2,0},{4,5},{5,7},{7,6},{6,4},{8,9},{9,11},{11,1... | collective-permute-start | bytes 712712 | tf_op jit(solution)/shard_map/ppermute | solution.py:331
  21.6 9.1 %collective-permute-start.11 = (bf16[1792,128]{1,0:T(8,128)(2,1)S(1)}, bf16[1792,128]{1,0:T(8,128)(2,1)S(1)}, u32[]{:S(2)}, u32[]{:S(2)}) collective-permute-start(bf16[1792,128]{1,0:T(8,128)(2,1)S(1)} %collective-permute-done.10.refs_6_), channel_id=1, source_target_pairs={{0,4},{4,0},{8,12},{12,8},{16,20},{20,16},{24,28},{28,24},{1,5},{5... | collective-permute-start | bytes 1376264 | tf_op jit(solution)/shard_map/ppermute | solution.py:334
  29.6 5.0 %collective-permute-start.9 = (bf16[1792,128]{1,0:T(8,128)(2,1)S(1)}, bf16[1792,128]{1,0:T(8,128)(2,1)S(1)}, u32[]{:S(2)}, u32[]{:S(2)}) collective-permute-start(bf16[1792,128]{1,0:T(8,128)(2,1)S(1)} %collective-permute-done.8.refs_4_), channel_id=1, source_target_pairs={{0,4},{4,0},{8,12},{12,8},{16,20},{20,16},{24,28},{28,24},{1,5},{5... | collective-permute-start | bytes 1376264 | tf_op jit(solution)/shard_map/ppermute | solution.py:334
  29.7 4.9 %collective-permute-start.7 = (bf16[1792,128]{1,0:T(8,128)(2,1)S(1)}, bf16[1792,128]{1,0:T(8,128)(2,1)S(1)}, u32[]{:S(2)}, u32[]{:S(2)}) collective-permute-start(bf16[1792,128]{1,0:T(8,128)(2,1)S(1)} %collective-permute-done.6.refs_2_), channel_id=1, source_target_pairs={{0,4},{4,0},{8,12},{12,8},{16,20},{20,16},{24,28},{28,24},{1,5},{5... | collective-permute-start | bytes 1376264 | tf_op jit(solution)/shard_map/ppermute | solution.py:334
  30.1 4.5 %collective-permute-start.5 = (bf16[1792,128]{1,0:T(8,128)(2,1)S(1)}, bf16[1792,128]{1,0:T(8,128)(2,1)S(1)}, u32[]{:S(2)}, u32[]{:S(2)}) collective-permute-start(bf16[1792,128]{1,0:T(8,128)(2,1)S(1)} %get-tuple-element.30.refs_0_), channel_id=1, source_target_pairs={{0,4},{4,0},{8,12},{12,8},{16,20},{20,16},{24,28},{28,24},{1,5},{5... | collective-permute-start | bytes 1376264 | tf_op jit(solution)/shard_map/ppermute | solution.py:334
  30.2 9.5 %collective-permute-start.2 = (bf16[928,128]{1,0:T(8,128)(2,1)S(1)}, bf16[928,128]{1,0:T(8,128)(2,1)S(1)}, u32[]{:S(2)}, u32[]{:S(2)}) collective-permute-start(bf16[928,128]{1,0:T(8,128)(2,1)S(1)} %collective-permute-done.1.a2), channel_id=1, source_target_pairs={{0,1},{1,3},{3,2},{2,0},{4,5},{5,7},{7,6},{6,4},{8,9},{9,11},{11,1... | collective-permute-start | bytes 712712 | tf_op jit(solution)/shard_map/ppermute | solution.py:331
  30.7 13.7 %collective-permute-start.15 = (bf16[928,128]{1,0:T(8,128)(2,1)S(1)}, bf16[928,128]{1,0:T(8,128)(2,1)S(1)}, u32[]{:S(2)}, u32[]{:S(2)}) collective-permute-start(bf16[928,128]{1,0:T(8,128)(2,1)S(1)} %collective-permute-done.4.b2), channel_id=1, source_target_pairs={{0,1},{1,3},{3,2},{2,0},{4,5},{5,7},{7,6},{6,4},{8,9},{9,11},{11,1... | collective-permute-start | bytes 712712 | tf_op jit(solution)/shard_map/ppermute | solution.py:331
  31.7 0.7 copy-start
  44.0 7.8 %collective-permute-start.12 = (bf16[896,128]{1,0:T(8,128)(2,1)S(1)}, bf16[896,128]{1,0:T(8,128)(2,1)S(1)}, u32[]{:S(2)}, u32[]{:S(2)}) collective-permute-start(bf16[896,128]{1,0:T(8,128)(2,1)S(1)} %get-tuple-element.36), channel_id=1, source_target_pairs={{0,1},{1,3},{3,2},{2,0},{4,5},{5,7},{7,6},{6,4},{8,9},{9,11},{11,1... | collective-permute-start | bytes 688136 | tf_op jit(solution)/shard_map/ppermute | solution.py:331
  52.6 13.2 %collective-permute-start.16 = (bf16[928,128]{1,0:T(8,128)(2,1)S(1)}, bf16[928,128]{1,0:T(8,128)(2,1)S(1)}, u32[]{:S(2)}, u32[]{:S(2)}) collective-permute-start(bf16[928,128]{1,0:T(8,128)(2,1)S(1)} %get-tuple-element.43), channel_id=1, source_target_pairs={{0,1},{1,3},{3,2},{2,0},{4,5},{5,7},{7,6},{6,4},{8,9},{9,11},{11,1... | collective-permute-start | bytes 712712 | tf_op jit(solution)/shard_map/ppermute | solution.py:331
  53.4 12.4 %collective-permute-start.13 = (bf16[896,128]{1,0:T(8,128)(2,1)S(1)}, bf16[896,128]{1,0:T(8,128)(2,1)S(1)}, u32[]{:S(2)}, u32[]{:S(2)}) collective-permute-start(bf16[896,128]{1,0:T(8,128)(2,1)S(1)} %add_convert_fusion.3), channel_id=1, source_target_pairs={{0,1},{1,3},{3,2},{2,0},{4,5},{5,7},{7,6},{6,4},{8,9},{9,11},{11,1... | collective-permute-start | bytes 688136 | tf_op jit(solution)/shard_map/ppermute | solution.py:331
  65.8 12.3 %collective-permute-start.17 = (bf16[928,128]{1,0:T(8,128)(2,1)S(1)}, bf16[928,128]{1,0:T(8,128)(2,1)S(1)}, u32[]{:S(2)}, u32[]{:S(2)}) collective-permute-start(bf16[928,128]{1,0:T(8,128)(2,1)S(1)} %add_convert_fusion.1), channel_id=1, source_target_pairs={{0,1},{1,3},{3,2},{2,0},{4,5},{5,7},{7,6},{6,4},{8,9},{9,11},{11,1... | collective-permute-start | bytes 712712 | tf_op jit(solution)/shard_map/ppermute | solution.py:331
  65.9 12.2 %collective-permute-start.14 = (bf16[896,128]{1,0:T(8,128)(2,1)S(1)}, bf16[896,128]{1,0:T(8,128)(2,1)S(1)}, u32[]{:S(2)}, u32[]{:S(2)}) collective-permute-start(bf16[896,128]{1,0:T(8,128)(2,1)S(1)} %add_convert_fusion.2), channel_id=1, source_target_pairs={{0,1},{1,3},{3,2},{2,0},{4,5},{5,7},{7,6},{6,4},{8,9},{9,11},{11,1... | collective-permute-start | bytes 688136 | tf_op jit(solution)/shard_map/ppermute | solution.py:331
  78.2 7.1 %collective-permute-start.18 = (bf16[928,128]{1,0:T(8,128)(2,1)S(1)}, bf16[928,128]{1,0:T(8,128)(2,1)S(1)}, u32[]{:S(2)}, u32[]{:S(2)}) collective-permute-start(bf16[928,128]{1,0:T(8,128)(2,1)S(1)} %add_convert_fusion), channel_id=1, source_target_pairs={{0,1},{1,3},{3,2},{2,0},{4,5},{5,7},{7,6},{6,4},{8,9},{9,11},{11,1... | collective-permute-start | bytes 712712 | tf_op jit(solution)/shard_map/ppermute | solution.py:331

commit v3 on v2

--- a/solution.py
+++ b/solution.py
@@ -22,6 +22,12 @@
 QROWS = 224
 OROWS = 448
 WROWS = 4 * QROWS + 2 * OROWS
+COST_X = 5_000_000_000
+COST_SQ = 1_000_000_000
+COST_CA = 100_000_000
+COST_CB = 1_000_000_000
+COST_F = 2_000_000_000
+COST_D = 1_000_000
 
 
 def gray(place):
@@ -147,29 +153,36 @@
     v_ref[...] = as_values(kv, row(kv.shape) < len_ref[0])
 
 
-def norm(blocks, gain_ref, out_ref, rows):
+def tiles_of(ref, rows):
     middle = lane((HALF // 2, 128)) < 64
-    pieces, square = [], None
-    for ref in blocks:
-        tail = ref[TAIL:BODY, :].astype(F32)
-        tail = jnp.concatenate([jnp.where(middle, tail, 0.0), jnp.where(middle, 0.0, tail)], axis=0)
-        tiles = [ref[t * HALF : (t + 1) * HALF, :].astype(F32) for t in range(3)] + [tail]
-        if rows > HALF:
-            tiles = [
-                jnp.concatenate(
-                    [
-                        tile,
-                        ref[BODY + 8 * t : BODY + 8 * t + 8, :].astype(F32),
-                        jnp.zeros((8, 128), F32),
-                    ],
-                    axis=0,
-                )
-                for t, tile in enumerate(tiles)
-            ]
-        pieces.append(tiles)
-        for tile in tiles:
-            square = tile * tile if square is None else square + tile * tile
-    mean = jnp.sum(square, axis=1, keepdims=True) * (1.0 / 1792.0)
+    tail = ref[TAIL:BODY, :].astype(F32)
+    tail = jnp.concatenate([jnp.where(middle, tail, 0.0), jnp.where(middle, 0.0, tail)], axis=0)
+    tiles = [ref[t * HALF : (t + 1) * HALF, :].astype(F32) for t in range(3)] + [tail]
+    if rows > HALF:
+        late = [ref[BODY + 8 * t : BODY + 8 * t + 8, :].astype(F32) for t in range(4)]
+        zeros = jnp.zeros((8, 128), F32)
+        tiles = [jnp.concatenate(parts + (zeros,), axis=0) for parts in zip(tiles, late)]
+    return tiles
+
+
+def squares(tiles):
+    total = tiles[0] * tiles[0]
+    for tile in tiles[1:]:
+        total = total + tile * tile
+    return total
+
+
+def square_b(ref, out):
+    out[...] = squares(tiles_of(ref, HALF + 16))
+
+
+def norm(blocks, gain_ref, sums, out_ref, rows):
+    pieces = [tiles_of(ref, rows) for ref in blocks]
+    total = None
+    for k, tiles in enumerate(pieces):
+        part = sums[k][...] if k in sums else squares(tiles)
+        total = part if total is None else total + part
+    mean = jnp.sum(total, axis=1, keepdims=True) * (1.0 / 1792.0)
     scale = jnp.broadcast_to(lax.rsqrt(mean + 1e-06), (rows, 128))
     for k, tiles in enumerate(pieces):
         for t, tile in enumerate(tiles):
@@ -178,11 +191,11 @@
 
 
 def norm_a(a0, a1, a2, a3, out):
-    norm((a0, a1, a2, a3), (a0, a1, a2, a3), out, HALF)
-
-
-def norm_b(b0, b1, b2, b3, a0, a1, a2, a3, out):
-    norm((b0, b1, b2, b3), (a0, a1, a2, a3), out, HALF + 16)
+    norm((a0, a1, a2, a3), (a0, a1, a2, a3), {}, out, HALF)
+
+
+def norm_b(b0, b1, b2, b3, s1, s2, a0, a1, a2, a3, out):
+    norm((b0, b1, b2, b3), (a0, a1, a2, a3), {1: s1, 2: s2}, out, HALF + 16)
 
 
 def project(normed, w_ref):
@@ -213,7 +226,7 @@
     return mask * total / below
 
 
-def emit(att, o_ref, first_ref, rest, tail_rows):
+def emit(att, o_ref, first_ref, rest):
     place = gray(lax.axis_index("col"))
     for s in range(4):
         part = dot(att, o_ref[gray((place + 3 - s) & 3)])
@@ -223,11 +236,6 @@
         last = part[:, 384:512]
         middle = lane((HALF // 2, 128)) < 64
         out[TAIL:BODY, :] = jnp.where(middle, last[: HALF // 2], last[HALF // 2 : HALF]).astype(out.dtype)
-        if tail_rows:
-            for t in range(4):
-                out[BODY + 8 * t : BODY + 8 * t + 8, :] = part[
-                    HALF : HALF + 8, t * 128 : (t + 1) * 128
-                ].astype(out.dtype)
 
 
 def chunk_a(normed, w_ref, o_ref, ck_ref, cv_ref, m_ref, first, r1, r2, r3, ka_ref, va_ref):
@@ -246,35 +254,40 @@
             keys = slice(b * 512, (b + 1) * 512)
             total += dot(weigh(dot_nt(q, ck_ref[keys, at])), cv_ref[keys, at])
         outs.append(divide(total, mask).astype(BF16))
-    emit(jnp.concatenate(outs, axis=1), o_ref, first, (r1, r2, r3), False)
+    emit(jnp.concatenate(outs, axis=1), o_ref, first, (r1, r2, r3))
 
 
 def chunk_b(
-    normed, w_ref, ck_ref, cv_ref, m_ref, ka_ref, va_ref, len_ref, cache,
-    att_ref, kb, vb, slab, sems,
+    normed, w_ref, o_ref, ck_ref, cv_ref, m_ref, ka_ref, va_ref, first, r1, r2, r3, late_ref, kb, vb
 ):
-    copies = [pltpu.make_async_copy(cache.at[d + 1], slab.at[d], sems.at[d]) for d in range(DEC)]
-    for copy in copies:
-        copy.start()
     kv, queries = project(normed, w_ref)
+    late_ref[:, 0:512] = kv[HALF:]
+    late_ref[:, 512:640] = queries[HALF:]
+    kv, queries = kv[:HALF], queries[:HALF]
     mask = m_ref[HALF : 2 * HALF, :]
-    kb[...] = as_keys(kv[:HALF])
-    vb[...] = as_values(kv[:HALF], jnp.concatenate([mask] * 4, axis=1) > 0.0)
+    kb[...] = as_keys(kv)
+    vb[...] = as_values(kv, jnp.concatenate([mask] * 4, axis=1) > 0.0)
     causal = lane((HALF, HALF)) <= row((HALF, HALF))
-    outs, late = [], []
+    outs = []
     for h in range(4):
         at = slice(h * LANES, (h + 1) * LANES)
         q, one = query_of(queries, h)
-        late.append(q[HALF:])
-        q = jnp.where(one, 1.0, q)[:HALF].astype(BF16)
+        q = jnp.where(one, 1.0, q).astype(BF16)
         total = dot(weigh(dot_nt(q, kb[:, at]), causal), vb[:, at])
         total += dot(weigh(dot_nt(q, ka_ref[:, at])), va_ref[:, at])
         for b in range(2):
             keys = slice(b * 512, (b + 1) * 512)
             total += dot(weigh(dot_nt(q, ck_ref[keys, at])), cv_ref[keys, at])
-        outs.append(divide(total, mask))
-    late = jnp.concatenate(late, axis=1)
-    fresh = kv[HALF:]
+        outs.append(divide(total, mask).astype(BF16))
+    emit(jnp.concatenate(outs, axis=1), o_ref, first, (r1, r2, r3))
+
+
+def decode(late_ref, o_ref, m_ref, len_ref, cache, own_ref, s1, s2, s3, slab, sems):
+    copies = [pltpu.make_async_copy(cache.at[d + 1], slab.at[d], sems.at[d]) for d in range(DEC)]
+    for copy in copies:
+        copy.start()
+    fresh = late_ref[:, 0:512]
+    late = jnp.concatenate([query_of(late_ref[:, 512:640], h)[0] for h in range(4)], axis=1)
     own = row((16, 512)) == lane((16, 512)) // LANES
     position = lane((16, 1024))
     decoded = jnp.zeros((16, 512), F32)
@@ -291,29 +304,29 @@
         below = jnp.sum(weight, axis=1, keepdims=True) + self_weight + 2.0 * (1.0 - live)
         value = jnp.sum(jnp.where(own, live * total / below, 0.0), axis=0, keepdims=True)
         decoded = jnp.where(row((16, 512)) == d, jnp.broadcast_to(value, (16, 512)), decoded)
-    att_ref[:HALF, :] = jnp.concatenate(outs, axis=1).astype(BF16)
-    att_ref[HALF:, :] = decoded.astype(BF16)
-
-
-def emit_b(att_ref, o_ref, first, r1, r2, r3):
-    emit(att_ref[...], o_ref, first, (r1, r2, r3), True)
-
-
-def finish(ra, pa, rb, pb, out):
-    for recv, part, base in ((ra, pa, 0), (rb, pb, HALF)):
-        for t in range(3):
-            at = slice(t * HALF, (t + 1) * HALF)
-            out[base : base + HALF, t * 128 : (t + 1) * 128] = (
-                recv[at, :].astype(F32) + part[at, :]
-            ).astype(BF16)
-        tail = recv[TAIL:BODY, :].astype(F32) + part[TAIL:BODY, :]
-        out[base : base + HALF // 2, 384:448] = tail[:, 0:64].astype(BF16)
-        out[base + HALF // 2 : base + HALF, 384:448] = tail[:, 64:128].astype(BF16)
-    for t in range(4):
-        at = slice(BODY + 8 * t, BODY + 8 * t + DEC)
-        width = 128 if t < 3 else 64
-        late = (rb[at, :].astype(F32) + pb[at, :])[:, 0:width]
-        out[SPAN_TOKENS:, t * 128 : t * 128 + width] = late.astype(BF16)
+    me = lax.axis_index("col")
+    for k, out in enumerate((own_ref, s1, s2, s3)):
+        out[...] = dot(decoded.astype(BF16), o_ref[(me + k) & 3])[0:8]
+
+
+def unpack_sum(recv, part, out, base):
+    for t in range(3):
+        at = slice(t * HALF, (t + 1) * HALF)
+        out[base : base + HALF, t * 128 : (t + 1) * 128] = (recv[at, :].astype(F32) + part[at, :]).astype(BF16)
+    tail = recv[TAIL:BODY, :].astype(F32) + part[TAIL:BODY, :]
+    out[base : base + HALF // 2, 384:448] = tail[:, 0:64].astype(BF16)
+    out[base + HALF // 2 : base + HALF, 384:448] = tail[:, 64:128].astype(BF16)
+
+
+def finish_a(recv, part, p0, p1, p2, p3, out, late):
+    unpack_sum(recv, part, out, 0)
+    late[...] = ((p0[...] + p1[...]) + (p2[...] + p3[...])).astype(BF16)
+
+
+def finish_b(done, late, recv, part, out):
+    out[:HALF, :] = done[...]
+    unpack_sum(recv, part, out, HALF)
+    out[SPAN_TOKENS:, :] = late[0:DEC, 0:448]
 
 
 def in_hbm(x):
@@ -342,12 +355,17 @@
         nbytes=300_000,
         name="pack",
     )(*(in_hbm(x) for x in (hidden, norm_gain, qkv_weight, out_weight)))
-    a, b = [a], [b]
-    for _ in range(3):
-        b.append(onward(b[-1]))
-        a.append(onward(a[-1]))
     plane = [own] + [across(own, k) for k in (2, 4, 6)]
-    blocks = [own, across(after(own, a[2], b[2]), 1)]
+
+    def sums(x, name):
+        return call(square_b, shaped((HALF + 16, 128), F32), [VMEM], flops=COST_SQ, nbytes=300_000, name=name)(x)
+
+    a1, b1 = onward(a), onward(b)
+    a2, b2 = onward(a1), onward(b1)
+    s1, s2 = sums(b1, "square_b1"), sums(b2, "square_b2")
+    a3 = after(onward(after(a2, s1)), s2, *plane[1:])
+    a, b = [a, a1, a2, a3], [b, b1, b2, onward(b2)]
+    blocks = [own, across(after(own, s2), 1)]
     for block in plane[1:]:
         blocks += [block, across(block, 1)]
     w, o = call(
@@ -357,9 +375,10 @@
         nbytes=300_000,
         name="place_weights",
     )(*blocks)
-    a[3] = after(a[3], w)
-    na = call(norm_a, shaped((HALF, 2048)), [VMEM] * 4, nbytes=30_000_000, name="norm_a")(*a)
-    nb = call(norm_b, shaped((HALF + 16, 2048)), [VMEM] * 8, nbytes=300_000, name="norm_b")(*b, *a)
+    na = call(norm_a, shaped((HALF, 2048)), [VMEM] * 4, flops=COST_X, nbytes=300_000, name="norm_a")(*a)
+    nb = call(norm_b, shaped((HALF + 16, 2048)), [VMEM] * 10, nbytes=300_000, name="norm_b")(
+        *b, s1, s2, *a
+    )
     ck, cv = call(
         prepare_cache,
         (shaped((1024, 512)), shaped((1024, 512))),
@@ -375,44 +394,51 @@
         chunk_a,
         (shaped((BODY, 128)), body, body, body, shaped((HALF, 512)), shaped((HALF, 512))),
         [VMEM] * 6,
-        flops=100_000_000,
+        flops=COST_CA,
         nbytes=300_000,
         name="chunk_a",
         mib=20,
     )(na, w, o, ck, cv, mask)
     send_a = onward(first)
-    att = call(
+    first, *rest_b, late = call(
         chunk_b,
-        shaped((HALF + 16, 512)),
-        [VMEM] * 7 + [SMEM, HBM],
-        scratch=[
-            pltpu.VMEM((HALF, 512), BF16),
-            pltpu.VMEM((HALF, 512), BF16),
-            pltpu.VMEM((DEC, 1024, 512), BF16),
-            pltpu.SemaphoreType.DMA((DEC,)),
-        ],
-        flops=100_000_000,
+        (shaped((BODY, 128)), body, body, body, shaped((16, 640), F32)),
+        [VMEM] * 8,
+        scratch=[pltpu.VMEM((HALF, 512), BF16), pltpu.VMEM((HALF, 512), BF16)],
+        flops=COST_CB,
         nbytes=300_000,
         name="chunk_b",
         mib=20,
-    )(nb, w, ck, cv, mask, ka, va, cached, in_hbm(cache))
-    arrived = send_a
-    body = shaped((BODY + EXTRA, 128), F32)
-    first, *rest_b = call(
-        emit_b,
-        (shaped((BODY + EXTRA, 128)), body, body, body),
-        [VMEM] * 2,
-        flops=600_000_000,
-        nbytes=4_000_000,
-        name="emit_b",
-    )(after(att, arrived), o)
+    )(nb, w, o, ck, cv, mask, ka, va)
     send_b = onward(first)
-    send_a = onward((arrived.astype(F32) + rest_a[0]).astype(BF16))
-    send_b = onward((after(send_b, send_a).astype(F32) + rest_b[0]).astype(BF16))
+    few = shaped((8, 512), F32)
+    parts = call(
+        decode,
+        (few, few, few, few),
+        [VMEM] * 3 + [SMEM, HBM],
+        scratch=[pltpu.VMEM((DEC, 1024, 512), BF16), pltpu.SemaphoreType.DMA((DEC,))],
+        flops=COST_D,
+        nbytes=300_000,
+        name="decode",
+        mib=12,
+    )(late, o, mask, cached, in_hbm(cache))
+    send_a = onward((send_a.astype(F32) + rest_a[0]).astype(BF16))
+    send_b = onward((after(send_b, parts[0]).astype(F32) + rest_b[0]).astype(BF16))
     send_a = onward((send_a.astype(F32) + rest_a[1]).astype(BF16))
-    send_b = onward((after(send_b, send_a).astype(F32) + rest_b[1]).astype(BF16))
-    return call(finish, shaped(hidden.shape), [VMEM] * 4, nbytes=300_000, name="finish")(
-        send_a, rest_a[2], send_b, rest_b[2]
+    send_b = onward((send_b.astype(F32) + rest_b[1]).astype(BF16))
+    parts = parts[:1] + tuple(
+        lax.ppermute(parts[k], "col", [(i, (i + k) % 4) for i in range(4)]) for k in (1, 2, 3)
+    )
+    done, late = call(
+        finish_a,
+        (shaped((HALF, hidden.shape[1])), shaped((8, 512))),
+        [VMEM] * 6,
+        flops=COST_F,
+        nbytes=300_000,
+        name="finish_a",
+    )(send_a, rest_a[2], *parts)
+    return call(finish_b, shaped(hidden.shape), [VMEM] * 4, nbytes=300_000, name="finish_b")(
+        done, late, send_b, rest_b[2]
     )
 
 

time: 86.4 us -> 76.1 us (0.88)
  waiting for transfers between devices: 50.7 us -> 29.1 us
  starting transfers between devices: 15.5 us -> 26.7 us
  Pallas kernels: 18.1 us -> 19.7 us
    ppermute x12, waiting for transfers between devices: 39.5 us -> 22.1 us  [onward(): return lax.ppermute(x, 'col', ring)]
    ppermute x7, waiting for transfers between devices: 11.2 us -> 3.84 us  [across(): return lax.ppermute(x, 'row', [(i, i ^ k) for i in range(8)])]
    ppermute x12, starting transfers between devices: 11.5 us -> 17.6 us  [onward(): return lax.ppermute(x, 'col', ring)]
    ppermute x0 -> x3, starting transfers between devices: none -> 4.89 us  [shards(): lax.ppermute(parts[k], 'col', [(i, (i + k) % 4) for i in range(4)])]
    ppermute x0 -> x3, waiting for transfers between devices: none -> 3.14 us  [shards(): lax.ppermute(parts[k], 'col', [(i, (i + k) % 4) for i in range(4)])]
    pallas_call x5 -> x8, Pallas kernels: 9.6 us -> 11.1 us  [the longest x1 4.68 us: shards(): call(chunk_b, (shaped((BODY, 128)), body, body, body, shaped((16, 640), F...]
  transfers between devices with their start and end apart: 19 -> 22, of which waited for: 10 -> 10; matrix products, arithmetic and copies ran while one was open for 1% -> 0% of each run, Pallas kernels for 17% -> 23%
where the time goes in v3:
time: 76.1 us; the launch traced here: 75.9 us
  waiting for transfers between devices  29.1 us (38%)
  starting transfers between devices  26.7 us (35%)
  Pallas kernels  19.7 us (26%)
    ppermute x12, waiting for transfers between devices, onward(): return lax.ppermute(x, 'col', ring)  22.1 us
    ppermute x12, starting transfers between devices, onward(): return lax.ppermute(x, 'col', ring)  17.6 us
    ppermute x3, starting transfers between devices, shards(): lax.ppermute(parts[k], 'col', [(i, (i + k) % 4) for i in range(4)])  4.89 us
    pallas_call x1, Pallas kernels, shards(): call(chunk_b, (shaped((BODY, 128)), body, body, body, shaped((16, 640), F...  4.68 us
    pallas_call x1, Pallas kernels, shards(): call(decode, (few, few, few, few), [VMEM] * 3 + [SMEM, HBM], scratch=[plt...  4.43 us
    ppermute x7, starting transfers between devices, across(): return lax.ppermute(x, 'row', [(i, i ^ k) for i in range(8)])  4.15 us
    ppermute x7, waiting for transfers between devices, across(): return lax.ppermute(x, 'row', [(i, i ^ k) for i in range(8)])  3.84 us
    pallas_call x1, Pallas kernels, shards(): call(chunk_a, (shaped((BODY, 128)), body, body, body, shaped((HALF, 512))...  3.64 us
  transfers between devices with their start and end apart: 22, of which 10 were waited for; matrix products, arithmetic and copies ran while one was open for 0% of the time, Pallas kernels for 23%

profile of v3, /device:TPU:0, one launch (start us, length us, event | category | flops | bytes accessed | tf_op | source)
XLA Modules:
  0.0 75.9 jit_solution(816772723691339378)
XLA Ops:
  0.0 1.5 %pack.1 = (bf16[928,128]{1,0:T(8,128)(2,1)S(1)}, bf16[928,128]{1,0:T(8,128)(2,1)S(1)}, bf16[1792,128]{1,0:T(8,128)(2,1)S(1)}) custom-call(bf16[516,448]{1,0:T(8,128)(2,1)} %hidden.1, bf16[448]{0:T(512)(128)(2,1)} %gains.1, bf16[224,576]{1,0:T(8,128)(2,1)} %qkv.1, bf16[448,224]{1,0:T(8,128)(2,1)} %outs.1), custom_call_target="tpu_custom_call" | custom-call | bytes 300000 | tf_op jit(solution)/shard_map/pack/pallas_call | solution.py:349
  1.5 3.1 %collective-permute-start = (bf16[928,128]{1,0:T(8,128)(2,1)S(1)}, bf16[928,128]{1,0:T(8,128)(2,1)S(1)}, u32[]{:S(2)}, u32[]{:S(2)}) collective-permute-start(bf16[928,128]{1,0:T(8,128)(2,1)S(1)} %get-tuple-element.33.a0), channel_id=1, source_target_pairs={{0,1},{1,3},{3,2},{2,0},{4,5},{5,7},{7,6},{6,4},{8,9},{9,11},{11,1... | collective-permute-start | bytes 712712 | tf_op jit(solution)/shard_map/ppermute | solution.py:344
  4.6 2.6 %collective-permute-start.2 = (bf16[928,128]{1,0:T(8,128)(2,1)S(1)}, bf16[928,128]{1,0:T(8,128)(2,1)S(1)}, u32[]{:S(2)}, u32[]{:S(2)}) collective-permute-start(bf16[928,128]{1,0:T(8,128)(2,1)S(1)} %get-tuple-element.34.b0), channel_id=1, source_target_pairs={{0,1},{1,3},{3,2},{2,0},{4,5},{5,7},{7,6},{6,4},{8,9},{9,11},{11,1... | collective-permute-start | bytes 712712 | tf_op jit(solution)/shard_map/ppermute | solution.py:344
  7.2 2.4 %collective-permute-start.7 = (bf16[1792,128]{1,0:T(8,128)(2,1)S(1)}, bf16[1792,128]{1,0:T(8,128)(2,1)S(1)}, u32[]{:S(2)}, u32[]{:S(2)}) collective-permute-start(bf16[1792,128]{1,0:T(8,128)(2,1)S(1)} %get-tuple-element.38.refs_0_), channel_id=1, source_target_pairs={{0,24},{4,28},{8,16},{12,20},{16,8},{20,12},{24,0},{28,4},{1,25},{... | collective-permute-start | bytes 1376264 | tf_op jit(solution)/shard_map/ppermute | solution.py:347
  10.7 1.5 %collective-permute-done.a1 = bf16[928,128]{1,0:T(8,128)(2,1)S(1)} collective-permute-done((bf16[928,128]{1,0:T(8,128)(2,1)S(1)}, bf16[928,128]{1,0:T(8,128)(2,1)S(1)}, u32[]{:S(2)}, u32[]{:S(2)}) %collective-permute-start) | collective-permute-done | bytes 237600 | tf_op jit(solution)/shard_map/ppermute | solution.py:344
  12.2 1.2 %collective-permute-start.1 = (bf16[928,128]{1,0:T(8,128)(2,1)S(1)}, bf16[928,128]{1,0:T(8,128)(2,1)S(1)}, u32[]{:S(2)}, u32[]{:S(2)}) collective-permute-start(bf16[928,128]{1,0:T(8,128)(2,1)S(1)} %collective-permute-done.a1), channel_id=1, source_target_pairs={{0,1},{1,3},{3,2},{2,0},{4,5},{5,7},{7,6},{6,4},{8,9},{9,11},{11,1... | collective-permute-start | bytes 712712 | tf_op jit(solution)/shard_map/ppermute | solution.py:344
  13.4 3.9 %collective-permute-done.2.ref.b1 = bf16[928,128]{1,0:T(8,128)(2,1)S(1)} collective-permute-done((bf16[928,128]{1,0:T(8,128)(2,1)S(1)}, bf16[928,128]{1,0:T(8,128)(2,1)S(1)}, u32[]{:S(2)}, u32[]{:S(2)}) %collective-permute-start.2) | collective-permute-done | bytes 237600 | tf_op jit(solution)/shard_map/ppermute | solution.py:344
  17.3 1.2 %collective-permute-start.4 = (bf16[928,128]{1,0:T(8,128)(2,1)S(1)}, bf16[928,128]{1,0:T(8,128)(2,1)S(1)}, u32[]{:S(2)}, u32[]{:S(2)}) collective-permute-start(bf16[928,128]{1,0:T(8,128)(2,1)S(1)} %collective-permute-done.2.ref.b1), channel_id=1, source_target_pairs={{0,1},{1,3},{3,2},{2,0},{4,5},{5,7},{7,6},{6,4},{8,9},{9,11},{11,1... | collective-permute-start | bytes 712712 | tf_op jit(solution)/shard_map/ppermute | solution.py:344
  18.5 3.9 %collective-permute-done.1.a2 = bf16[928,128]{1,0:T(8,128)(2,1)S(1)} collective-permute-done((bf16[928,128]{1,0:T(8,128)(2,1)S(1)}, bf16[928,128]{1,0:T(8,128)(2,1)S(1)}, u32[]{:S(2)}, u32[]{:S(2)}) %collective-permute-start.1) | collective-permute-done | bytes 237600 | tf_op jit(solution)/shard_map/ppermute | solution.py:344
  22.4 1.2 %collective-permute-start.3 = (bf16[928,128]{1,0:T(8,128)(2,1)S(1)}, bf16[928,128]{1,0:T(8,128)(2,1)S(1)}, u32[]{:S(2)}, u32[]{:S(2)}) collective-permute-start(bf16[928,128]{1,0:T(8,128)(2,1)S(1)} %collective-permute-done.1.a2), channel_id=1, source_target_pairs={{0,1},{1,3},{3,2},{2,0},{4,5},{5,7},{7,6},{6,4},{8,9},{9,11},{11,1... | collective-permute-start | bytes 712712 | tf_op jit(solution)/shard_map/ppermute | solution.py:344
  23.6 2.2 %prepare_cache.1 = (bf16[1024,512]{1,0:T(8,128)(2,1)S(1)}, bf16[1024,512]{1,0:T(8,128)(2,1)S(1)}) custom-call(bf16[5,1024,512]{2,1,0:T(8,128)(2,1)} %cache.3, s32[5]{0:T(128)S(1)} %copy-done), custom_call_target="tpu_custom_call" | custom-call | bytes 300000 | tf_op jit(solution)/shard_map/prepare_cache/pallas_call | solution.py:382
  25.9 3.7 %collective-permute-done.6.refs_4_ = bf16[1792,128]{1,0:T(8,128)(2,1)S(1)} collective-permute-done((bf16[1792,128]{1,0:T(8,128)(2,1)S(1)}, bf16[1792,128]{1,0:T(8,128)(2,1)S(1)}, u32[]{:S(2)}, u32[]{:S(2)}) %collective-permute-start.6) | collective-permute-done | bytes 458784 | tf_op jit(solution)/shard_map/ppermute | solution.py:347
  30.4 1.4 %collective-permute-done.3.a3 = bf16[928,128]{1,0:T(8,128)(2,1)S(1)} collective-permute-done((bf16[928,128]{1,0:T(8,128)(2,1)S(1)}, bf16[928,128]{1,0:T(8,128)(2,1)S(1)}, u32[]{:S(2)}, u32[]{:S(2)}) %collective-permute-start.3) | collective-permute-done | bytes 237600 | tf_op jit(solution)/shard_map/ppermute | solution.py:344
  33.1 1.1 %place_weights.1 = (bf16[4,512,640]{2,1,0:T(8,128)(2,1)S(1)}, bf16[4,512,512]{2,1,0:T(8,128)(2,1)S(1)}) custom-call(bf16[1792,128]{1,0:T(8,128)(2,1)S(1)} %get-tuple-element.38.refs_0_, bf16[1792,128]{1,0:T(8,128)(2,1)S(1)} %collective-permute-done.8.refs_1_, bf16[1792,128]{1,0:T(8,128)(2,1)S(1)} %collective-permute-done.5.refs_2_, ...), custom_call_target="tpu_custom_call" | custom-call | bytes 300000 | tf_op jit(solution)/shard_map/place_weights/pallas_call | solution.py:371
  34.4 3.6 %chunk_a.1 = (bf16[896,128]{1,0:T(8,128)(2,1)S(1)}, f32[896,128]{1,0:T(8,128)S(1)}, f32[896,128]{1,0:T(8,128)S(1)}, f32[896,128]{1,0:T(8,128)S(1)}, bf16[256,512...) custom-call(bf16[256,2048]{1,0:T(8,128)(2,1)S(1)} %norm_a.1.normed, bf16[4,512,640]{2,1,0:T(8,128)(2,1)S(1)} %get-tuple-element.39.w_ref, ...), custom_call_target="tpu_custom_call" | custom-call | flops 100000000 | bytes 300000 | tf_op jit(solution)/shard_map/chunk_a/pallas_call | solution.py:393
  38.1 3.6 %collective-permute-start.12 = (bf16[896,128]{1,0:T(8,128)(2,1)S(1)}, bf16[896,128]{1,0:T(8,128)(2,1)S(1)}, u32[]{:S(2)}, u32[]{:S(2)}) collective-permute-start(bf16[896,128]{1,0:T(8,128)(2,1)S(1)} %get-tuple-element.43), channel_id=1, source_target_pairs={{0,1},{1,3},{3,2},{2,0},{4,5},{5,7},{7,6},{6,4},{8,9},{9,11},{11,1... | collective-permute-start | bytes 688136 | tf_op jit(solution)/shard_map/ppermute | solution.py:344
  42.1 4.7 %chunk_b.1 = (bf16[896,128]{1,0:T(8,128)(2,1)S(1)}, f32[896,128]{1,0:T(8,128)S(1)}, f32[896,128]{1,0:T(8,128)S(1)}, f32[896,128]{1,0:T(8,128)S(1)}, f32[16,640]{1,0:T(8,128)S(1)}) custom-call(bf16[272,2048]{1,0:T(8,128)(2,1)S(1)} %norm_b.1.normed, bf16[4,512,640]{2,1,0:T(8,128)(2,1)S(1)} %get-tuple-element.39.w_ref, ...), custom_call_target="tpu_custom_call" | custom-call | flops 1000000000 | bytes 300000 | tf_op jit(solution)/shard_map/chunk_b/pallas_call | solution.py:403
  46.9 4.4 %decode.1 = (f32[8,512]{1,0:T(8,128)S(1)}, f32[8,512]{1,0:T(8,128)S(1)}, f32[8,512]{1,0:T(8,128)S(1)}, f32[8,512]{1,0:T(8,128)S(1)}) custom-call(f32[16,640]{1,0:T(8,128)S(1)} %get-tuple-element.49.late_ref, bf16[4,512,512]{2,1,0:T(8,128)(2,1)S(1)} %get-tuple-element.40.o_ref, f32[516,128]{1,0:T(8,128)S(1)} %broadcast_in_dim.2.m_ref, s32[5]{0:T(128)S(1)} %copy-done, ...), custom_call_target="tpu_custom_call" | custom-call | flops 1000000 | bytes 300000 | tf_op jit(solution)/shard_map/decode/pallas_call | solution.py:415
  51.4 1.9 %collective-permute-start.13 = (bf16[896,128]{1,0:T(8,128)(2,1)S(1)}, bf16[896,128]{1,0:T(8,128)(2,1)S(1)}, u32[]{:S(2)}, u32[]{:S(2)}) collective-permute-start(bf16[896,128]{1,0:T(8,128)(2,1)S(1)} %add_convert_fusion.3), channel_id=1, source_target_pairs={{0,1},{1,3},{3,2},{2,0},{4,5},{5,7},{7,6},{6,4},{8,9},{9,11},{11,1... | collective-permute-start | bytes 688136 | tf_op jit(solution)/shard_map/ppermute | solution.py:344
  54.2 6.6 %collective-permute-done.13 = bf16[896,128]{1,0:T(8,128)(2,1)S(1)} collective-permute-done((bf16[896,128]{1,0:T(8,128)(2,1)S(1)}, bf16[896,128]{1,0:T(8,128)(2,1)S(1)}, u32[]{:S(2)}, u32[]{:S(2)}) %collective-permute-start.13) | collective-permute-done | bytes 229408 | tf_op jit(solution)/shard_map/ppermute | solution.py:344
  61.9 3.9 %collective-permute-done.20 = bf16[896,128]{1,0:T(8,128)(2,1)S(1)} collective-permute-done((bf16[896,128]{1,0:T(8,128)(2,1)S(1)}, bf16[896,128]{1,0:T(8,128)(2,1)S(1)}, u32[]{:S(2)}, u32[]{:S(2)}) %collective-permute-start.20) | collective-permute-done | bytes 229408 | tf_op jit(solution)/shard_map/ppermute | solution.py:344
  67.8 2.1 %collective-permute-start.17 = (f32[8,512]{1,0:T(8,128)S(1)}, f32[8,512]{1,0:T(8,128)S(1)}, u32[]{:S(2)}, u32[]{:S(2)}) collective-permute-start(f32[8,512]{1,0:T(8,128)S(1)} %get-tuple-element.52), channel_id=1, source_target_pairs={{0,2},{1,3},{2,0},{3,1},{4,6},{5,7},{6,4},{7,5},{8,10},{9,11},{10,... | collective-permute-start | bytes 49160 | tf_op jit(solution)/shard_map/ppermute | solution.py:430
  69.9 1.8 %collective-permute-start.18 = (f32[8,512]{1,0:T(8,128)S(1)}, f32[8,512]{1,0:T(8,128)S(1)}, u32[]{:S(2)}, u32[]{:S(2)}) collective-permute-start(f32[8,512]{1,0:T(8,128)S(1)} %get-tuple-element.53), channel_id=1, source_target_pairs={{0,3},{1,0},{2,1},{3,2},{4,7},{5,4},{6,5},{7,6},{8,11},{9,8},{10,9... | collective-permute-start | bytes 49160 | tf_op jit(solution)/shard_map/ppermute | solution.py:430
  71.7 3.1 %collective-permute-done.16.p1 = f32[8,512]{1,0:T(8,128)S(1)} collective-permute-done((f32[8,512]{1,0:T(8,128)S(1)}, f32[8,512]{1,0:T(8,128)S(1)}, u32[]{:S(2)}, u32[]{:S(2)}) %collective-permute-start.16) | collective-permute-done | bytes 16416 | tf_op jit(solution)/shard_map/ppermute | solution.py:430
  (42 shorter events, 9.0 us)
Async XLA Ops:
  0.0 23.6 %copy-start.1 = (s32[516]{0:T(1024)S(1)}, s32[516]{0:T(1024)}, u32[]{:S(2)}) copy-start(s32[516]{0:T(1024)} %param.13) | copy-start | bytes 6196
  0.0 23.6 %copy-start = (s32[5]{0:T(128)S(1)}, s32[5]{0:T(128)}, u32[]{:S(2)}) copy-start(s32[5]{0:T(128)} %len_ref.3) | copy-start | bytes 64
  1.5 10.7 %collective-permute-start = (bf16[928,128]{1,0:T(8,128)(2,1)S(1)}, bf16[928,128]{1,0:T(8,128)(2,1)S(1)}, u32[]{:S(2)}, u32[]{:S(2)}) collective-permute-start(bf16[928,128]{1,0:T(8,128)(2,1)S(1)} %get-tuple-element.33.a0), channel_id=1, source_target_pairs={{0,1},{1,3},{3,2},{2,0},{4,5},{5,7},{7,6},{6,4},{8,9},{9,11},{11,1... | collective-permute-start | bytes 712712 | tf_op jit(solution)/shard_map/ppermute | solution.py:344
  4.6 12.7 %collective-permute-start.2 = (bf16[928,128]{1,0:T(8,128)(2,1)S(1)}, bf16[928,128]{1,0:T(8,128)(2,1)S(1)}, u32[]{:S(2)}, u32[]{:S(2)}) collective-permute-start(bf16[928,128]{1,0:T(8,128)(2,1)S(1)} %get-tuple-element.34.b0), channel_id=1, source_target_pairs={{0,1},{1,3},{3,2},{2,0},{4,5},{5,7},{7,6},{6,4},{8,9},{9,11},{11,1... | collective-permute-start | bytes 712712 | tf_op jit(solution)/shard_map/ppermute | solution.py:344
  7.2 18.6 %collective-permute-start.7 = (bf16[1792,128]{1,0:T(8,128)(2,1)S(1)}, bf16[1792,128]{1,0:T(8,128)(2,1)S(1)}, u32[]{:S(2)}, u32[]{:S(2)}) collective-permute-start(bf16[1792,128]{1,0:T(8,128)(2,1)S(1)} %get-tuple-element.38.refs_0_), channel_id=1, source_target_pairs={{0,24},{4,28},{8,16},{12,20},{16,8},{20,12},{24,0},{28,4},{1,25},{... | collective-permute-start | bytes 1376264 | tf_op jit(solution)/shard_map/ppermute | solution.py:347
  9.7 20.0 %collective-permute-start.6 = (bf16[1792,128]{1,0:T(8,128)(2,1)S(1)}, bf16[1792,128]{1,0:T(8,128)(2,1)S(1)}, u32[]{:S(2)}, u32[]{:S(2)}) collective-permute-start(bf16[1792,128]{1,0:T(8,128)(2,1)S(1)} %get-tuple-element.38.refs_0_), channel_id=1, source_target_pairs={{0,16},{4,20},{8,24},{12,28},{16,0},{20,4},{24,8},{28,12},{1,17},{... | collective-permute-start | bytes 1376264 | tf_op jit(solution)/shard_map/ppermute | solution.py:347
  10.2 19.6 %collective-permute-start.5 = (bf16[1792,128]{1,0:T(8,128)(2,1)S(1)}, bf16[1792,128]{1,0:T(8,128)(2,1)S(1)}, u32[]{:S(2)}, u32[]{:S(2)}) collective-permute-start(bf16[1792,128]{1,0:T(8,128)(2,1)S(1)} %get-tuple-element.38.refs_0_), channel_id=1, source_target_pairs={{0,8},{4,12},{8,0},{12,4},{16,24},{20,28},{24,16},{28,20},{1,9},{5... | collective-permute-start | bytes 1376264 | tf_op jit(solution)/shard_map/ppermute | solution.py:347
  12.2 10.2 %collective-permute-start.1 = (bf16[928,128]{1,0:T(8,128)(2,1)S(1)}, bf16[928,128]{1,0:T(8,128)(2,1)S(1)}, u32[]{:S(2)}, u32[]{:S(2)}) collective-permute-start(bf16[928,128]{1,0:T(8,128)(2,1)S(1)} %collective-permute-done.a1), channel_id=1, source_target_pairs={{0,1},{1,3},{3,2},{2,0},{4,5},{5,7},{7,6},{6,4},{8,9},{9,11},{11,1... | collective-permute-start | bytes 712712 | tf_op jit(solution)/shard_map/ppermute | solution.py:344
  17.3 12.8 %collective-permute-start.4 = (bf16[928,128]{1,0:T(8,128)(2,1)S(1)}, bf16[928,128]{1,0:T(8,128)(2,1)S(1)}, u32[]{:S(2)}, u32[]{:S(2)}) collective-permute-start(bf16[928,128]{1,0:T(8,128)(2,1)S(1)} %collective-permute-done.2.ref.b1), channel_id=1, source_target_pairs={{0,1},{1,3},{3,2},{2,0},{4,5},{5,7},{7,6},{6,4},{8,9},{9,11},{11,1... | collective-permute-start | bytes 712712 | tf_op jit(solution)/shard_map/ppermute | solution.py:344
  22.4 9.4 %collective-permute-start.3 = (bf16[928,128]{1,0:T(8,128)(2,1)S(1)}, bf16[928,128]{1,0:T(8,128)(2,1)S(1)}, u32[]{:S(2)}, u32[]{:S(2)}) collective-permute-start(bf16[928,128]{1,0:T(8,128)(2,1)S(1)} %collective-permute-done.1.a2), channel_id=1, source_target_pairs={{0,1},{1,3},{3,2},{2,0},{4,5},{5,7},{7,6},{6,4},{8,9},{9,11},{11,1... | collective-permute-start | bytes 712712 | tf_op jit(solution)/shard_map/ppermute | solution.py:344
  25.8 7.3 %collective-permute-start.11 = (bf16[1792,128]{1,0:T(8,128)(2,1)S(1)}, bf16[1792,128]{1,0:T(8,128)(2,1)S(1)}, u32[]{:S(2)}, u32[]{:S(2)}) collective-permute-start(bf16[1792,128]{1,0:T(8,128)(2,1)S(1)} %collective-permute-done.7.refs_6_), channel_id=1, source_target_pairs={{0,4},{4,0},{8,12},{12,8},{16,20},{20,16},{24,28},{28,24},{1,5},{5... | collective-permute-start | bytes 1376264 | tf_op jit(solution)/shard_map/ppermute | solution.py:347
  29.6 3.5 %collective-permute-start.10 = (bf16[1792,128]{1,0:T(8,128)(2,1)S(1)}, bf16[1792,128]{1,0:T(8,128)(2,1)S(1)}, u32[]{:S(2)}, u32[]{:S(2)}) collective-permute-start(bf16[1792,128]{1,0:T(8,128)(2,1)S(1)} %collective-permute-done.6.refs_4_), channel_id=1, source_target_pairs={{0,4},{4,0},{8,12},{12,8},{16,20},{20,16},{24,28},{28,24},{1,5},{5... | collective-permute-start | bytes 1376264 | tf_op jit(solution)/shard_map/ppermute | solution.py:347
  29.7 3.4 %collective-permute-start.9 = (bf16[1792,128]{1,0:T(8,128)(2,1)S(1)}, bf16[1792,128]{1,0:T(8,128)(2,1)S(1)}, u32[]{:S(2)}, u32[]{:S(2)}) collective-permute-start(bf16[1792,128]{1,0:T(8,128)(2,1)S(1)} %collective-permute-done.5.refs_2_), channel_id=1, source_target_pairs={{0,4},{4,0},{8,12},{12,8},{16,20},{20,16},{24,28},{28,24},{1,5},{5... | collective-permute-start | bytes 1376264 | tf_op jit(solution)/shard_map/ppermute | solution.py:347
  30.2 2.9 %collective-permute-start.8 = (bf16[1792,128]{1,0:T(8,128)(2,1)S(1)}, bf16[1792,128]{1,0:T(8,128)(2,1)S(1)}, u32[]{:S(2)}, u32[]{:S(2)}) collective-permute-start(bf16[1792,128]{1,0:T(8,128)(2,1)S(1)} %get-tuple-element.38.refs_0_), channel_id=1, source_target_pairs={{0,4},{4,0},{8,12},{12,8},{16,20},{20,16},{24,28},{28,24},{1,5},{5... | collective-permute-start | bytes 1376264 | tf_op jit(solution)/shard_map/ppermute | solution.py:347
  31.8 9.9 %collective-permute-start.15 = (bf16[928,128]{1,0:T(8,128)(2,1)S(1)}, bf16[928,128]{1,0:T(8,128)(2,1)S(1)}, u32[]{:S(2)}, u32[]{:S(2)}) collective-permute-start(bf16[928,128]{1,0:T(8,128)(2,1)S(1)} %collective-permute-done.4.ref.b2), channel_id=1, source_target_pairs={{0,1},{1,3},{3,2},{2,0},{4,5},{5,7},{7,6},{6,4},{8,9},{9,11},{11,1... | collective-permute-start | bytes 712712 | tf_op jit(solution)/shard_map/ppermute | solution.py:344
  38.1 13.3 %collective-permute-start.12 = (bf16[896,128]{1,0:T(8,128)(2,1)S(1)}, bf16[896,128]{1,0:T(8,128)(2,1)S(1)}, u32[]{:S(2)}, u32[]{:S(2)}) collective-permute-start(bf16[896,128]{1,0:T(8,128)(2,1)S(1)} %get-tuple-element.43), channel_id=1, source_target_pairs={{0,1},{1,3},{3,2},{2,0},{4,5},{5,7},{7,6},{6,4},{8,9},{9,11},{11,1... | collective-permute-start | bytes 688136 | tf_op jit(solution)/shard_map/ppermute | solution.py:344
  46.8 7.3 %collective-permute-start.19 = (bf16[896,128]{1,0:T(8,128)(2,1)S(1)}, bf16[896,128]{1,0:T(8,128)(2,1)S(1)}, u32[]{:S(2)}, u32[]{:S(2)}) collective-permute-start(bf16[896,128]{1,0:T(8,128)(2,1)S(1)} %get-tuple-element.56), channel_id=1, source_target_pairs={{0,1},{1,3},{3,2},{2,0},{4,5},{5,7},{7,6},{6,4},{8,9},{9,11},{11,1... | collective-permute-start | bytes 688136 | tf_op jit(solution)/shard_map/ppermute | solution.py:344
  51.4 9.5 %collective-permute-start.13 = (bf16[896,128]{1,0:T(8,128)(2,1)S(1)}, bf16[896,128]{1,0:T(8,128)(2,1)S(1)}, u32[]{:S(2)}, u32[]{:S(2)}) collective-permute-start(bf16[896,128]{1,0:T(8,128)(2,1)S(1)} %add_convert_fusion.3), channel_id=1, source_target_pairs={{0,1},{1,3},{3,2},{2,0},{4,5},{5,7},{7,6},{6,4},{8,9},{9,11},{11,1... | collective-permute-start | bytes 688136 | tf_op jit(solution)/shard_map/ppermute | solution.py:344
  54.2 11.6 %collective-permute-start.20 = (bf16[896,128]{1,0:T(8,128)(2,1)S(1)}, bf16[896,128]{1,0:T(8,128)(2,1)S(1)}, u32[]{:S(2)}, u32[]{:S(2)}) collective-permute-start(bf16[896,128]{1,0:T(8,128)(2,1)S(1)} %add_convert_fusion.1), channel_id=1, source_target_pairs={{0,1},{1,3},{3,2},{2,0},{4,5},{5,7},{7,6},{6,4},{8,9},{9,11},{11,1... | collective-permute-start | bytes 688136 | tf_op jit(solution)/shard_map/ppermute | solution.py:344
  60.9 14.0 %collective-permute-start.14 = (bf16[896,128]{1,0:T(8,128)(2,1)S(1)}, bf16[896,128]{1,0:T(8,128)(2,1)S(1)}, u32[]{:S(2)}, u32[]{:S(2)}) collective-permute-start(bf16[896,128]{1,0:T(8,128)(2,1)S(1)} %add_convert_fusion.2), channel_id=1, source_target_pairs={{0,1},{1,3},{3,2},{2,0},{4,5},{5,7},{7,6},{6,4},{8,9},{9,11},{11,1... | collective-permute-start | bytes 688136 | tf_op jit(solution)/shard_map/ppermute | solution.py:344
  65.8 9.2 %collective-permute-start.21 = (bf16[896,128]{1,0:T(8,128)(2,1)S(1)}, bf16[896,128]{1,0:T(8,128)(2,1)S(1)}, u32[]{:S(2)}, u32[]{:S(2)}) collective-permute-start(bf16[896,128]{1,0:T(8,128)(2,1)S(1)} %add_convert_fusion), channel_id=1, source_target_pairs={{0,1},{1,3},{3,2},{2,0},{4,5},{5,7},{7,6},{6,4},{8,9},{9,11},{11,1... | collective-permute-start | bytes 688136 | tf_op jit(solution)/shard_map/ppermute | solution.py:344
  66.8 8.0 %collective-permute-start.16 = (f32[8,512]{1,0:T(8,128)S(1)}, f32[8,512]{1,0:T(8,128)S(1)}, u32[]{:S(2)}, u32[]{:S(2)}) collective-permute-start(f32[8,512]{1,0:T(8,128)S(1)} %get-tuple-element.51), channel_id=1, source_target_pairs={{0,1},{1,2},{2,3},{3,0},{4,5},{5,6},{6,7},{7,4},{8,9},{9,10},{10,1... | collective-permute-start | bytes 49160 | tf_op jit(solution)/shard_map/ppermute | solution.py:430
  67.8 7.1 %collective-permute-start.17 = (f32[8,512]{1,0:T(8,128)S(1)}, f32[8,512]{1,0:T(8,128)S(1)}, u32[]{:S(2)}, u32[]{:S(2)}) collective-permute-start(f32[8,512]{1,0:T(8,128)S(1)} %get-tuple-element.52), channel_id=1, source_target_pairs={{0,2},{1,3},{2,0},{3,1},{4,6},{5,7},{6,4},{7,5},{8,10},{9,11},{10,... | collective-permute-start | bytes 49160 | tf_op jit(solution)/shard_map/ppermute | solution.py:430
  69.9 5.0 %collective-permute-start.18 = (f32[8,512]{1,0:T(8,128)S(1)}, f32[8,512]{1,0:T(8,128)S(1)}, u32[]{:S(2)}, u32[]{:S(2)}) collective-permute-start(f32[8,512]{1,0:T(8,128)S(1)} %get-tuple-element.53), channel_id=1, source_target_pairs={{0,3},{1,0},{2,1},{3,2},{4,7},{5,4},{6,5},{7,6},{8,11},{9,8},{10,9... | collective-permute-start | bytes 49160 | tf_op jit(solution)/shard_map/ppermute | solution.py:430

commit v4 on v3

--- a/solution.py
+++ b/solution.py
@@ -18,7 +18,7 @@
 HBM = pl.BlockSpec(memory_space=pltpu.MemorySpace.HBM)
 TAIL = 3 * HALF
 BODY = TAIL + HALF // 2
-EXTRA = 32
+EXTRA = 16
 QROWS = 224
 OROWS = 448
 WROWS = 4 * QROWS + 2 * OROWS
@@ -26,8 +26,10 @@
 COST_SQ = 1_000_000_000
 COST_CA = 100_000_000
 COST_CB = 1_000_000_000
-COST_F = 2_000_000_000
+COST_F = 1_000_000
+COST_G = 10_000_000
 COST_D = 1_000_000
+COST_E = 1_000_000
 
 
 def gray(place):
@@ -83,11 +85,11 @@
         ref[BODY:, :] = jnp.zeros((EXTRA, 128), BF16)
     gain = g_ref[...].reshape(1, 448)
     for t in range(3):
-        a_ref[BODY + 8 * t : BODY + 8 * t + 1, :] = gain[:, t * 128 : (t + 1) * 128]
-        b_ref[BODY + 8 * t : BODY + 8 * t + DEC, :] = h_ref[SPAN_TOKENS:, t * 128 : (t + 1) * 128]
+        a_ref[BODY + t : BODY + t + 1, :] = gain[:, t * 128 : (t + 1) * 128]
+        b_ref[BODY + DEC * t : BODY + DEC * (t + 1), :] = h_ref[SPAN_TOKENS:, t * 128 : (t + 1) * 128]
     last = gain[:, 384:448]
-    a_ref[BODY + 24 : BODY + 25, :] = jnp.concatenate([last, last], axis=1)
-    b_ref[BODY + 24 : BODY + 24 + DEC, 0:64] = h_ref[SPAN_TOKENS:, 384:448]
+    a_ref[BODY + 3 : BODY + 4, :] = jnp.concatenate([last, last], axis=1)
+    b_ref[BODY + 3 * DEC :, 0:64] = h_ref[SPAN_TOKENS:, 384:448]
     copies[2].wait()
     copies[3].wait()
     width = FEATURE_WIDTH + LANES
@@ -159,8 +161,9 @@
     tail = jnp.concatenate([jnp.where(middle, tail, 0.0), jnp.where(middle, 0.0, tail)], axis=0)
     tiles = [ref[t * HALF : (t + 1) * HALF, :].astype(F32) for t in range(3)] + [tail]
     if rows > HALF:
-        late = [ref[BODY + 8 * t : BODY + 8 * t + 8, :].astype(F32) for t in range(4)]
-        zeros = jnp.zeros((8, 128), F32)
+        extra = ref[BODY:, :].astype(F32)
+        late = [extra[DEC * t : DEC * (t + 1), :] for t in range(4)]
+        zeros = jnp.zeros((16 - DEC, 128), F32)
         tiles = [jnp.concatenate(parts + (zeros,), axis=0) for parts in zip(tiles, late)]
     return tiles
 
@@ -186,16 +189,12 @@
     scale = jnp.broadcast_to(lax.rsqrt(mean + 1e-06), (rows, 128))
     for k, tiles in enumerate(pieces):
         for t, tile in enumerate(tiles):
-            gain = gain_ref[k][BODY + 8 * t : BODY + 8 * t + 1, :].astype(F32)
+            gain = gain_ref[k][BODY + t : BODY + t + 1, :].astype(F32)
             out_ref[:, k * 512 + t * 128 : k * 512 + (t + 1) * 128] = (tile * scale * gain).astype(BF16)
 
 
 def norm_a(a0, a1, a2, a3, out):
     norm((a0, a1, a2, a3), (a0, a1, a2, a3), {}, out, HALF)
-
-
-def norm_b(b0, b1, b2, b3, s1, s2, a0, a1, a2, a3, out):
-    norm((b0, b1, b2, b3), (a0, a1, a2, a3), {1: s1, 2: s2}, out, HALF + 16)
 
 
 def project(normed, w_ref):
@@ -226,16 +225,31 @@
     return mask * total / below
 
 
-def emit(att, o_ref, first_ref, rest):
+def emit(att, o_ref, outs, start, recv=None):
     place = gray(lax.axis_index("col"))
-    for s in range(4):
+    middle = lane((HALF // 2, 128)) < 64
+    for s, out in enumerate(outs, start):
         part = dot(att, o_ref[gray((place + 3 - s) & 3)])
-        out = first_ref if s == 0 else rest[s - 1]
-        for t in range(3):
-            out[t * HALF : (t + 1) * HALF, :] = part[:HALF, t * 128 : (t + 1) * 128].astype(out.dtype)
+        tiles = [part[:, t * 128 : (t + 1) * 128] for t in range(3)]
         last = part[:, 384:512]
-        middle = lane((HALF // 2, 128)) < 64
-        out[TAIL:BODY, :] = jnp.where(middle, last[: HALF // 2], last[HALF // 2 : HALF]).astype(out.dtype)
+        tiles.append(jnp.where(middle, last[: HALF // 2], last[HALF // 2 :]))
+        for t, tile in enumerate(tiles):
+            at = slice(t * HALF, t * HALF + tile.shape[0])
+            if recv is not None:
+                tile = tile + recv[at, :].astype(F32)
+            out[at, :] = tile.astype(out.dtype)
+
+
+def hop_1(att_ref, o_ref, recv, out):
+    emit(att_ref[...], o_ref, (out,), 1, recv)
+
+
+def hop_2(att_ref, o_ref, recv, out):
+    emit(att_ref[...], o_ref, (out,), 2, recv)
+
+
+def hop_3(att_ref, o_ref, out):
+    emit(att_ref[...], o_ref, (out,), 3)
 
 
 def chunk_a(normed, w_ref, o_ref, ck_ref, cv_ref, m_ref, first, r1, r2, r3, ka_ref, va_ref):
@@ -254,12 +268,13 @@
             keys = slice(b * 512, (b + 1) * 512)
             total += dot(weigh(dot_nt(q, ck_ref[keys, at])), cv_ref[keys, at])
         outs.append(divide(total, mask).astype(BF16))
-    emit(jnp.concatenate(outs, axis=1), o_ref, first, (r1, r2, r3))
+    emit(jnp.concatenate(outs, axis=1), o_ref, (first, r1, r2, r3), 0)
 
 
 def chunk_b(
-    normed, w_ref, o_ref, ck_ref, cv_ref, m_ref, ka_ref, va_ref, first, r1, r2, r3, late_ref, kb, vb
+    b0, b1, b2, b3, s1, s2, a0, a1, a2, a3, w_ref, o_ref, ck_ref, cv_ref, m_ref, ka_ref, va_ref, first, att_ref, late_ref, normed, kb, vb
 ):
+    norm((b0, b1, b2, b3), (a0, a1, a2, a3), {1: s1, 2: s2}, normed, HALF + 16)
     kv, queries = project(normed, w_ref)
     late_ref[:, 0:512] = kv[HALF:]
     late_ref[:, 512:640] = queries[HALF:]
@@ -279,34 +294,69 @@
             keys = slice(b * 512, (b + 1) * 512)
             total += dot(weigh(dot_nt(q, ck_ref[keys, at])), cv_ref[keys, at])
         outs.append(divide(total, mask).astype(BF16))
-    emit(jnp.concatenate(outs, axis=1), o_ref, first, (r1, r2, r3))
-
-
-def decode(late_ref, o_ref, m_ref, len_ref, cache, own_ref, s1, s2, s3, slab, sems):
-    copies = [pltpu.make_async_copy(cache.at[d + 1], slab.at[d], sems.at[d]) for d in range(DEC)]
-    for copy in copies:
-        copy.start()
+    att = jnp.concatenate(outs, axis=1)
+    att_ref[...] = att
+    emit(att, o_ref, (first,), 0)
+
+
+def decode(late_ref, o_ref, m_ref, len_ref, cache, first, r1, r2, r3, slab, total_ref, below_ref, sems):
+    steps = [(d, b) for d in range(DEC) for b in range(2)]
+
+    def copy(d, b):
+        at = pl.ds(b * 512, 512)
+        return pltpu.make_async_copy(cache.at[d + 1, at], slab.at[d, at], sems.at[d, b])
+
+    for d, b in steps:
+
+        @pl.when(b * 512 < len_ref[d + 1])
+        def _():
+            copy(d, b).start()
+
     fresh = late_ref[:, 0:512]
     late = jnp.concatenate([query_of(late_ref[:, 512:640], h)[0] for h in range(4)], axis=1)
     own = row((16, 512)) == lane((16, 512)) // LANES
-    position = lane((16, 1024))
+    queries = []
+    for d in range(DEC):
+        q = jnp.where(own, jnp.broadcast_to(late[d : d + 1], (16, 512)), 0.0)
+        queries.append(q.astype(BF16))
+        new = jnp.broadcast_to(fresh[d : d + 1], (16, 512))
+        live = m_ref[2 * HALF + d : 2 * HALF + d + 1, 0:1]
+        self_score = jnp.sum(q * new, axis=1, keepdims=True) + 1.0
+        self_weight = (self_score * self_score + 1.0) * live
+        total_ref[d] = self_weight.astype(BF16).astype(F32) * new
+        below_ref[d] = jnp.broadcast_to(self_weight + 2.0 * (1.0 - live), (16, 128))
+    for d, b in steps:
+
+        @pl.when(b * 512 < len_ref[d + 1])
+        def _():
+            copy(d, b).wait()
+            keys = slab[d, b * 512 : (b + 1) * 512, :]
+            score = dot_nt(queries[d], keys) + 1.0
+            position = b * 512 + lane((16, 512))
+            weight = jnp.where(position < len_ref[d + 1], score * score + 1.0, 0.0)
+            total_ref[d] += dot(weight.astype(BF16), keys)
+            below_ref[d] += jnp.broadcast_to(jnp.sum(weight, axis=1, keepdims=True), (16, 128))
+
     decoded = jnp.zeros((16, 512), F32)
     for d in range(DEC):
-        copies[d].wait()
-        q = jnp.where(own, jnp.broadcast_to(late[d : d + 1], (16, 512)), 0.0)
-        new = jnp.broadcast_to(fresh[d : d + 1], (16, 512))
         live = m_ref[2 * HALF + d : 2 * HALF + d + 1, 0:1]
-        score = dot_nt(q.astype(BF16), slab[d]) + 1.0
-        weight = jnp.where(position < len_ref[d + 1], score * score + 1.0, 0.0)
-        self_score = jnp.sum(q * new, axis=1, keepdims=True) + 1.0
-        self_weight = (self_score * self_score + 1.0) * live
-        total = dot(weight.astype(BF16), slab[d]) + self_weight.astype(BF16).astype(F32) * new
-        below = jnp.sum(weight, axis=1, keepdims=True) + self_weight + 2.0 * (1.0 - live)
-        value = jnp.sum(jnp.where(own, live * total / below, 0.0), axis=0, keepdims=True)
+        ratio = live * total_ref[d] / below_ref[d][:, 0:1]
+        value = jnp.sum(jnp.where(own, ratio, 0.0), axis=0, keepdims=True)
         decoded = jnp.where(row((16, 512)) == d, jnp.broadcast_to(value, (16, 512)), decoded)
-    me = lax.axis_index("col")
-    for k, out in enumerate((own_ref, s1, s2, s3)):
-        out[...] = dot(decoded.astype(BF16), o_ref[(me + k) & 3])[0:8]
+    place = gray(lax.axis_index("col"))
+    for s, out in enumerate((first, r1, r2, r3)):
+        part = dot(decoded.astype(BF16), o_ref[gray((place + 3 - s) & 3)])
+        out[...] = jnp.concatenate(
+            [part[0:DEC, t * 128 : (t + 1) * 128] for t in range(4)], axis=0
+        ).astype(out.dtype)
+
+
+def join(recv, part, new_ref, out):
+    out[:BODY, :] = (recv[:BODY, :].astype(F32) + part[...]).astype(BF16)
+    late = new_ref[...].astype(F32)
+    if recv.shape[0] > BODY:
+        late = late + recv[BODY:, :].astype(F32)
+    out[BODY:, :] = late.astype(BF16)
 
 
 def unpack_sum(recv, part, out, base):
@@ -318,15 +368,18 @@
     out[base + HALF // 2 : base + HALF, 384:448] = tail[:, 64:128].astype(BF16)
 
 
-def finish_a(recv, part, p0, p1, p2, p3, out, late):
+def finish_a(recv, part, back, own_late, out, late):
     unpack_sum(recv, part, out, 0)
-    late[...] = ((p0[...] + p1[...]) + (p2[...] + p3[...])).astype(BF16)
-
-
-def finish_b(done, late, recv, part, out):
+    late[...] = recv[BODY:, :].astype(F32) + (back[...].astype(F32) + own_late[...])
+
+
+def finish(done, late, recv, part, out):
     out[:HALF, :] = done[...]
     unpack_sum(recv, part, out, HALF)
-    out[SPAN_TOKENS:, :] = late[0:DEC, 0:448]
+    for t in range(4):
+        width = 128 if t < 3 else 64
+        rows = late[DEC * t : DEC * (t + 1), 0:width]
+        out[SPAN_TOKENS:, t * 128 : t * 128 + width] = rows.astype(BF16)
 
 
 def in_hbm(x):
@@ -376,9 +429,6 @@
         name="place_weights",
     )(*blocks)
     na = call(norm_a, shaped((HALF, 2048)), [VMEM] * 4, flops=COST_X, nbytes=300_000, name="norm_a")(*a)
-    nb = call(norm_b, shaped((HALF + 16, 2048)), [VMEM] * 10, nbytes=300_000, name="norm_b")(
-        *b, s1, s2, *a
-    )
     ck, cv = call(
         prepare_cache,
         (shaped((1024, 512)), shaped((1024, 512))),
@@ -389,10 +439,11 @@
         mib=12,
     )(in_hbm(cache), cached)
     mask = jnp.broadcast_to(token_mask.astype(F32)[:, None], (token_mask.shape[0], 128))
-    body = shaped((BODY, 128), F32)
+    parts = (shaped((BODY, 128), F32),) * 3
+    wide, wire = shaped((HALF, 512)), shaped((BODY, 128))
     first, *rest_a, ka, va = call(
         chunk_a,
-        (shaped((BODY, 128)), body, body, body, shaped((HALF, 512)), shaped((HALF, 512))),
+        (wire, *parts, wide, wide),
         [VMEM] * 6,
         flops=COST_CA,
         nbytes=300_000,
@@ -400,45 +451,62 @@
         mib=20,
     )(na, w, o, ck, cv, mask)
     send_a = onward(first)
-    first, *rest_b, late = call(
+    first, att, late = call(
         chunk_b,
-        (shaped((BODY, 128)), body, body, body, shaped((16, 640), F32)),
-        [VMEM] * 8,
-        scratch=[pltpu.VMEM((HALF, 512), BF16), pltpu.VMEM((HALF, 512), BF16)],
+        (wire, wide, shaped((16, 640), F32)),
+        [VMEM] * 17,
+        scratch=[
+            pltpu.VMEM((HALF + 16, 2048), BF16),
+            pltpu.VMEM((HALF, 512), BF16),
+            pltpu.VMEM((HALF, 512), BF16),
+        ],
         flops=COST_CB,
         nbytes=300_000,
         name="chunk_b",
         mib=20,
-    )(nb, w, o, ck, cv, mask, ka, va)
+    )(*b, s1, s2, *a, w, o, ck, cv, mask, ka, va)
     send_b = onward(first)
-    few = shaped((8, 512), F32)
-    parts = call(
+    own_b = call(hop_3, parts[0], [VMEM] * 2, flops=COST_E, nbytes=300_000, name="hop_3")(att, o)
+
+    def hop(body, recv, name):
+        return onward(call(body, wire, [VMEM] * 3, nbytes=300_000, name=name)(att, o, recv))
+
+    few = shaped((EXTRA, 128), F32)
+    back, *late = call(
         decode,
-        (few, few, few, few),
+        (shaped((EXTRA, 128)), few, few, few),
         [VMEM] * 3 + [SMEM, HBM],
-        scratch=[pltpu.VMEM((DEC, 1024, 512), BF16), pltpu.SemaphoreType.DMA((DEC,))],
+        scratch=[
+            pltpu.VMEM((DEC, 1024, 512), BF16),
+            pltpu.VMEM((DEC, 16, 512), F32),
+            pltpu.VMEM((DEC, 16, 128), F32),
+            pltpu.SemaphoreType.DMA((DEC, 2)),
+        ],
         flops=COST_D,
         nbytes=300_000,
         name="decode",
         mib=12,
     )(late, o, mask, cached, in_hbm(cache))
-    send_a = onward((send_a.astype(F32) + rest_a[0]).astype(BF16))
-    send_b = onward((after(send_b, parts[0]).astype(F32) + rest_b[0]).astype(BF16))
-    send_a = onward((send_a.astype(F32) + rest_a[1]).astype(BF16))
-    send_b = onward((send_b.astype(F32) + rest_b[1]).astype(BF16))
-    parts = parts[:1] + tuple(
-        lax.ppermute(parts[k], "col", [(i, (i + k) % 4) for i in range(4)]) for k in (1, 2, 3)
-    )
-    done, late = call(
+
+    back = lax.ppermute(back, "col", [(gray((p + 1) % 4), gray(p)) for p in range(4)])
+
+    def joined(recv, part, new, name):
+        return call(join, shaped((BODY + EXTRA, 128)), [VMEM] * 3, nbytes=300_000, name=name)(recv, part, new)
+
+    send_a = onward(joined(send_a, rest_a[0], late[0], "join_1"))
+    send_b = hop(hop_1, send_b, "hop_1")
+    send_a = onward(joined(after(send_a, back), rest_a[1], late[1], "join_2"))
+    send_b = hop(hop_2, send_b, "hop_2")
+    done = call(
         finish_a,
-        (shaped((HALF, hidden.shape[1])), shaped((8, 512))),
-        [VMEM] * 6,
+        (shaped((HALF, hidden.shape[1])), few),
+        [VMEM] * 4,
         flops=COST_F,
         nbytes=300_000,
         name="finish_a",
-    )(send_a, rest_a[2], *parts)
-    return call(finish_b, shaped(hidden.shape), [VMEM] * 4, nbytes=300_000, name="finish_b")(
-        done, late, send_b, rest_b[2]
+    )(send_a, rest_a[2], back, late[2])
+    return call(finish, shaped(hidden.shape), [VMEM] * 4, flops=COST_G, nbytes=300_000, name="finish")(
+        *done, send_b, own_b
     )
 
 

time: 76.1 us -> 73.5 us (0.966)
  waiting for transfers between devices: 29.1 us -> 26 us
    ppermute x12, waiting for transfers between devices: 22.1 us -> 19.3 us  [onward(): return lax.ppermute(x, 'col', ring)]
    ppermute x12, starting transfers between devices: 17.6 us -> 19.8 us  [onward(): return lax.ppermute(x, 'col', ring)]
    ppermute x3 -> x1, starting transfers between devices: 4.89 us -> 2.91 us  [shards(): lax.ppermute(back, 'col', [(gray((p + 1) % 4), gray(p)) for p in range(4)])]
    ppermute x3 -> x1, waiting for transfers between devices: 3.14 us -> 2.77 us  [shards(): lax.ppermute(back, 'col', [(gray((p + 1) % 4), gray(p)) for p in range(4)])]
    pallas_call x6 -> x10, Pallas kernels: 14.2 us -> 14.3 us  [the longest x1 4.49 us: shards(): call(chunk_b, (wire, wide, shaped((16, 640), F32)), [VMEM] * 17, scratch=...]
  transfers between devices with their start and end apart: 22 -> 20, of which waited for: 10 -> 11; matrix products, arithmetic and copies ran while one was open for 0% -> 0% of each run, Pallas kernels for 23% -> 24%
where the time goes in v4:
time: 73.5 us; the launch traced here: 73.4 us
  starting transfers between devices  27.3 us (37%)
  waiting for transfers between devices  26 us (35%)
  Pallas kernels  19.8 us (27%)
    ppermute x12, starting transfers between devices, onward(): return lax.ppermute(x, 'col', ring)  19.8 us
    ppermute x12, waiting for transfers between devices, onward(): return lax.ppermute(x, 'col', ring)  19.3 us
    ppermute x7, starting transfers between devices, across(): return lax.ppermute(x, 'row', [(i, i ^ k) for i in range(8)])  4.57 us
    pallas_call x1, Pallas kernels, shards(): call(chunk_b, (wire, wide, shaped((16, 640), F32)), [VMEM] * 17, scratch=...  4.49 us
    pallas_call x1, Pallas kernels, shards(): call(decode, (shaped((EXTRA, 128)), few, few, few), [VMEM] * 3 + [SMEM, H...  4.14 us
    ppermute x7, waiting for transfers between devices, across(): return lax.ppermute(x, 'row', [(i, i ^ k) for i in range(8)])  3.92 us
    pallas_call x1, Pallas kernels, shards(): call(chunk_a, (wire, *parts, wide, wide), [VMEM] * 6, flops=COST_CA, nbyt...  3.64 us
    ppermute x1, starting transfers between devices, shards(): lax.ppermute(back, 'col', [(gray((p + 1) % 4), gray(p)) for p in range(4)])  2.91 us
  transfers between devices with their start and end apart: 20, of which 11 were waited for; matrix products, arithmetic and copies ran while one was open for 0% of the time, Pallas kernels for 24%

profile of v4, /device:TPU:0, one launch (start us, length us, event | category | flops | bytes accessed | tf_op | source)
XLA Modules:
  0.0 73.4 jit_solution(13846085629620081727)
XLA Ops:
  0.0 1.5 %pack.1 = (bf16[912,128]{1,0:T(8,128)(2,1)S(1)}, bf16[912,128]{1,0:T(8,128)(2,1)S(1)}, bf16[1792,128]{1,0:T(8,128)(2,1)S(1)}) custom-call(bf16[516,448]{1,0:T(8,128)(2,1)} %hidden.1, bf16[448]{0:T(512)(128)(2,1)} %gains.1, bf16[224,576]{1,0:T(8,128)(2,1)} %qkv.1, bf16[448,224]{1,0:T(8,128)(2,1)} %outs.1), custom_call_target="tpu_custom_call" | custom-call | bytes 300000 | tf_op jit(solution)/shard_map/pack/pallas_call | solution.py:402
  1.5 3.1 %collective-permute-start = (bf16[912,128]{1,0:T(8,128)(2,1)S(1)}, bf16[912,128]{1,0:T(8,128)(2,1)S(1)}, u32[]{:S(2)}, u32[]{:S(2)}) collective-permute-start(bf16[912,128]{1,0:T(8,128)(2,1)S(1)} %get-tuple-element.31.a0), channel_id=1, source_target_pairs={{0,1},{1,3},{3,2},{2,0},{4,5},{5,7},{7,6},{6,4},{8,9},{9,11},{11,1... | collective-permute-start | bytes 700424 | tf_op jit(solution)/shard_map/ppermute | solution.py:397
  4.6 2.6 %collective-permute-start.2 = (bf16[912,128]{1,0:T(8,128)(2,1)S(1)}, bf16[912,128]{1,0:T(8,128)(2,1)S(1)}, u32[]{:S(2)}, u32[]{:S(2)}) collective-permute-start(bf16[912,128]{1,0:T(8,128)(2,1)S(1)} %get-tuple-element.32.b0), channel_id=1, source_target_pairs={{0,1},{1,3},{3,2},{2,0},{4,5},{5,7},{7,6},{6,4},{8,9},{9,11},{11,1... | collective-permute-start | bytes 700424 | tf_op jit(solution)/shard_map/ppermute | solution.py:397
  7.2 1.5 %collective-permute-start.6 = (bf16[1792,128]{1,0:T(8,128)(2,1)S(1)}, bf16[1792,128]{1,0:T(8,128)(2,1)S(1)}, u32[]{:S(2)}, u32[]{:S(2)}) collective-permute-start(bf16[1792,128]{1,0:T(8,128)(2,1)S(1)} %get-tuple-element.36.refs_0_), channel_id=1, source_target_pairs={{0,16},{4,20},{8,24},{12,28},{16,0},{20,4},{24,8},{28,12},{1,17},{... | collective-permute-start | bytes 1376264 | tf_op jit(solution)/shard_map/ppermute | solution.py:400
  8.7 1.4 %collective-permute-start.7 = (bf16[1792,128]{1,0:T(8,128)(2,1)S(1)}, bf16[1792,128]{1,0:T(8,128)(2,1)S(1)}, u32[]{:S(2)}, u32[]{:S(2)}) collective-permute-start(bf16[1792,128]{1,0:T(8,128)(2,1)S(1)} %get-tuple-element.36.refs_0_), channel_id=1, source_target_pairs={{0,24},{4,28},{8,16},{12,20},{16,8},{20,12},{24,0},{28,4},{1,25},{... | collective-permute-start | bytes 1376264 | tf_op jit(solution)/shard_map/ppermute | solution.py:400
  10.7 1.5 %collective-permute-done.a1 = bf16[912,128]{1,0:T(8,128)(2,1)S(1)} collective-permute-done((bf16[912,128]{1,0:T(8,128)(2,1)S(1)}, bf16[912,128]{1,0:T(8,128)(2,1)S(1)}, u32[]{:S(2)}, u32[]{:S(2)}) %collective-permute-start) | collective-permute-done | bytes 233504 | tf_op jit(solution)/shard_map/ppermute | solution.py:397
  12.2 1.2 %collective-permute-start.1 = (bf16[912,128]{1,0:T(8,128)(2,1)S(1)}, bf16[912,128]{1,0:T(8,128)(2,1)S(1)}, u32[]{:S(2)}, u32[]{:S(2)}) collective-permute-start(bf16[912,128]{1,0:T(8,128)(2,1)S(1)} %collective-permute-done.a1), channel_id=1, source_target_pairs={{0,1},{1,3},{3,2},{2,0},{4,5},{5,7},{7,6},{6,4},{8,9},{9,11},{11,1... | collective-permute-start | bytes 700424 | tf_op jit(solution)/shard_map/ppermute | solution.py:397
  13.3 3.8 %collective-permute-done.2.ref.b1 = bf16[912,128]{1,0:T(8,128)(2,1)S(1)} collective-permute-done((bf16[912,128]{1,0:T(8,128)(2,1)S(1)}, bf16[912,128]{1,0:T(8,128)(2,1)S(1)}, u32[]{:S(2)}, u32[]{:S(2)}) %collective-permute-start.2) | collective-permute-done | bytes 233504 | tf_op jit(solution)/shard_map/ppermute | solution.py:397
  17.2 1.2 %collective-permute-start.4 = (bf16[912,128]{1,0:T(8,128)(2,1)S(1)}, bf16[912,128]{1,0:T(8,128)(2,1)S(1)}, u32[]{:S(2)}, u32[]{:S(2)}) collective-permute-start(bf16[912,128]{1,0:T(8,128)(2,1)S(1)} %collective-permute-done.2.ref.b1), channel_id=1, source_target_pairs={{0,1},{1,3},{3,2},{2,0},{4,5},{5,7},{7,6},{6,4},{8,9},{9,11},{11,1... | collective-permute-start | bytes 700424 | tf_op jit(solution)/shard_map/ppermute | solution.py:397
  18.4 3.8 %collective-permute-done.1.a2 = bf16[912,128]{1,0:T(8,128)(2,1)S(1)} collective-permute-done((bf16[912,128]{1,0:T(8,128)(2,1)S(1)}, bf16[912,128]{1,0:T(8,128)(2,1)S(1)}, u32[]{:S(2)}, u32[]{:S(2)}) %collective-permute-start.1) | collective-permute-done | bytes 233504 | tf_op jit(solution)/shard_map/ppermute | solution.py:397
  22.2 1.2 %collective-permute-start.3 = (bf16[912,128]{1,0:T(8,128)(2,1)S(1)}, bf16[912,128]{1,0:T(8,128)(2,1)S(1)}, u32[]{:S(2)}, u32[]{:S(2)}) collective-permute-start(bf16[912,128]{1,0:T(8,128)(2,1)S(1)} %collective-permute-done.1.a2), channel_id=1, source_target_pairs={{0,1},{1,3},{3,2},{2,0},{4,5},{5,7},{7,6},{6,4},{8,9},{9,11},{11,1... | collective-permute-start | bytes 700424 | tf_op jit(solution)/shard_map/ppermute | solution.py:397
  23.3 2.2 %prepare_cache.1 = (bf16[1024,512]{1,0:T(8,128)(2,1)S(1)}, bf16[1024,512]{1,0:T(8,128)(2,1)S(1)}) custom-call(bf16[5,1024,512]{2,1,0:T(8,128)(2,1)} %cache.3, s32[5]{0:T(128)S(1)} %copy-done), custom_call_target="tpu_custom_call" | custom-call | bytes 300000 | tf_op jit(solution)/shard_map/prepare_cache/pallas_call | solution.py:432
  25.5 3.2 %collective-permute-done.6.refs_4_ = bf16[1792,128]{1,0:T(8,128)(2,1)S(1)} collective-permute-done((bf16[1792,128]{1,0:T(8,128)(2,1)S(1)}, bf16[1792,128]{1,0:T(8,128)(2,1)S(1)}, u32[]{:S(2)}, u32[]{:S(2)}) %collective-permute-start.6) | collective-permute-done | bytes 458784 | tf_op jit(solution)/shard_map/ppermute | solution.py:400
  34.0 3.6 %chunk_a.1 = (bf16[896,128]{1,0:T(8,128)(2,1)S(1)}, f32[896,128]{1,0:T(8,128)S(1)}, f32[896,128]{1,0:T(8,128)S(1)}, f32[896,128]{1,0:T(8,128)S(1)}, bf16[256,512...) custom-call(bf16[256,2048]{1,0:T(8,128)(2,1)S(1)} %norm_a.1.normed, bf16[4,512,640]{2,1,0:T(8,128)(2,1)S(1)} %get-tuple-element.37.w_ref, ...), custom_call_target="tpu_custom_call" | custom-call | flops 100000000 | bytes 300000 | tf_op jit(solution)/shard_map/chunk_a/pallas_call | solution.py:444
  37.6 3.4 %collective-permute-start.12 = (bf16[896,128]{1,0:T(8,128)(2,1)S(1)}, bf16[896,128]{1,0:T(8,128)(2,1)S(1)}, u32[]{:S(2)}, u32[]{:S(2)}) collective-permute-start(bf16[896,128]{1,0:T(8,128)(2,1)S(1)} %get-tuple-element.41), channel_id=1, source_target_pairs={{0,1},{1,3},{3,2},{2,0},{4,5},{5,7},{7,6},{6,4},{8,9},{9,11},{11,1... | collective-permute-start | bytes 688136 | tf_op jit(solution)/shard_map/ppermute | solution.py:397
  41.0 4.5 %chunk_b.1 = (bf16[896,128]{1,0:T(8,128)(2,1)S(1)}, bf16[256,512]{1,0:T(8,128)(2,1)S(1)}, f32[16,640]{1,0:T(8,128)S(1)}) custom-call(bf16[912,128]{1,0:T(8,128)(2,1)S(1)} %get-tuple-element.32.b0, bf16[912,128]{1,0:T(8,128)(2,1)S(1)} %collective-permute-done.2.ref.b1, bf16[912,128]{1,0:T(8,128)(2,1)S(1)} %collective-permute-done.4.ref.b2, ...), custom_call_target="tpu_custom_call" | custom-call | flops 1000000000 | bytes 300000 | tf_op jit(solution)/shard_map/chunk_b/pallas_call | solution.py:454
  45.6 4.1 %decode.1 = (bf16[16,128]{1,0:T(8,128)(2,1)S(1)}, f32[16,128]{1,0:T(8,128)S(1)}, f32[16,128]{1,0:T(8,128)S(1)}, f32[16,128]{1,0:T(8,128)S(1)}) custom-call(f32[16,640]{1,0:T(8,128)S(1)} %get-tuple-element.45.late_ref, bf16[4,512,512]{2,1,0:T(8,128)(2,1)S(1)} %get-tuple-element.38.o_ref, f32[516,128]{1,0:T(8,128)S(1)} %broadcast_in_dim.2.m_ref, ...), custom_call_target="tpu_custom_call" | custom-call | flops 1000000 | bytes 300000 | tf_op jit(solution)/shard_map/decode/pallas_call | solution.py:475
  49.8 2.0 %collective-permute-start.14 = (bf16[912,128]{1,0:T(8,128)(2,1)S(1)}, bf16[912,128]{1,0:T(8,128)(2,1)S(1)}, u32[]{:S(2)}, u32[]{:S(2)}) collective-permute-start(bf16[912,128]{1,0:T(8,128)(2,1)S(1)} %join_1.1), channel_id=1, source_target_pairs={{0,1},{1,3},{3,2},{2,0},{4,5},{5,7},{7,6},{6,4},{8,9},{9,11},{11,1... | collective-permute-start | bytes 700424 | tf_op jit(solution)/shard_map/ppermute | solution.py:397
  51.8 1.8 %collective-permute-done.17.recv = bf16[896,128]{1,0:T(8,128)(2,1)S(1)} collective-permute-done((bf16[896,128]{1,0:T(8,128)(2,1)S(1)}, bf16[896,128]{1,0:T(8,128)(2,1)S(1)}, u32[]{:S(2)}, u32[]{:S(2)}) %collective-permute-start.17) | collective-permute-done | bytes 229408 | tf_op jit(solution)/shard_map/ppermute | solution.py:397
  54.0 2.9 %collective-permute-start.15 = (bf16[16,128]{1,0:T(8,128)(2,1)S(1)}, bf16[16,128]{1,0:T(8,128)(2,1)S(1)}, u32[]{:S(2)}, u32[]{:S(2)}) collective-permute-start(bf16[16,128]{1,0:T(8,128)(2,1)S(1)} %get-tuple-element.47), channel_id=1, source_target_pairs={{1,0},{3,1},{2,3},{0,2},{5,4},{7,5},{6,7},{4,6},{9,8},{11,9},{10,1... | collective-permute-start | bytes 12296 | tf_op jit(solution)/shard_map/ppermute | solution.py:491
  56.9 2.8 %collective-permute-done.15.back = bf16[16,128]{1,0:T(8,128)(2,1)S(1)} collective-permute-done((bf16[16,128]{1,0:T(8,128)(2,1)S(1)}, bf16[16,128]{1,0:T(8,128)(2,1)S(1)}, u32[]{:S(2)}, u32[]{:S(2)}) %collective-permute-start.15) | collective-permute-done | bytes 4128 | tf_op jit(solution)/shard_map/ppermute | solution.py:491
  59.7 4.2 %collective-permute-start.16 = (bf16[912,128]{1,0:T(8,128)(2,1)S(1)}, bf16[912,128]{1,0:T(8,128)(2,1)S(1)}, u32[]{:S(2)}, u32[]{:S(2)}) collective-permute-start(bf16[912,128]{1,0:T(8,128)(2,1)S(1)} %join_2.1), channel_id=1, source_target_pairs={{0,1},{1,3},{3,2},{2,0},{4,5},{5,7},{7,6},{6,4},{8,9},{9,11},{11,1... | collective-permute-start | bytes 700424 | tf_op jit(solution)/shard_map/ppermute | solution.py:397
  65.2 4.7 %collective-permute-done.16.recv = bf16[912,128]{1,0:T(8,128)(2,1)S(1)} collective-permute-done((bf16[912,128]{1,0:T(8,128)(2,1)S(1)}, bf16[912,128]{1,0:T(8,128)(2,1)S(1)}, u32[]{:S(2)}, u32[]{:S(2)}) %collective-permute-start.16) | collective-permute-done | bytes 233504 | tf_op jit(solution)/shard_map/ppermute | solution.py:397
  70.0 2.5 %collective-permute-done.19.recv = bf16[896,128]{1,0:T(8,128)(2,1)S(1)} collective-permute-done((bf16[896,128]{1,0:T(8,128)(2,1)S(1)}, bf16[896,128]{1,0:T(8,128)(2,1)S(1)}, u32[]{:S(2)}, u32[]{:S(2)}) %collective-permute-start.19) | collective-permute-done | bytes 229408 | tf_op jit(solution)/shard_map/ppermute | solution.py:397
  (38 shorter events, 8.5 us)
Async XLA Ops:
  0.0 23.3 %copy-start.1 = (s32[516]{0:T(1024)S(1)}, s32[516]{0:T(1024)}, u32[]{:S(2)}) copy-start(s32[516]{0:T(1024)} %param.13) | copy-start | bytes 6196
  0.0 23.3 %copy-start = (s32[5]{0:T(128)S(1)}, s32[5]{0:T(128)}, u32[]{:S(2)}) copy-start(s32[5]{0:T(128)} %len_ref.3) | copy-start | bytes 64
  1.5 10.6 %collective-permute-start = (bf16[912,128]{1,0:T(8,128)(2,1)S(1)}, bf16[912,128]{1,0:T(8,128)(2,1)S(1)}, u32[]{:S(2)}, u32[]{:S(2)}) collective-permute-start(bf16[912,128]{1,0:T(8,128)(2,1)S(1)} %get-tuple-element.31.a0), channel_id=1, source_target_pairs={{0,1},{1,3},{3,2},{2,0},{4,5},{5,7},{7,6},{6,4},{8,9},{9,11},{11,1... | collective-permute-start | bytes 700424 | tf_op jit(solution)/shard_map/ppermute | solution.py:397
  4.6 12.5 %collective-permute-start.2 = (bf16[912,128]{1,0:T(8,128)(2,1)S(1)}, bf16[912,128]{1,0:T(8,128)(2,1)S(1)}, u32[]{:S(2)}, u32[]{:S(2)}) collective-permute-start(bf16[912,128]{1,0:T(8,128)(2,1)S(1)} %get-tuple-element.32.b0), channel_id=1, source_target_pairs={{0,1},{1,3},{3,2},{2,0},{4,5},{5,7},{7,6},{6,4},{8,9},{9,11},{11,1... | collective-permute-start | bytes 700424 | tf_op jit(solution)/shard_map/ppermute | solution.py:397
  7.2 21.5 %collective-permute-start.6 = (bf16[1792,128]{1,0:T(8,128)(2,1)S(1)}, bf16[1792,128]{1,0:T(8,128)(2,1)S(1)}, u32[]{:S(2)}, u32[]{:S(2)}) collective-permute-start(bf16[1792,128]{1,0:T(8,128)(2,1)S(1)} %get-tuple-element.36.refs_0_), channel_id=1, source_target_pairs={{0,16},{4,20},{8,24},{12,28},{16,0},{20,4},{24,8},{28,12},{1,17},{... | collective-permute-start | bytes 1376264 | tf_op jit(solution)/shard_map/ppermute | solution.py:400
  8.7 20.0 %collective-permute-start.7 = (bf16[1792,128]{1,0:T(8,128)(2,1)S(1)}, bf16[1792,128]{1,0:T(8,128)(2,1)S(1)}, u32[]{:S(2)}, u32[]{:S(2)}) collective-permute-start(bf16[1792,128]{1,0:T(8,128)(2,1)S(1)} %get-tuple-element.36.refs_0_), channel_id=1, source_target_pairs={{0,24},{4,28},{8,16},{12,20},{16,8},{20,12},{24,0},{28,4},{1,25},{... | collective-permute-start | bytes 1376264 | tf_op jit(solution)/shard_map/ppermute | solution.py:400
  10.2 19.8 %collective-permute-start.5 = (bf16[1792,128]{1,0:T(8,128)(2,1)S(1)}, bf16[1792,128]{1,0:T(8,128)(2,1)S(1)}, u32[]{:S(2)}, u32[]{:S(2)}) collective-permute-start(bf16[1792,128]{1,0:T(8,128)(2,1)S(1)} %get-tuple-element.36.refs_0_), channel_id=1, source_target_pairs={{0,8},{4,12},{8,0},{12,4},{16,24},{20,28},{24,16},{28,20},{1,9},{5... | collective-permute-start | bytes 1376264 | tf_op jit(solution)/shard_map/ppermute | solution.py:400
  12.2 10.0 %collective-permute-start.1 = (bf16[912,128]{1,0:T(8,128)(2,1)S(1)}, bf16[912,128]{1,0:T(8,128)(2,1)S(1)}, u32[]{:S(2)}, u32[]{:S(2)}) collective-permute-start(bf16[912,128]{1,0:T(8,128)(2,1)S(1)} %collective-permute-done.a1), channel_id=1, source_target_pairs={{0,1},{1,3},{3,2},{2,0},{4,5},{5,7},{7,6},{6,4},{8,9},{9,11},{11,1... | collective-permute-start | bytes 700424 | tf_op jit(solution)/shard_map/ppermute | solution.py:397
  17.2 12.8 %collective-permute-start.4 = (bf16[912,128]{1,0:T(8,128)(2,1)S(1)}, bf16[912,128]{1,0:T(8,128)(2,1)S(1)}, u32[]{:S(2)}, u32[]{:S(2)}) collective-permute-start(bf16[912,128]{1,0:T(8,128)(2,1)S(1)} %collective-permute-done.2.ref.b1), channel_id=1, source_target_pairs={{0,1},{1,3},{3,2},{2,0},{4,5},{5,7},{7,6},{6,4},{8,9},{9,11},{11,1... | collective-permute-start | bytes 700424 | tf_op jit(solution)/shard_map/ppermute | solution.py:397
  22.2 9.2 %collective-permute-start.3 = (bf16[912,128]{1,0:T(8,128)(2,1)S(1)}, bf16[912,128]{1,0:T(8,128)(2,1)S(1)}, u32[]{:S(2)}, u32[]{:S(2)}) collective-permute-start(bf16[912,128]{1,0:T(8,128)(2,1)S(1)} %collective-permute-done.1.a2), channel_id=1, source_target_pairs={{0,1},{1,3},{3,2},{2,0},{4,5},{5,7},{7,6},{6,4},{8,9},{9,11},{11,1... | collective-permute-start | bytes 700424 | tf_op jit(solution)/shard_map/ppermute | solution.py:397
  28.7 3.9 %collective-permute-start.10 = (bf16[1792,128]{1,0:T(8,128)(2,1)S(1)}, bf16[1792,128]{1,0:T(8,128)(2,1)S(1)}, u32[]{:S(2)}, u32[]{:S(2)}) collective-permute-start(bf16[1792,128]{1,0:T(8,128)(2,1)S(1)} %collective-permute-done.6.refs_4_), channel_id=1, source_target_pairs={{0,4},{4,0},{8,12},{12,8},{16,20},{20,16},{24,28},{28,24},{1,5},{5... | collective-permute-start | bytes 1376264 | tf_op jit(solution)/shard_map/ppermute | solution.py:400
  28.7 3.9 %collective-permute-start.11 = (bf16[1792,128]{1,0:T(8,128)(2,1)S(1)}, bf16[1792,128]{1,0:T(8,128)(2,1)S(1)}, u32[]{:S(2)}, u32[]{:S(2)}) collective-permute-start(bf16[1792,128]{1,0:T(8,128)(2,1)S(1)} %collective-permute-done.7.refs_6_), channel_id=1, source_target_pairs={{0,4},{4,0},{8,12},{12,8},{16,20},{20,16},{24,28},{28,24},{1,5},{5... | collective-permute-start | bytes 1376264 | tf_op jit(solution)/shard_map/ppermute | solution.py:400
  30.0 2.7 %collective-permute-start.9 = (bf16[1792,128]{1,0:T(8,128)(2,1)S(1)}, bf16[1792,128]{1,0:T(8,128)(2,1)S(1)}, u32[]{:S(2)}, u32[]{:S(2)}) collective-permute-start(bf16[1792,128]{1,0:T(8,128)(2,1)S(1)} %collective-permute-done.5.refs_2_), channel_id=1, source_target_pairs={{0,4},{4,0},{8,12},{12,8},{16,20},{20,16},{24,28},{28,24},{1,5},{5... | collective-permute-start | bytes 1376264 | tf_op jit(solution)/shard_map/ppermute | solution.py:400
  30.0 2.7 %collective-permute-start.8 = (bf16[1792,128]{1,0:T(8,128)(2,1)S(1)}, bf16[1792,128]{1,0:T(8,128)(2,1)S(1)}, u32[]{:S(2)}, u32[]{:S(2)}) collective-permute-start(bf16[1792,128]{1,0:T(8,128)(2,1)S(1)} %get-tuple-element.36.refs_0_), channel_id=1, source_target_pairs={{0,4},{4,0},{8,12},{12,8},{16,20},{20,16},{24,28},{28,24},{1,5},{5... | collective-permute-start | bytes 1376264 | tf_op jit(solution)/shard_map/ppermute | solution.py:400
  31.3 9.7 %collective-permute-start.13 = (bf16[912,128]{1,0:T(8,128)(2,1)S(1)}, bf16[912,128]{1,0:T(8,128)(2,1)S(1)}, u32[]{:S(2)}, u32[]{:S(2)}) collective-permute-start(bf16[912,128]{1,0:T(8,128)(2,1)S(1)} %collective-permute-done.4.ref.b2), channel_id=1, source_target_pairs={{0,1},{1,3},{3,2},{2,0},{4,5},{5,7},{7,6},{6,4},{8,9},{9,11},{11,1... | collective-permute-start | bytes 700424 | tf_op jit(solution)/shard_map/ppermute | solution.py:397
  37.6 12.2 %collective-permute-start.12 = (bf16[896,128]{1,0:T(8,128)(2,1)S(1)}, bf16[896,128]{1,0:T(8,128)(2,1)S(1)}, u32[]{:S(2)}, u32[]{:S(2)}) collective-permute-start(bf16[896,128]{1,0:T(8,128)(2,1)S(1)} %get-tuple-element.41), channel_id=1, source_target_pairs={{0,1},{1,3},{3,2},{2,0},{4,5},{5,7},{7,6},{6,4},{8,9},{9,11},{11,1... | collective-permute-start | bytes 688136 | tf_op jit(solution)/shard_map/ppermute | solution.py:397
  45.5 8.1 %collective-permute-start.17 = (bf16[896,128]{1,0:T(8,128)(2,1)S(1)}, bf16[896,128]{1,0:T(8,128)(2,1)S(1)}, u32[]{:S(2)}, u32[]{:S(2)}) collective-permute-start(bf16[896,128]{1,0:T(8,128)(2,1)S(1)} %get-tuple-element.56), channel_id=1, source_target_pairs={{0,1},{1,3},{3,2},{2,0},{4,5},{5,7},{7,6},{6,4},{8,9},{9,11},{11,1... | collective-permute-start | bytes 688136 | tf_op jit(solution)/shard_map/ppermute | solution.py:397
  49.8 9.8 %collective-permute-start.14 = (bf16[912,128]{1,0:T(8,128)(2,1)S(1)}, bf16[912,128]{1,0:T(8,128)(2,1)S(1)}, u32[]{:S(2)}, u32[]{:S(2)}) collective-permute-start(bf16[912,128]{1,0:T(8,128)(2,1)S(1)} %join_1.1), channel_id=1, source_target_pairs={{0,1},{1,3},{3,2},{2,0},{4,5},{5,7},{7,6},{6,4},{8,9},{9,11},{11,1... | collective-permute-start | bytes 700424 | tf_op jit(solution)/shard_map/ppermute | solution.py:397
  53.9 10.5 %collective-permute-start.18 = (bf16[896,128]{1,0:T(8,128)(2,1)S(1)}, bf16[896,128]{1,0:T(8,128)(2,1)S(1)}, u32[]{:S(2)}, u32[]{:S(2)}) collective-permute-start(bf16[896,128]{1,0:T(8,128)(2,1)S(1)} %hop_1.1), channel_id=1, source_target_pairs={{0,1},{1,3},{3,2},{2,0},{4,5},{5,7},{7,6},{6,4},{8,9},{9,11},{11,1... | collective-permute-start | bytes 688136 | tf_op jit(solution)/shard_map/ppermute | solution.py:397
  54.0 5.7 %collective-permute-start.15 = (bf16[16,128]{1,0:T(8,128)(2,1)S(1)}, bf16[16,128]{1,0:T(8,128)(2,1)S(1)}, u32[]{:S(2)}, u32[]{:S(2)}) collective-permute-start(bf16[16,128]{1,0:T(8,128)(2,1)S(1)} %get-tuple-element.47), channel_id=1, source_target_pairs={{1,0},{3,1},{2,3},{0,2},{5,4},{7,5},{6,7},{4,6},{9,8},{11,9},{10,1... | collective-permute-start | bytes 12296 | tf_op jit(solution)/shard_map/ppermute | solution.py:491
  59.7 10.1 %collective-permute-start.16 = (bf16[912,128]{1,0:T(8,128)(2,1)S(1)}, bf16[912,128]{1,0:T(8,128)(2,1)S(1)}, u32[]{:S(2)}, u32[]{:S(2)}) collective-permute-start(bf16[912,128]{1,0:T(8,128)(2,1)S(1)} %join_2.1), channel_id=1, source_target_pairs={{0,1},{1,3},{3,2},{2,0},{4,5},{5,7},{7,6},{6,4},{8,9},{9,11},{11,1... | collective-permute-start | bytes 700424 | tf_op jit(solution)/shard_map/ppermute | solution.py:397
  64.8 7.7 %collective-permute-start.19 = (bf16[896,128]{1,0:T(8,128)(2,1)S(1)}, bf16[896,128]{1,0:T(8,128)(2,1)S(1)}, u32[]{:S(2)}, u32[]{:S(2)}) collective-permute-start(bf16[896,128]{1,0:T(8,128)(2,1)S(1)} %hop_2.1), channel_id=1, source_target_pairs={{0,1},{1,3},{3,2},{2,0},{4,5},{5,7},{7,6},{6,4},{8,9},{9,11},{11,1... | collective-permute-start | bytes 688136 | tf_op jit(solution)/shard_map/ppermute | solution.py:397

commit v5 on v4

--- a/solution.py
+++ b/solution.py
@@ -26,7 +26,7 @@
 COST_SQ = 1_000_000_000
 COST_CA = 100_000_000
 COST_CB = 1_000_000_000
-COST_F = 1_000_000
+COST_F = 2_000_000_000
 COST_G = 10_000_000
 COST_D = 1_000_000
 COST_E = 1_000_000
@@ -240,12 +240,14 @@
             out[at, :] = tile.astype(out.dtype)
 
 
-def hop_1(att_ref, o_ref, recv, out):
+def hop_1(att_ref, o_ref, recv, late, out):
     emit(att_ref[...], o_ref, (out,), 1, recv)
-
-
-def hop_2(att_ref, o_ref, recv, out):
+    out[BODY:, :] = late[...].astype(BF16)
+
+
+def hop_2(att_ref, o_ref, recv, late, out):
     emit(att_ref[...], o_ref, (out,), 2, recv)
+    out[BODY:, :] = (recv[BODY:, :].astype(F32) + late[...]).astype(BF16)
 
 
 def hop_3(att_ref, o_ref, out):
@@ -351,14 +353,6 @@
         ).astype(out.dtype)
 
 
-def join(recv, part, new_ref, out):
-    out[:BODY, :] = (recv[:BODY, :].astype(F32) + part[...]).astype(BF16)
-    late = new_ref[...].astype(F32)
-    if recv.shape[0] > BODY:
-        late = late + recv[BODY:, :].astype(F32)
-    out[BODY:, :] = late.astype(BF16)
-
-
 def unpack_sum(recv, part, out, base):
     for t in range(3):
         at = slice(t * HALF, (t + 1) * HALF)
@@ -368,14 +362,14 @@
     out[base + HALF // 2 : base + HALF, 384:448] = tail[:, 64:128].astype(BF16)
 
 
-def finish_a(recv, part, back, own_late, out, late):
+def finish_a(recv, part, out):
     unpack_sum(recv, part, out, 0)
-    late[...] = recv[BODY:, :].astype(F32) + (back[...].astype(F32) + own_late[...])
-
-
-def finish(done, late, recv, part, out):
+
+
+def finish(done, recv, part, back, own_late, out):
     out[:HALF, :] = done[...]
     unpack_sum(recv, part, out, HALF)
+    late = recv[BODY:, :].astype(F32) + (back[...].astype(F32) + own_late[...])
     for t in range(4):
         width = 128 if t < 3 else 64
         rows = late[DEC * t : DEC * (t + 1), 0:width]
@@ -468,9 +462,6 @@
     send_b = onward(first)
     own_b = call(hop_3, parts[0], [VMEM] * 2, flops=COST_E, nbytes=300_000, name="hop_3")(att, o)
 
-    def hop(body, recv, name):
-        return onward(call(body, wire, [VMEM] * 3, nbytes=300_000, name=name)(att, o, recv))
-
     few = shaped((EXTRA, 128), F32)
     back, *late = call(
         decode,
@@ -490,23 +481,20 @@
 
     back = lax.ppermute(back, "col", [(gray((p + 1) % 4), gray(p)) for p in range(4)])
 
-    def joined(recv, part, new, name):
-        return call(join, shaped((BODY + EXTRA, 128)), [VMEM] * 3, nbytes=300_000, name=name)(recv, part, new)
-
-    send_a = onward(joined(send_a, rest_a[0], late[0], "join_1"))
-    send_b = hop(hop_1, send_b, "hop_1")
-    send_a = onward(joined(after(send_a, back), rest_a[1], late[1], "join_2"))
-    send_b = hop(hop_2, send_b, "hop_2")
+    def hop(body, recv, new, name):
+        return onward(
+            call(body, shaped((BODY + EXTRA, 128)), [VMEM] * 4, nbytes=300_000, name=name)(att, o, recv, new)
+        )
+
+    send_a = onward((send_a.astype(F32) + rest_a[0]).astype(BF16))
+    send_b = hop(hop_1, send_b, late[0], "hop_1")
+    send_a = onward((send_a.astype(F32) + rest_a[1]).astype(BF16))
+    send_b = hop(hop_2, send_b, late[1], "hop_2")
     done = call(
-        finish_a,
-        (shaped((HALF, hidden.shape[1])), few),
-        [VMEM] * 4,
-        flops=COST_F,
-        nbytes=300_000,
-        name="finish_a",
-    )(send_a, rest_a[2], back, late[2])
-    return call(finish, shaped(hidden.shape), [VMEM] * 4, flops=COST_G, nbytes=300_000, name="finish")(
-        *done, send_b, own_b
+        finish_a, shaped((HALF, hidden.shape[1])), [VMEM] * 2, flops=COST_F, nbytes=300_000, name="finish_a"
+    )(send_a, rest_a[2])
+    return call(finish, shaped(hidden.shape), [VMEM] * 5, flops=COST_G, nbytes=300_000, name="finish")(
+        done, send_b, own_b, back, late[2]
     )
 
 

time: 73.5 us -> 73.5 us (level)
  waiting for transfers between devices: 26 us -> 30.7 us
  starting transfers between devices: 27.3 us -> 22.9 us
    ppermute x12, waiting for transfers between devices: 19.3 us -> 26.8 us  [onward(): return lax.ppermute(x, 'col', ring)]
    ppermute x12, starting transfers between devices: 19.8 us -> 15.4 us  [onward(): return lax.ppermute(x, 'col', ring)]
    ppermute x1, waiting for transfers between devices: 2.77 us -> 0.01 us  [shards(): lax.ppermute(back, 'col', [(gray((p + 1) % 4), gray(p)) for p in range(4)])]
    pallas_call x6 -> x4, Pallas kernels: 1.71 us -> 1.61 us  [the longest x1 0.88 us: shards(): call(finish, shaped(hidden.shape), [VMEM] * 5, flops=COST_G, nbytes=30000...]
  transfers between devices with their start and end apart: 20 -> 20, of which waited for: 11 -> 12; matrix products, arithmetic and copies ran while one was open for 0% -> 0% of each run, Pallas kernels for 24% -> 23%
where the time goes in v5:
time: 73.5 us; the launch traced here: 73.3 us
  waiting for transfers between devices  30.7 us (42%)
  starting transfers between devices  22.9 us (31%)
  Pallas kernels  19.2 us (26%)
    ppermute x12, waiting for transfers between devices, onward(): return lax.ppermute(x, 'col', ring)  26.8 us
    ppermute x12, starting transfers between devices, onward(): return lax.ppermute(x, 'col', ring)  15.4 us
    ppermute x7, starting transfers between devices, across(): return lax.ppermute(x, 'row', [(i, i ^ k) for i in range(8)])  4.57 us
    pallas_call x1, Pallas kernels, shards(): call(chunk_b, (wire, wide, shaped((16, 640), F32)), [VMEM] * 17, scratch=...  4.49 us
    ppermute x7, waiting for transfers between devices, across(): return lax.ppermute(x, 'row', [(i, i ^ k) for i in range(8)])  3.92 us
    pallas_call x1, Pallas kernels, shards(): call(decode, (shaped((EXTRA, 128)), few, few, few), [VMEM] * 3 + [SMEM, H...  3.73 us
    pallas_call x1, Pallas kernels, shards(): call(chunk_a, (wire, *parts, wide, wide), [VMEM] * 6, flops=COST_CA, nbyt...  3.63 us
    ppermute x1, starting transfers between devices, shards(): lax.ppermute(back, 'col', [(gray((p + 1) % 4), gray(p)) for p in range(4)])  2.91 us
  transfers between devices with their start and end apart: 20, of which 12 were waited for; matrix products, arithmetic and copies ran while one was open for 0% of the time, Pallas kernels for 23%

profile of v5, /device:TPU:0, one launch (start us, length us, event | category | flops | bytes accessed | tf_op | source)
XLA Modules:
  0.0 73.3 jit_solution(7505899758916461404)
XLA Ops:
  0.0 1.5 %pack.1 = (bf16[912,128]{1,0:T(8,128)(2,1)S(1)}, bf16[912,128]{1,0:T(8,128)(2,1)S(1)}, bf16[1792,128]{1,0:T(8,128)(2,1)S(1)}) custom-call(bf16[516,448]{1,0:T(8,128)(2,1)} %hidden.1, bf16[448]{0:T(512)(128)(2,1)} %gains.1, bf16[224,576]{1,0:T(8,128)(2,1)} %qkv.1, bf16[448,224]{1,0:T(8,128)(2,1)} %outs.1), custom_call_target="tpu_custom_call" | custom-call | bytes 300000 | tf_op jit(solution)/shard_map/pack/pallas_call | solution.py:396
  1.5 3.1 %collective-permute-start = (bf16[912,128]{1,0:T(8,128)(2,1)S(1)}, bf16[912,128]{1,0:T(8,128)(2,1)S(1)}, u32[]{:S(2)}, u32[]{:S(2)}) collective-permute-start(bf16[912,128]{1,0:T(8,128)(2,1)S(1)} %get-tuple-element.28.a0), channel_id=1, source_target_pairs={{0,1},{1,3},{3,2},{2,0},{4,5},{5,7},{7,6},{6,4},{8,9},{9,11},{11,1... | collective-permute-start | bytes 700424 | tf_op jit(solution)/shard_map/ppermute | solution.py:391
  4.6 2.6 %collective-permute-start.2 = (bf16[912,128]{1,0:T(8,128)(2,1)S(1)}, bf16[912,128]{1,0:T(8,128)(2,1)S(1)}, u32[]{:S(2)}, u32[]{:S(2)}) collective-permute-start(bf16[912,128]{1,0:T(8,128)(2,1)S(1)} %get-tuple-element.29.b0), channel_id=1, source_target_pairs={{0,1},{1,3},{3,2},{2,0},{4,5},{5,7},{7,6},{6,4},{8,9},{9,11},{11,1... | collective-permute-start | bytes 700424 | tf_op jit(solution)/shard_map/ppermute | solution.py:391
  7.2 1.5 %collective-permute-start.6 = (bf16[1792,128]{1,0:T(8,128)(2,1)S(1)}, bf16[1792,128]{1,0:T(8,128)(2,1)S(1)}, u32[]{:S(2)}, u32[]{:S(2)}) collective-permute-start(bf16[1792,128]{1,0:T(8,128)(2,1)S(1)} %get-tuple-element.33.refs_0_), channel_id=1, source_target_pairs={{0,16},{4,20},{8,24},{12,28},{16,0},{20,4},{24,8},{28,12},{1,17},{... | collective-permute-start | bytes 1376264 | tf_op jit(solution)/shard_map/ppermute | solution.py:394
  8.7 1.4 %collective-permute-start.7 = (bf16[1792,128]{1,0:T(8,128)(2,1)S(1)}, bf16[1792,128]{1,0:T(8,128)(2,1)S(1)}, u32[]{:S(2)}, u32[]{:S(2)}) collective-permute-start(bf16[1792,128]{1,0:T(8,128)(2,1)S(1)} %get-tuple-element.33.refs_0_), channel_id=1, source_target_pairs={{0,24},{4,28},{8,16},{12,20},{16,8},{20,12},{24,0},{28,4},{1,25},{... | collective-permute-start | bytes 1376264 | tf_op jit(solution)/shard_map/ppermute | solution.py:394
  10.7 1.5 %collective-permute-done.a1 = bf16[912,128]{1,0:T(8,128)(2,1)S(1)} collective-permute-done((bf16[912,128]{1,0:T(8,128)(2,1)S(1)}, bf16[912,128]{1,0:T(8,128)(2,1)S(1)}, u32[]{:S(2)}, u32[]{:S(2)}) %collective-permute-start) | collective-permute-done | bytes 233504 | tf_op jit(solution)/shard_map/ppermute | solution.py:391
  12.2 1.2 %collective-permute-start.1 = (bf16[912,128]{1,0:T(8,128)(2,1)S(1)}, bf16[912,128]{1,0:T(8,128)(2,1)S(1)}, u32[]{:S(2)}, u32[]{:S(2)}) collective-permute-start(bf16[912,128]{1,0:T(8,128)(2,1)S(1)} %collective-permute-done.a1), channel_id=1, source_target_pairs={{0,1},{1,3},{3,2},{2,0},{4,5},{5,7},{7,6},{6,4},{8,9},{9,11},{11,1... | collective-permute-start | bytes 700424 | tf_op jit(solution)/shard_map/ppermute | solution.py:391
  13.3 3.8 %collective-permute-done.2.ref.b1 = bf16[912,128]{1,0:T(8,128)(2,1)S(1)} collective-permute-done((bf16[912,128]{1,0:T(8,128)(2,1)S(1)}, bf16[912,128]{1,0:T(8,128)(2,1)S(1)}, u32[]{:S(2)}, u32[]{:S(2)}) %collective-permute-start.2) | collective-permute-done | bytes 233504 | tf_op jit(solution)/shard_map/ppermute | solution.py:391
  17.2 1.2 %collective-permute-start.4 = (bf16[912,128]{1,0:T(8,128)(2,1)S(1)}, bf16[912,128]{1,0:T(8,128)(2,1)S(1)}, u32[]{:S(2)}, u32[]{:S(2)}) collective-permute-start(bf16[912,128]{1,0:T(8,128)(2,1)S(1)} %collective-permute-done.2.ref.b1), channel_id=1, source_target_pairs={{0,1},{1,3},{3,2},{2,0},{4,5},{5,7},{7,6},{6,4},{8,9},{9,11},{11,1... | collective-permute-start | bytes 700424 | tf_op jit(solution)/shard_map/ppermute | solution.py:391
  18.4 3.8 %collective-permute-done.1.a2 = bf16[912,128]{1,0:T(8,128)(2,1)S(1)} collective-permute-done((bf16[912,128]{1,0:T(8,128)(2,1)S(1)}, bf16[912,128]{1,0:T(8,128)(2,1)S(1)}, u32[]{:S(2)}, u32[]{:S(2)}) %collective-permute-start.1) | collective-permute-done | bytes 233504 | tf_op jit(solution)/shard_map/ppermute | solution.py:391
  22.2 1.2 %collective-permute-start.3 = (bf16[912,128]{1,0:T(8,128)(2,1)S(1)}, bf16[912,128]{1,0:T(8,128)(2,1)S(1)}, u32[]{:S(2)}, u32[]{:S(2)}) collective-permute-start(bf16[912,128]{1,0:T(8,128)(2,1)S(1)} %collective-permute-done.1.a2), channel_id=1, source_target_pairs={{0,1},{1,3},{3,2},{2,0},{4,5},{5,7},{7,6},{6,4},{8,9},{9,11},{11,1... | collective-permute-start | bytes 700424 | tf_op jit(solution)/shard_map/ppermute | solution.py:391
  23.3 2.2 %prepare_cache.1 = (bf16[1024,512]{1,0:T(8,128)(2,1)S(1)}, bf16[1024,512]{1,0:T(8,128)(2,1)S(1)}) custom-call(bf16[5,1024,512]{2,1,0:T(8,128)(2,1)} %cache.3, s32[5]{0:T(128)S(1)} %copy-done), custom_call_target="tpu_custom_call" | custom-call | bytes 300000 | tf_op jit(solution)/shard_map/prepare_cache/pallas_call | solution.py:426
  25.5 3.2 %collective-permute-done.6.refs_4_ = bf16[1792,128]{1,0:T(8,128)(2,1)S(1)} collective-permute-done((bf16[1792,128]{1,0:T(8,128)(2,1)S(1)}, bf16[1792,128]{1,0:T(8,128)(2,1)S(1)}, u32[]{:S(2)}, u32[]{:S(2)}) %collective-permute-start.6) | collective-permute-done | bytes 458784 | tf_op jit(solution)/shard_map/ppermute | solution.py:394
  34.0 3.6 %chunk_a.1 = (bf16[896,128]{1,0:T(8,128)(2,1)S(1)}, f32[896,128]{1,0:T(8,128)S(1)}, f32[896,128]{1,0:T(8,128)S(1)}, f32[896,128]{1,0:T(8,128)S(1)}, bf16[256,512...) custom-call(bf16[256,2048]{1,0:T(8,128)(2,1)S(1)} %norm_a.1.normed, bf16[4,512,640]{2,1,0:T(8,128)(2,1)S(1)} %get-tuple-element.34.w_ref, ...), custom_call_target="tpu_custom_call" | custom-call | flops 100000000 | bytes 300000 | tf_op jit(solution)/shard_map/chunk_a/pallas_call | solution.py:438
  37.6 3.4 %collective-permute-start.12 = (bf16[896,128]{1,0:T(8,128)(2,1)S(1)}, bf16[896,128]{1,0:T(8,128)(2,1)S(1)}, u32[]{:S(2)}, u32[]{:S(2)}) collective-permute-start(bf16[896,128]{1,0:T(8,128)(2,1)S(1)} %get-tuple-element.38), channel_id=1, source_target_pairs={{0,1},{1,3},{3,2},{2,0},{4,5},{5,7},{7,6},{6,4},{8,9},{9,11},{11,1... | collective-permute-start | bytes 688136 | tf_op jit(solution)/shard_map/ppermute | solution.py:391
  41.0 4.5 %chunk_b.1 = (bf16[896,128]{1,0:T(8,128)(2,1)S(1)}, bf16[256,512]{1,0:T(8,128)(2,1)S(1)}, f32[16,640]{1,0:T(8,128)S(1)}) custom-call(bf16[912,128]{1,0:T(8,128)(2,1)S(1)} %get-tuple-element.29.b0, bf16[912,128]{1,0:T(8,128)(2,1)S(1)} %collective-permute-done.2.ref.b1, bf16[912,128]{1,0:T(8,128)(2,1)S(1)} %collective-permute-done.4.ref.b2, ...), custom_call_target="tpu_custom_call" | custom-call | flops 1000000000 | bytes 300000 | tf_op jit(solution)/shard_map/chunk_b/pallas_call | solution.py:448
  46.1 1.8 %collective-permute-start.13 = (bf16[896,128]{1,0:T(8,128)(2,1)S(1)}, bf16[896,128]{1,0:T(8,128)(2,1)S(1)}, u32[]{:S(2)}, u32[]{:S(2)}) collective-permute-start(bf16[896,128]{1,0:T(8,128)(2,1)S(1)} %add_convert_fusion.1), channel_id=1, source_target_pairs={{0,1},{1,3},{3,2},{2,0},{4,5},{5,7},{7,6},{6,4},{8,9},{9,11},{11,1... | collective-permute-start | bytes 688136 | tf_op jit(solution)/shard_map/ppermute | solution.py:391
  47.9 3.7 %decode.1 = (bf16[16,128]{1,0:T(8,128)(2,1)S(1)}, f32[16,128]{1,0:T(8,128)S(1)}, f32[16,128]{1,0:T(8,128)S(1)}, f32[16,128]{1,0:T(8,128)S(1)}) custom-call(f32[16,640]{1,0:T(8,128)S(1)} %get-tuple-element.46.late_ref, bf16[4,512,512]{2,1,0:T(8,128)(2,1)S(1)} %get-tuple-element.35.o_ref, f32[516,128]{1,0:T(8,128)S(1)} %broadcast_in_dim.2.m_ref, ...), custom_call_target="tpu_custom_call" | custom-call | flops 1000000 | bytes 300000 | tf_op jit(solution)/shard_map/decode/pallas_call | solution.py:466
  51.6 3.4 %collective-permute-done.16.recv = bf16[896,128]{1,0:T(8,128)(2,1)S(1)} collective-permute-done((bf16[896,128]{1,0:T(8,128)(2,1)S(1)}, bf16[896,128]{1,0:T(8,128)(2,1)S(1)}, u32[]{:S(2)}, u32[]{:S(2)}) %collective-permute-start.16) | collective-permute-done | bytes 229408 | tf_op jit(solution)/shard_map/ppermute | solution.py:391
  55.4 4.5 %collective-permute-done.13 = bf16[896,128]{1,0:T(8,128)(2,1)S(1)} collective-permute-done((bf16[896,128]{1,0:T(8,128)(2,1)S(1)}, bf16[896,128]{1,0:T(8,128)(2,1)S(1)}, u32[]{:S(2)}, u32[]{:S(2)}) %collective-permute-start.13) | collective-permute-done | bytes 229408 | tf_op jit(solution)/shard_map/ppermute | solution.py:391
  60.1 4.9 %collective-permute-done.17.recv = bf16[912,128]{1,0:T(8,128)(2,1)S(1)} collective-permute-done((bf16[912,128]{1,0:T(8,128)(2,1)S(1)}, bf16[912,128]{1,0:T(8,128)(2,1)S(1)}, u32[]{:S(2)}, u32[]{:S(2)}) %collective-permute-start.17) | collective-permute-done | bytes 233504 | tf_op jit(solution)/shard_map/ppermute | solution.py:391
  65.4 2.9 %collective-permute-start.19 = (bf16[16,128]{1,0:T(8,128)(2,1)S(1)}, bf16[16,128]{1,0:T(8,128)(2,1)S(1)}, u32[]{:S(2)}, u32[]{:S(2)}) collective-permute-start(bf16[16,128]{1,0:T(8,128)(2,1)S(1)} %get-tuple-element.49), channel_id=1, source_target_pairs={{1,0},{3,1},{2,3},{0,2},{5,4},{7,5},{6,7},{4,6},{9,8},{11,9},{10,1... | collective-permute-start | bytes 12296 | tf_op jit(solution)/shard_map/ppermute | solution.py:482
  68.6 1.3 %collective-permute-done.14.recv = bf16[896,128]{1,0:T(8,128)(2,1)S(1)} collective-permute-done((bf16[896,128]{1,0:T(8,128)(2,1)S(1)}, bf16[896,128]{1,0:T(8,128)(2,1)S(1)}, u32[]{:S(2)}, u32[]{:S(2)}) %collective-permute-start.14) | collective-permute-done | bytes 229408 | tf_op jit(solution)/shard_map/ppermute | solution.py:391
  70.0 2.4 %collective-permute-done.18.recv = bf16[912,128]{1,0:T(8,128)(2,1)S(1)} collective-permute-done((bf16[912,128]{1,0:T(8,128)(2,1)S(1)}, bf16[912,128]{1,0:T(8,128)(2,1)S(1)}, u32[]{:S(2)}, u32[]{:S(2)}) %collective-permute-start.18) | collective-permute-done | bytes 233504 | tf_op jit(solution)/shard_map/ppermute | solution.py:391
  (38 shorter events, 8.5 us)
Async XLA Ops:
  0.0 23.3 %copy-start.1 = (s32[516]{0:T(1024)S(1)}, s32[516]{0:T(1024)}, u32[]{:S(2)}) copy-start(s32[516]{0:T(1024)} %param.13) | copy-start | bytes 6196
  0.0 23.3 %copy-start = (s32[5]{0:T(128)S(1)}, s32[5]{0:T(128)}, u32[]{:S(2)}) copy-start(s32[5]{0:T(128)} %len_ref.3) | copy-start | bytes 64
  1.5 10.6 %collective-permute-start = (bf16[912,128]{1,0:T(8,128)(2,1)S(1)}, bf16[912,128]{1,0:T(8,128)(2,1)S(1)}, u32[]{:S(2)}, u32[]{:S(2)}) collective-permute-start(bf16[912,128]{1,0:T(8,128)(2,1)S(1)} %get-tuple-element.28.a0), channel_id=1, source_target_pairs={{0,1},{1,3},{3,2},{2,0},{4,5},{5,7},{7,6},{6,4},{8,9},{9,11},{11,1... | collective-permute-start | bytes 700424 | tf_op jit(solution)/shard_map/ppermute | solution.py:391
  4.6 12.5 %collective-permute-start.2 = (bf16[912,128]{1,0:T(8,128)(2,1)S(1)}, bf16[912,128]{1,0:T(8,128)(2,1)S(1)}, u32[]{:S(2)}, u32[]{:S(2)}) collective-permute-start(bf16[912,128]{1,0:T(8,128)(2,1)S(1)} %get-tuple-element.29.b0), channel_id=1, source_target_pairs={{0,1},{1,3},{3,2},{2,0},{4,5},{5,7},{7,6},{6,4},{8,9},{9,11},{11,1... | collective-permute-start | bytes 700424 | tf_op jit(solution)/shard_map/ppermute | solution.py:391
  7.2 21.5 %collective-permute-start.6 = (bf16[1792,128]{1,0:T(8,128)(2,1)S(1)}, bf16[1792,128]{1,0:T(8,128)(2,1)S(1)}, u32[]{:S(2)}, u32[]{:S(2)}) collective-permute-start(bf16[1792,128]{1,0:T(8,128)(2,1)S(1)} %get-tuple-element.33.refs_0_), channel_id=1, source_target_pairs={{0,16},{4,20},{8,24},{12,28},{16,0},{20,4},{24,8},{28,12},{1,17},{... | collective-permute-start | bytes 1376264 | tf_op jit(solution)/shard_map/ppermute | solution.py:394
  8.7 20.0 %collective-permute-start.7 = (bf16[1792,128]{1,0:T(8,128)(2,1)S(1)}, bf16[1792,128]{1,0:T(8,128)(2,1)S(1)}, u32[]{:S(2)}, u32[]{:S(2)}) collective-permute-start(bf16[1792,128]{1,0:T(8,128)(2,1)S(1)} %get-tuple-element.33.refs_0_), channel_id=1, source_target_pairs={{0,24},{4,28},{8,16},{12,20},{16,8},{20,12},{24,0},{28,4},{1,25},{... | collective-permute-start | bytes 1376264 | tf_op jit(solution)/shard_map/ppermute | solution.py:394
  10.2 19.8 %collective-permute-start.5 = (bf16[1792,128]{1,0:T(8,128)(2,1)S(1)}, bf16[1792,128]{1,0:T(8,128)(2,1)S(1)}, u32[]{:S(2)}, u32[]{:S(2)}) collective-permute-start(bf16[1792,128]{1,0:T(8,128)(2,1)S(1)} %get-tuple-element.33.refs_0_), channel_id=1, source_target_pairs={{0,8},{4,12},{8,0},{12,4},{16,24},{20,28},{24,16},{28,20},{1,9},{5... | collective-permute-start | bytes 1376264 | tf_op jit(solution)/shard_map/ppermute | solution.py:394
  12.2 10.0 %collective-permute-start.1 = (bf16[912,128]{1,0:T(8,128)(2,1)S(1)}, bf16[912,128]{1,0:T(8,128)(2,1)S(1)}, u32[]{:S(2)}, u32[]{:S(2)}) collective-permute-start(bf16[912,128]{1,0:T(8,128)(2,1)S(1)} %collective-permute-done.a1), channel_id=1, source_target_pairs={{0,1},{1,3},{3,2},{2,0},{4,5},{5,7},{7,6},{6,4},{8,9},{9,11},{11,1... | collective-permute-start | bytes 700424 | tf_op jit(solution)/shard_map/ppermute | solution.py:391
  17.2 12.8 %collective-permute-start.4 = (bf16[912,128]{1,0:T(8,128)(2,1)S(1)}, bf16[912,128]{1,0:T(8,128)(2,1)S(1)}, u32[]{:S(2)}, u32[]{:S(2)}) collective-permute-start(bf16[912,128]{1,0:T(8,128)(2,1)S(1)} %collective-permute-done.2.ref.b1), channel_id=1, source_target_pairs={{0,1},{1,3},{3,2},{2,0},{4,5},{5,7},{7,6},{6,4},{8,9},{9,11},{11,1... | collective-permute-start | bytes 700424 | tf_op jit(solution)/shard_map/ppermute | solution.py:391
  22.2 9.2 %collective-permute-start.3 = (bf16[912,128]{1,0:T(8,128)(2,1)S(1)}, bf16[912,128]{1,0:T(8,128)(2,1)S(1)}, u32[]{:S(2)}, u32[]{:S(2)}) collective-permute-start(bf16[912,128]{1,0:T(8,128)(2,1)S(1)} %collective-permute-done.1.a2), channel_id=1, source_target_pairs={{0,1},{1,3},{3,2},{2,0},{4,5},{5,7},{7,6},{6,4},{8,9},{9,11},{11,1... | collective-permute-start | bytes 700424 | tf_op jit(solution)/shard_map/ppermute | solution.py:391
  28.7 3.9 %collective-permute-start.10 = (bf16[1792,128]{1,0:T(8,128)(2,1)S(1)}, bf16[1792,128]{1,0:T(8,128)(2,1)S(1)}, u32[]{:S(2)}, u32[]{:S(2)}) collective-permute-start(bf16[1792,128]{1,0:T(8,128)(2,1)S(1)} %collective-permute-done.6.refs_4_), channel_id=1, source_target_pairs={{0,4},{4,0},{8,12},{12,8},{16,20},{20,16},{24,28},{28,24},{1,5},{5... | collective-permute-start | bytes 1376264 | tf_op jit(solution)/shard_map/ppermute | solution.py:394
  28.7 3.9 %collective-permute-start.11 = (bf16[1792,128]{1,0:T(8,128)(2,1)S(1)}, bf16[1792,128]{1,0:T(8,128)(2,1)S(1)}, u32[]{:S(2)}, u32[]{:S(2)}) collective-permute-start(bf16[1792,128]{1,0:T(8,128)(2,1)S(1)} %collective-permute-done.7.refs_6_), channel_id=1, source_target_pairs={{0,4},{4,0},{8,12},{12,8},{16,20},{20,16},{24,28},{28,24},{1,5},{5... | collective-permute-start | bytes 1376264 | tf_op jit(solution)/shard_map/ppermute | solution.py:394
  30.0 2.7 %collective-permute-start.9 = (bf16[1792,128]{1,0:T(8,128)(2,1)S(1)}, bf16[1792,128]{1,0:T(8,128)(2,1)S(1)}, u32[]{:S(2)}, u32[]{:S(2)}) collective-permute-start(bf16[1792,128]{1,0:T(8,128)(2,1)S(1)} %collective-permute-done.5.refs_2_), channel_id=1, source_target_pairs={{0,4},{4,0},{8,12},{12,8},{16,20},{20,16},{24,28},{28,24},{1,5},{5... | collective-permute-start | bytes 1376264 | tf_op jit(solution)/shard_map/ppermute | solution.py:394
  30.0 2.7 %collective-permute-start.8 = (bf16[1792,128]{1,0:T(8,128)(2,1)S(1)}, bf16[1792,128]{1,0:T(8,128)(2,1)S(1)}, u32[]{:S(2)}, u32[]{:S(2)}) collective-permute-start(bf16[1792,128]{1,0:T(8,128)(2,1)S(1)} %get-tuple-element.33.refs_0_), channel_id=1, source_target_pairs={{0,4},{4,0},{8,12},{12,8},{16,20},{20,16},{24,28},{28,24},{1,5},{5... | collective-permute-start | bytes 1376264 | tf_op jit(solution)/shard_map/ppermute | solution.py:394
  31.3 9.7 %collective-permute-start.15 = (bf16[912,128]{1,0:T(8,128)(2,1)S(1)}, bf16[912,128]{1,0:T(8,128)(2,1)S(1)}, u32[]{:S(2)}, u32[]{:S(2)}) collective-permute-start(bf16[912,128]{1,0:T(8,128)(2,1)S(1)} %collective-permute-done.4.ref.b2), channel_id=1, source_target_pairs={{0,1},{1,3},{3,2},{2,0},{4,5},{5,7},{7,6},{6,4},{8,9},{9,11},{11,1... | collective-permute-start | bytes 700424 | tf_op jit(solution)/shard_map/ppermute | solution.py:391
  37.6 8.4 %collective-permute-start.12 = (bf16[896,128]{1,0:T(8,128)(2,1)S(1)}, bf16[896,128]{1,0:T(8,128)(2,1)S(1)}, u32[]{:S(2)}, u32[]{:S(2)}) collective-permute-start(bf16[896,128]{1,0:T(8,128)(2,1)S(1)} %get-tuple-element.38), channel_id=1, source_target_pairs={{0,1},{1,3},{3,2},{2,0},{4,5},{5,7},{7,6},{6,4},{8,9},{9,11},{11,1... | collective-permute-start | bytes 688136 | tf_op jit(solution)/shard_map/ppermute | solution.py:391
  45.5 9.5 %collective-permute-start.16 = (bf16[896,128]{1,0:T(8,128)(2,1)S(1)}, bf16[896,128]{1,0:T(8,128)(2,1)S(1)}, u32[]{:S(2)}, u32[]{:S(2)}) collective-permute-start(bf16[896,128]{1,0:T(8,128)(2,1)S(1)} %get-tuple-element.45), channel_id=1, source_target_pairs={{0,1},{1,3},{3,2},{2,0},{4,5},{5,7},{7,6},{6,4},{8,9},{9,11},{11,1... | collective-permute-start | bytes 688136 | tf_op jit(solution)/shard_map/ppermute | solution.py:391
  46.1 13.9 %collective-permute-start.13 = (bf16[896,128]{1,0:T(8,128)(2,1)S(1)}, bf16[896,128]{1,0:T(8,128)(2,1)S(1)}, u32[]{:S(2)}, u32[]{:S(2)}) collective-permute-start(bf16[896,128]{1,0:T(8,128)(2,1)S(1)} %add_convert_fusion.1), channel_id=1, source_target_pairs={{0,1},{1,3},{3,2},{2,0},{4,5},{5,7},{7,6},{6,4},{8,9},{9,11},{11,1... | collective-permute-start | bytes 688136 | tf_op jit(solution)/shard_map/ppermute | solution.py:391
  55.3 9.7 %collective-permute-start.17 = (bf16[912,128]{1,0:T(8,128)(2,1)S(1)}, bf16[912,128]{1,0:T(8,128)(2,1)S(1)}, u32[]{:S(2)}, u32[]{:S(2)}) collective-permute-start(bf16[912,128]{1,0:T(8,128)(2,1)S(1)} %hop_1.1), channel_id=1, source_target_pairs={{0,1},{1,3},{3,2},{2,0},{4,5},{5,7},{7,6},{6,4},{8,9},{9,11},{11,1... | collective-permute-start | bytes 700424 | tf_op jit(solution)/shard_map/ppermute | solution.py:391
  60.0 9.8 %collective-permute-start.14 = (bf16[896,128]{1,0:T(8,128)(2,1)S(1)}, bf16[896,128]{1,0:T(8,128)(2,1)S(1)}, u32[]{:S(2)}, u32[]{:S(2)}) collective-permute-start(bf16[896,128]{1,0:T(8,128)(2,1)S(1)} %add_convert_fusion), channel_id=1, source_target_pairs={{0,1},{1,3},{3,2},{2,0},{4,5},{5,7},{7,6},{6,4},{8,9},{9,11},{11,1... | collective-permute-start | bytes 688136 | tf_op jit(solution)/shard_map/ppermute | solution.py:391
  65.3 7.1 %collective-permute-start.18 = (bf16[912,128]{1,0:T(8,128)(2,1)S(1)}, bf16[912,128]{1,0:T(8,128)(2,1)S(1)}, u32[]{:S(2)}, u32[]{:S(2)}) collective-permute-start(bf16[912,128]{1,0:T(8,128)(2,1)S(1)} %hop_2.1), channel_id=1, source_target_pairs={{0,1},{1,3},{3,2},{2,0},{4,5},{5,7},{7,6},{6,4},{8,9},{9,11},{11,1... | collective-permute-start | bytes 700424 | tf_op jit(solution)/shard_map/ppermute | solution.py:391
  65.4 4.6 %collective-permute-start.19 = (bf16[16,128]{1,0:T(8,128)(2,1)S(1)}, bf16[16,128]{1,0:T(8,128)(2,1)S(1)}, u32[]{:S(2)}, u32[]{:S(2)}) collective-permute-start(bf16[16,128]{1,0:T(8,128)(2,1)S(1)} %get-tuple-element.49), channel_id=1, source_target_pairs={{1,0},{3,1},{2,3},{0,2},{5,4},{7,5},{6,7},{4,6},{9,8},{11,9},{10,1... | collective-permute-start | bytes 12296 | tf_op jit(solution)/shard_map/ppermute | solution.py:482

commit v6 on v5

--- a/solution.py
+++ b/solution.py
@@ -82,7 +82,7 @@
         low = h_ref[base : base + HALF // 2, 384:448]
         high = h_ref[base + HALF // 2 : base + HALF, 384:448]
         ref[TAIL:BODY, :] = jnp.concatenate([low, high], axis=1)
-        ref[BODY:, :] = jnp.zeros((EXTRA, 128), BF16)
+        ref[BODY:, :] = jnp.zeros((ref.shape[0] - BODY, 128), BF16)
     gain = g_ref[...].reshape(1, 448)
     for t in range(3):
         a_ref[BODY + t : BODY + t + 1, :] = gain[:, t * 128 : (t + 1) * 128]
@@ -395,7 +395,7 @@
 
     a, b, own = call(
         pack,
-        (shaped((BODY + EXTRA, 128)), shaped((BODY + EXTRA, 128)), shaped((WROWS, 128))),
+        (shaped((BODY + 8, 128)), shaped((BODY + EXTRA, 128)), shaped((WROWS, 128))),
         [HBM] * 4,
         scratch=[pltpu.VMEM(x.shape, BF16) for x in (hidden, norm_gain, qkv_weight, out_weight)]
         + [pltpu.SemaphoreType.DMA((4,))],

time: 73.5 us -> 73.3 us (level)
  no operation moved by 1% of the time
where the time goes in v6:
time: 73.3 us; the launch traced here: 73.2 us
  waiting for transfers between devices  30.3 us (41%)
  starting transfers between devices  22.8 us (31%)
  Pallas kernels  19.6 us (27%)
    ppermute x12, waiting for transfers between devices, onward(): return lax.ppermute(x, 'col', ring)  26.3 us
    ppermute x12, starting transfers between devices, onward(): return lax.ppermute(x, 'col', ring)  15.3 us
    ppermute x7, starting transfers between devices, across(): return lax.ppermute(x, 'row', [(i, i ^ k) for i in range(8)])  4.57 us
    pallas_call x1, Pallas kernels, shards(): call(chunk_b, (wire, wide, shaped((16, 640), F32)), [VMEM] * 17, scratch=...  4.47 us
    pallas_call x1, Pallas kernels, shards(): call(decode, (shaped((EXTRA, 128)), few, few, few), [VMEM] * 3 + [SMEM, H...  4.14 us
    ppermute x7, waiting for transfers between devices, across(): return lax.ppermute(x, 'row', [(i, i ^ k) for i in range(8)])  4.01 us
    pallas_call x1, Pallas kernels, shards(): call(chunk_a, (wire, *parts, wide, wide), [VMEM] * 6, flops=COST_CA, nbyt...  3.64 us
    ppermute x1, starting transfers between devices, shards(): lax.ppermute(back, 'col', [(gray((p + 1) % 4), gray(p)) for p in range(4)])  2.91 us
  transfers between devices with their start and end apart: 20, of which 12 were waited for; matrix products, arithmetic and copies ran while one was open for 0% of the time, Pallas kernels for 23%

profile of v6, /device:TPU:0, one launch (start us, length us, event | category | flops | bytes accessed | tf_op | source)
XLA Modules:
  0.0 73.2 jit_solution(3397150908688801373)
XLA Ops:
  0.0 1.5 %pack.1 = (bf16[904,128]{1,0:T(8,128)(2,1)S(1)}, bf16[912,128]{1,0:T(8,128)(2,1)S(1)}, bf16[1792,128]{1,0:T(8,128)(2,1)S(1)}) custom-call(bf16[516,448]{1,0:T(8,128)(2,1)} %hidden.1, bf16[448]{0:T(512)(128)(2,1)} %gains.1, bf16[224,576]{1,0:T(8,128)(2,1)} %qkv.1, bf16[448,224]{1,0:T(8,128)(2,1)} %outs.1), custom_call_target="tpu_custom_call" | custom-call | bytes 300000 | tf_op jit(solution)/shard_map/pack/pallas_call | solution.py:396
  1.5 3.1 %collective-permute-start = (bf16[904,128]{1,0:T(8,128)(2,1)S(1)}, bf16[904,128]{1,0:T(8,128)(2,1)S(1)}, u32[]{:S(2)}, u32[]{:S(2)}) collective-permute-start(bf16[904,128]{1,0:T(8,128)(2,1)S(1)} %get-tuple-element.28.a0), channel_id=1, source_target_pairs={{0,1},{1,3},{3,2},{2,0},{4,5},{5,7},{7,6},{6,4},{8,9},{9,11},{11,1... | collective-permute-start | bytes 694280 | tf_op jit(solution)/shard_map/ppermute | solution.py:391
  4.6 2.6 %collective-permute-start.2 = (bf16[912,128]{1,0:T(8,128)(2,1)S(1)}, bf16[912,128]{1,0:T(8,128)(2,1)S(1)}, u32[]{:S(2)}, u32[]{:S(2)}) collective-permute-start(bf16[912,128]{1,0:T(8,128)(2,1)S(1)} %get-tuple-element.29.b0), channel_id=1, source_target_pairs={{0,1},{1,3},{3,2},{2,0},{4,5},{5,7},{7,6},{6,4},{8,9},{9,11},{11,1... | collective-permute-start | bytes 700424 | tf_op jit(solution)/shard_map/ppermute | solution.py:391
  7.2 1.5 %collective-permute-start.6 = (bf16[1792,128]{1,0:T(8,128)(2,1)S(1)}, bf16[1792,128]{1,0:T(8,128)(2,1)S(1)}, u32[]{:S(2)}, u32[]{:S(2)}) collective-permute-start(bf16[1792,128]{1,0:T(8,128)(2,1)S(1)} %get-tuple-element.33.refs_0_), channel_id=1, source_target_pairs={{0,16},{4,20},{8,24},{12,28},{16,0},{20,4},{24,8},{28,12},{1,17},{... | collective-permute-start | bytes 1376264 | tf_op jit(solution)/shard_map/ppermute | solution.py:394
  8.7 1.4 %collective-permute-start.7 = (bf16[1792,128]{1,0:T(8,128)(2,1)S(1)}, bf16[1792,128]{1,0:T(8,128)(2,1)S(1)}, u32[]{:S(2)}, u32[]{:S(2)}) collective-permute-start(bf16[1792,128]{1,0:T(8,128)(2,1)S(1)} %get-tuple-element.33.refs_0_), channel_id=1, source_target_pairs={{0,24},{4,28},{8,16},{12,20},{16,8},{20,12},{24,0},{28,4},{1,25},{... | collective-permute-start | bytes 1376264 | tf_op jit(solution)/shard_map/ppermute | solution.py:394
  10.7 1.4 %collective-permute-done.a1 = bf16[904,128]{1,0:T(8,128)(2,1)S(1)} collective-permute-done((bf16[904,128]{1,0:T(8,128)(2,1)S(1)}, bf16[904,128]{1,0:T(8,128)(2,1)S(1)}, u32[]{:S(2)}, u32[]{:S(2)}) %collective-permute-start) | collective-permute-done | bytes 231456 | tf_op jit(solution)/shard_map/ppermute | solution.py:391
  12.1 1.2 %collective-permute-start.1 = (bf16[904,128]{1,0:T(8,128)(2,1)S(1)}, bf16[904,128]{1,0:T(8,128)(2,1)S(1)}, u32[]{:S(2)}, u32[]{:S(2)}) collective-permute-start(bf16[904,128]{1,0:T(8,128)(2,1)S(1)} %collective-permute-done.a1), channel_id=1, source_target_pairs={{0,1},{1,3},{3,2},{2,0},{4,5},{5,7},{7,6},{6,4},{8,9},{9,11},{11,1... | collective-permute-start | bytes 694280 | tf_op jit(solution)/shard_map/ppermute | solution.py:391
  13.3 3.8 %collective-permute-done.2.ref.b1 = bf16[912,128]{1,0:T(8,128)(2,1)S(1)} collective-permute-done((bf16[912,128]{1,0:T(8,128)(2,1)S(1)}, bf16[912,128]{1,0:T(8,128)(2,1)S(1)}, u32[]{:S(2)}, u32[]{:S(2)}) %collective-permute-start.2) | collective-permute-done | bytes 233504 | tf_op jit(solution)/shard_map/ppermute | solution.py:391
  17.1 1.2 %collective-permute-start.4 = (bf16[912,128]{1,0:T(8,128)(2,1)S(1)}, bf16[912,128]{1,0:T(8,128)(2,1)S(1)}, u32[]{:S(2)}, u32[]{:S(2)}) collective-permute-start(bf16[912,128]{1,0:T(8,128)(2,1)S(1)} %collective-permute-done.2.ref.b1), channel_id=1, source_target_pairs={{0,1},{1,3},{3,2},{2,0},{4,5},{5,7},{7,6},{6,4},{8,9},{9,11},{11,1... | collective-permute-start | bytes 700424 | tf_op jit(solution)/shard_map/ppermute | solution.py:391
  18.3 3.7 %collective-permute-done.1.a2 = bf16[904,128]{1,0:T(8,128)(2,1)S(1)} collective-permute-done((bf16[904,128]{1,0:T(8,128)(2,1)S(1)}, bf16[904,128]{1,0:T(8,128)(2,1)S(1)}, u32[]{:S(2)}, u32[]{:S(2)}) %collective-permute-start.1) | collective-permute-done | bytes 231456 | tf_op jit(solution)/shard_map/ppermute | solution.py:391
  22.1 1.2 %collective-permute-start.3 = (bf16[904,128]{1,0:T(8,128)(2,1)S(1)}, bf16[904,128]{1,0:T(8,128)(2,1)S(1)}, u32[]{:S(2)}, u32[]{:S(2)}) collective-permute-start(bf16[904,128]{1,0:T(8,128)(2,1)S(1)} %collective-permute-done.1.a2), channel_id=1, source_target_pairs={{0,1},{1,3},{3,2},{2,0},{4,5},{5,7},{7,6},{6,4},{8,9},{9,11},{11,1... | collective-permute-start | bytes 694280 | tf_op jit(solution)/shard_map/ppermute | solution.py:391
  23.2 2.2 %prepare_cache.1 = (bf16[1024,512]{1,0:T(8,128)(2,1)S(1)}, bf16[1024,512]{1,0:T(8,128)(2,1)S(1)}) custom-call(bf16[5,1024,512]{2,1,0:T(8,128)(2,1)} %cache.3, s32[5]{0:T(128)S(1)} %copy-done), custom_call_target="tpu_custom_call" | custom-call | bytes 300000 | tf_op jit(solution)/shard_map/prepare_cache/pallas_call | solution.py:426
  25.5 3.3 %collective-permute-done.6.refs_4_ = bf16[1792,128]{1,0:T(8,128)(2,1)S(1)} collective-permute-done((bf16[1792,128]{1,0:T(8,128)(2,1)S(1)}, bf16[1792,128]{1,0:T(8,128)(2,1)S(1)}, u32[]{:S(2)}, u32[]{:S(2)}) %collective-permute-start.6) | collective-permute-done | bytes 458784 | tf_op jit(solution)/shard_map/ppermute | solution.py:394
  33.8 3.6 %chunk_a.1 = (bf16[896,128]{1,0:T(8,128)(2,1)S(1)}, f32[896,128]{1,0:T(8,128)S(1)}, f32[896,128]{1,0:T(8,128)S(1)}, f32[896,128]{1,0:T(8,128)S(1)}, bf16[256,512...) custom-call(bf16[256,2048]{1,0:T(8,128)(2,1)S(1)} %norm_a.1.normed, bf16[4,512,640]{2,1,0:T(8,128)(2,1)S(1)} %get-tuple-element.34.w_ref, ...), custom_call_target="tpu_custom_call" | custom-call | flops 100000000 | bytes 300000 | tf_op jit(solution)/shard_map/chunk_a/pallas_call | solution.py:438
  37.5 3.4 %collective-permute-start.12 = (bf16[896,128]{1,0:T(8,128)(2,1)S(1)}, bf16[896,128]{1,0:T(8,128)(2,1)S(1)}, u32[]{:S(2)}, u32[]{:S(2)}) collective-permute-start(bf16[896,128]{1,0:T(8,128)(2,1)S(1)} %get-tuple-element.38), channel_id=1, source_target_pairs={{0,1},{1,3},{3,2},{2,0},{4,5},{5,7},{7,6},{6,4},{8,9},{9,11},{11,1... | collective-permute-start | bytes 688136 | tf_op jit(solution)/shard_map/ppermute | solution.py:391
  40.9 4.5 %chunk_b.1 = (bf16[896,128]{1,0:T(8,128)(2,1)S(1)}, bf16[256,512]{1,0:T(8,128)(2,1)S(1)}, f32[16,640]{1,0:T(8,128)S(1)}) custom-call(bf16[912,128]{1,0:T(8,128)(2,1)S(1)} %get-tuple-element.29.b0, bf16[912,128]{1,0:T(8,128)(2,1)S(1)} %collective-permute-done.2.ref.b1, bf16[912,128]{1,0:T(8,128)(2,1)S(1)} %collective-permute-done.4.ref.b2, ...), custom_call_target="tpu_custom_call" | custom-call | flops 1000000000 | bytes 300000 | tf_op jit(solution)/shard_map/chunk_b/pallas_call | solution.py:448
  46.1 1.6 %collective-permute-start.13 = (bf16[896,128]{1,0:T(8,128)(2,1)S(1)}, bf16[896,128]{1,0:T(8,128)(2,1)S(1)}, u32[]{:S(2)}, u32[]{:S(2)}) collective-permute-start(bf16[896,128]{1,0:T(8,128)(2,1)S(1)} %add_convert_fusion.1), channel_id=1, source_target_pairs={{0,1},{1,3},{3,2},{2,0},{4,5},{5,7},{7,6},{6,4},{8,9},{9,11},{11,1... | collective-permute-start | bytes 688136 | tf_op jit(solution)/shard_map/ppermute | solution.py:391
  47.7 4.1 %decode.1 = (bf16[16,128]{1,0:T(8,128)(2,1)S(1)}, f32[16,128]{1,0:T(8,128)S(1)}, f32[16,128]{1,0:T(8,128)S(1)}, f32[16,128]{1,0:T(8,128)S(1)}) custom-call(f32[16,640]{1,0:T(8,128)S(1)} %get-tuple-element.46.late_ref, bf16[4,512,512]{2,1,0:T(8,128)(2,1)S(1)} %get-tuple-element.35.o_ref, f32[516,128]{1,0:T(8,128)S(1)} %broadcast_in_dim.2.m_ref, ...), custom_call_target="tpu_custom_call" | custom-call | flops 1000000 | bytes 300000 | tf_op jit(solution)/shard_map/decode/pallas_call | solution.py:466
  51.9 3.0 %collective-permute-done.16.recv = bf16[896,128]{1,0:T(8,128)(2,1)S(1)} collective-permute-done((bf16[896,128]{1,0:T(8,128)(2,1)S(1)}, bf16[896,128]{1,0:T(8,128)(2,1)S(1)}, u32[]{:S(2)}, u32[]{:S(2)}) %collective-permute-start.16) | collective-permute-done | bytes 229408 | tf_op jit(solution)/shard_map/ppermute | solution.py:391
  55.3 4.5 %collective-permute-done.13 = bf16[896,128]{1,0:T(8,128)(2,1)S(1)} collective-permute-done((bf16[896,128]{1,0:T(8,128)(2,1)S(1)}, bf16[896,128]{1,0:T(8,128)(2,1)S(1)}, u32[]{:S(2)}, u32[]{:S(2)}) %collective-permute-start.13) | collective-permute-done | bytes 229408 | tf_op jit(solution)/shard_map/ppermute | solution.py:391
  59.9 4.9 %collective-permute-done.17.recv = bf16[912,128]{1,0:T(8,128)(2,1)S(1)} collective-permute-done((bf16[912,128]{1,0:T(8,128)(2,1)S(1)}, bf16[912,128]{1,0:T(8,128)(2,1)S(1)}, u32[]{:S(2)}, u32[]{:S(2)}) %collective-permute-start.17) | collective-permute-done | bytes 233504 | tf_op jit(solution)/shard_map/ppermute | solution.py:391
  65.2 2.9 %collective-permute-start.19 = (bf16[16,128]{1,0:T(8,128)(2,1)S(1)}, bf16[16,128]{1,0:T(8,128)(2,1)S(1)}, u32[]{:S(2)}, u32[]{:S(2)}) collective-permute-start(bf16[16,128]{1,0:T(8,128)(2,1)S(1)} %get-tuple-element.49), channel_id=1, source_target_pairs={{1,0},{3,1},{2,3},{0,2},{5,4},{7,5},{6,7},{4,6},{9,8},{11,9},{10,1... | collective-permute-start | bytes 12296 | tf_op jit(solution)/shard_map/ppermute | solution.py:482
  68.4 1.3 %collective-permute-done.14.recv = bf16[896,128]{1,0:T(8,128)(2,1)S(1)} collective-permute-done((bf16[896,128]{1,0:T(8,128)(2,1)S(1)}, bf16[896,128]{1,0:T(8,128)(2,1)S(1)}, u32[]{:S(2)}, u32[]{:S(2)}) %collective-permute-start.14) | collective-permute-done | bytes 229408 | tf_op jit(solution)/shard_map/ppermute | solution.py:391
  69.8 2.4 %collective-permute-done.18.recv = bf16[912,128]{1,0:T(8,128)(2,1)S(1)} collective-permute-done((bf16[912,128]{1,0:T(8,128)(2,1)S(1)}, bf16[912,128]{1,0:T(8,128)(2,1)S(1)}, u32[]{:S(2)}, u32[]{:S(2)}) %collective-permute-start.18) | collective-permute-done | bytes 233504 | tf_op jit(solution)/shard_map/ppermute | solution.py:391
  (38 shorter events, 8.5 us)
Async XLA Ops:
  0.0 23.2 %copy-start.1 = (s32[516]{0:T(1024)S(1)}, s32[516]{0:T(1024)}, u32[]{:S(2)}) copy-start(s32[516]{0:T(1024)} %param.13) | copy-start | bytes 6196
  0.0 23.2 %copy-start = (s32[5]{0:T(128)S(1)}, s32[5]{0:T(128)}, u32[]{:S(2)}) copy-start(s32[5]{0:T(128)} %len_ref.3) | copy-start | bytes 64
  1.5 10.6 %collective-permute-start = (bf16[904,128]{1,0:T(8,128)(2,1)S(1)}, bf16[904,128]{1,0:T(8,128)(2,1)S(1)}, u32[]{:S(2)}, u32[]{:S(2)}) collective-permute-start(bf16[904,128]{1,0:T(8,128)(2,1)S(1)} %get-tuple-element.28.a0), channel_id=1, source_target_pairs={{0,1},{1,3},{3,2},{2,0},{4,5},{5,7},{7,6},{6,4},{8,9},{9,11},{11,1... | collective-permute-start | bytes 694280 | tf_op jit(solution)/shard_map/ppermute | solution.py:391
  4.6 12.5 %collective-permute-start.2 = (bf16[912,128]{1,0:T(8,128)(2,1)S(1)}, bf16[912,128]{1,0:T(8,128)(2,1)S(1)}, u32[]{:S(2)}, u32[]{:S(2)}) collective-permute-start(bf16[912,128]{1,0:T(8,128)(2,1)S(1)} %get-tuple-element.29.b0), channel_id=1, source_target_pairs={{0,1},{1,3},{3,2},{2,0},{4,5},{5,7},{7,6},{6,4},{8,9},{9,11},{11,1... | collective-permute-start | bytes 700424 | tf_op jit(solution)/shard_map/ppermute | solution.py:391
  7.2 21.5 %collective-permute-start.6 = (bf16[1792,128]{1,0:T(8,128)(2,1)S(1)}, bf16[1792,128]{1,0:T(8,128)(2,1)S(1)}, u32[]{:S(2)}, u32[]{:S(2)}) collective-permute-start(bf16[1792,128]{1,0:T(8,128)(2,1)S(1)} %get-tuple-element.33.refs_0_), channel_id=1, source_target_pairs={{0,16},{4,20},{8,24},{12,28},{16,0},{20,4},{24,8},{28,12},{1,17},{... | collective-permute-start | bytes 1376264 | tf_op jit(solution)/shard_map/ppermute | solution.py:394
  8.7 20.0 %collective-permute-start.7 = (bf16[1792,128]{1,0:T(8,128)(2,1)S(1)}, bf16[1792,128]{1,0:T(8,128)(2,1)S(1)}, u32[]{:S(2)}, u32[]{:S(2)}) collective-permute-start(bf16[1792,128]{1,0:T(8,128)(2,1)S(1)} %get-tuple-element.33.refs_0_), channel_id=1, source_target_pairs={{0,24},{4,28},{8,16},{12,20},{16,8},{20,12},{24,0},{28,4},{1,25},{... | collective-permute-start | bytes 1376264 | tf_op jit(solution)/shard_map/ppermute | solution.py:394
  10.2 19.8 %collective-permute-start.5 = (bf16[1792,128]{1,0:T(8,128)(2,1)S(1)}, bf16[1792,128]{1,0:T(8,128)(2,1)S(1)}, u32[]{:S(2)}, u32[]{:S(2)}) collective-permute-start(bf16[1792,128]{1,0:T(8,128)(2,1)S(1)} %get-tuple-element.33.refs_0_), channel_id=1, source_target_pairs={{0,8},{4,12},{8,0},{12,4},{16,24},{20,28},{24,16},{28,20},{1,9},{5... | collective-permute-start | bytes 1376264 | tf_op jit(solution)/shard_map/ppermute | solution.py:394
  12.1 10.0 %collective-permute-start.1 = (bf16[904,128]{1,0:T(8,128)(2,1)S(1)}, bf16[904,128]{1,0:T(8,128)(2,1)S(1)}, u32[]{:S(2)}, u32[]{:S(2)}) collective-permute-start(bf16[904,128]{1,0:T(8,128)(2,1)S(1)} %collective-permute-done.a1), channel_id=1, source_target_pairs={{0,1},{1,3},{3,2},{2,0},{4,5},{5,7},{7,6},{6,4},{8,9},{9,11},{11,1... | collective-permute-start | bytes 694280 | tf_op jit(solution)/shard_map/ppermute | solution.py:391
  17.1 12.9 %collective-permute-start.4 = (bf16[912,128]{1,0:T(8,128)(2,1)S(1)}, bf16[912,128]{1,0:T(8,128)(2,1)S(1)}, u32[]{:S(2)}, u32[]{:S(2)}) collective-permute-start(bf16[912,128]{1,0:T(8,128)(2,1)S(1)} %collective-permute-done.2.ref.b1), channel_id=1, source_target_pairs={{0,1},{1,3},{3,2},{2,0},{4,5},{5,7},{7,6},{6,4},{8,9},{9,11},{11,1... | collective-permute-start | bytes 700424 | tf_op jit(solution)/shard_map/ppermute | solution.py:391
  22.1 9.1 %collective-permute-start.3 = (bf16[904,128]{1,0:T(8,128)(2,1)S(1)}, bf16[904,128]{1,0:T(8,128)(2,1)S(1)}, u32[]{:S(2)}, u32[]{:S(2)}) collective-permute-start(bf16[904,128]{1,0:T(8,128)(2,1)S(1)} %collective-permute-done.1.a2), channel_id=1, source_target_pairs={{0,1},{1,3},{3,2},{2,0},{4,5},{5,7},{7,6},{6,4},{8,9},{9,11},{11,1... | collective-permute-start | bytes 694280 | tf_op jit(solution)/shard_map/ppermute | solution.py:391
  28.7 3.8 %collective-permute-start.10 = (bf16[1792,128]{1,0:T(8,128)(2,1)S(1)}, bf16[1792,128]{1,0:T(8,128)(2,1)S(1)}, u32[]{:S(2)}, u32[]{:S(2)}) collective-permute-start(bf16[1792,128]{1,0:T(8,128)(2,1)S(1)} %collective-permute-done.6.refs_4_), channel_id=1, source_target_pairs={{0,4},{4,0},{8,12},{12,8},{16,20},{20,16},{24,28},{28,24},{1,5},{5... | collective-permute-start | bytes 1376264 | tf_op jit(solution)/shard_map/ppermute | solution.py:394
  28.7 3.8 %collective-permute-start.11 = (bf16[1792,128]{1,0:T(8,128)(2,1)S(1)}, bf16[1792,128]{1,0:T(8,128)(2,1)S(1)}, u32[]{:S(2)}, u32[]{:S(2)}) collective-permute-start(bf16[1792,128]{1,0:T(8,128)(2,1)S(1)} %collective-permute-done.7.refs_6_), channel_id=1, source_target_pairs={{0,4},{4,0},{8,12},{12,8},{16,20},{20,16},{24,28},{28,24},{1,5},{5... | collective-permute-start | bytes 1376264 | tf_op jit(solution)/shard_map/ppermute | solution.py:394
  30.0 2.6 %collective-permute-start.9 = (bf16[1792,128]{1,0:T(8,128)(2,1)S(1)}, bf16[1792,128]{1,0:T(8,128)(2,1)S(1)}, u32[]{:S(2)}, u32[]{:S(2)}) collective-permute-start(bf16[1792,128]{1,0:T(8,128)(2,1)S(1)} %collective-permute-done.5.refs_2_), channel_id=1, source_target_pairs={{0,4},{4,0},{8,12},{12,8},{16,20},{20,16},{24,28},{28,24},{1,5},{5... | collective-permute-start | bytes 1376264 | tf_op jit(solution)/shard_map/ppermute | solution.py:394
  30.0 2.5 %collective-permute-start.8 = (bf16[1792,128]{1,0:T(8,128)(2,1)S(1)}, bf16[1792,128]{1,0:T(8,128)(2,1)S(1)}, u32[]{:S(2)}, u32[]{:S(2)}) collective-permute-start(bf16[1792,128]{1,0:T(8,128)(2,1)S(1)} %get-tuple-element.33.refs_0_), channel_id=1, source_target_pairs={{0,4},{4,0},{8,12},{12,8},{16,20},{20,16},{24,28},{28,24},{1,5},{5... | collective-permute-start | bytes 1376264 | tf_op jit(solution)/shard_map/ppermute | solution.py:394
  31.2 9.7 %collective-permute-start.15 = (bf16[912,128]{1,0:T(8,128)(2,1)S(1)}, bf16[912,128]{1,0:T(8,128)(2,1)S(1)}, u32[]{:S(2)}, u32[]{:S(2)}) collective-permute-start(bf16[912,128]{1,0:T(8,128)(2,1)S(1)} %collective-permute-done.4.ref.b2), channel_id=1, source_target_pairs={{0,1},{1,3},{3,2},{2,0},{4,5},{5,7},{7,6},{6,4},{8,9},{9,11},{11,1... | collective-permute-start | bytes 700424 | tf_op jit(solution)/shard_map/ppermute | solution.py:391
  37.5 8.5 %collective-permute-start.12 = (bf16[896,128]{1,0:T(8,128)(2,1)S(1)}, bf16[896,128]{1,0:T(8,128)(2,1)S(1)}, u32[]{:S(2)}, u32[]{:S(2)}) collective-permute-start(bf16[896,128]{1,0:T(8,128)(2,1)S(1)} %get-tuple-element.38), channel_id=1, source_target_pairs={{0,1},{1,3},{3,2},{2,0},{4,5},{5,7},{7,6},{6,4},{8,9},{9,11},{11,1... | collective-permute-start | bytes 688136 | tf_op jit(solution)/shard_map/ppermute | solution.py:391
  45.4 9.5 %collective-permute-start.16 = (bf16[896,128]{1,0:T(8,128)(2,1)S(1)}, bf16[896,128]{1,0:T(8,128)(2,1)S(1)}, u32[]{:S(2)}, u32[]{:S(2)}) collective-permute-start(bf16[896,128]{1,0:T(8,128)(2,1)S(1)} %get-tuple-element.45), channel_id=1, source_target_pairs={{0,1},{1,3},{3,2},{2,0},{4,5},{5,7},{7,6},{6,4},{8,9},{9,11},{11,1... | collective-permute-start | bytes 688136 | tf_op jit(solution)/shard_map/ppermute | solution.py:391
  46.1 13.7 %collective-permute-start.13 = (bf16[896,128]{1,0:T(8,128)(2,1)S(1)}, bf16[896,128]{1,0:T(8,128)(2,1)S(1)}, u32[]{:S(2)}, u32[]{:S(2)}) collective-permute-start(bf16[896,128]{1,0:T(8,128)(2,1)S(1)} %add_convert_fusion.1), channel_id=1, source_target_pairs={{0,1},{1,3},{3,2},{2,0},{4,5},{5,7},{7,6},{6,4},{8,9},{9,11},{11,1... | collective-permute-start | bytes 688136 | tf_op jit(solution)/shard_map/ppermute | solution.py:391
  55.2 9.7 %collective-permute-start.17 = (bf16[912,128]{1,0:T(8,128)(2,1)S(1)}, bf16[912,128]{1,0:T(8,128)(2,1)S(1)}, u32[]{:S(2)}, u32[]{:S(2)}) collective-permute-start(bf16[912,128]{1,0:T(8,128)(2,1)S(1)} %hop_1.1), channel_id=1, source_target_pairs={{0,1},{1,3},{3,2},{2,0},{4,5},{5,7},{7,6},{6,4},{8,9},{9,11},{11,1... | collective-permute-start | bytes 700424 | tf_op jit(solution)/shard_map/ppermute | solution.py:391
  59.9 9.8 %collective-permute-start.14 = (bf16[896,128]{1,0:T(8,128)(2,1)S(1)}, bf16[896,128]{1,0:T(8,128)(2,1)S(1)}, u32[]{:S(2)}, u32[]{:S(2)}) collective-permute-start(bf16[896,128]{1,0:T(8,128)(2,1)S(1)} %add_convert_fusion), channel_id=1, source_target_pairs={{0,1},{1,3},{3,2},{2,0},{4,5},{5,7},{7,6},{6,4},{8,9},{9,11},{11,1... | collective-permute-start | bytes 688136 | tf_op jit(solution)/shard_map/ppermute | solution.py:391
  65.2 7.1 %collective-permute-start.18 = (bf16[912,128]{1,0:T(8,128)(2,1)S(1)}, bf16[912,128]{1,0:T(8,128)(2,1)S(1)}, u32[]{:S(2)}, u32[]{:S(2)}) collective-permute-start(bf16[912,128]{1,0:T(8,128)(2,1)S(1)} %hop_2.1), channel_id=1, source_target_pairs={{0,1},{1,3},{3,2},{2,0},{4,5},{5,7},{7,6},{6,4},{8,9},{9,11},{11,1... | collective-permute-start | bytes 700424 | tf_op jit(solution)/shard_map/ppermute | solution.py:391
  65.2 4.6 %collective-permute-start.19 = (bf16[16,128]{1,0:T(8,128)(2,1)S(1)}, bf16[16,128]{1,0:T(8,128)(2,1)S(1)}, u32[]{:S(2)}, u32[]{:S(2)}) collective-permute-start(bf16[16,128]{1,0:T(8,128)(2,1)S(1)} %get-tuple-element.49), channel_id=1, source_target_pairs={{1,0},{3,1},{2,3},{0,2},{5,4},{7,5},{6,7},{4,6},{9,8},{11,9},{10,1... | collective-permute-start | bytes 12296 | tf_op jit(solution)/shard_map/ppermute | solution.py:482
